TPU v7x, 32 devices: a whole 2x2x4 slice. The times are simulated.
32 devices in a mesh: dp: 16 (over z, y, x), seq: 2 (over core).
Axes of the slice: x: 2, y: 2, z: 4, core: 2. Of those that a mesh axis runs over, the one named last changes fastest.
Arguments:
- latents: float32 [16, 256, 48], P('dp', 'seq'), may hold values from -6 to 6
- valid: int32 [16, 256], P('dp', 'seq'), may hold values 0 or 1
- class_labels: int32 [16], replicated, may hold values from 0 to 447
- group_perm: int32 [16], P('dp'), may hold values from 0 to 15, as said below
- patch_weight: bfloat16 [48, 768], replicated, may hold values from -0.875 to 0.875
- pos_table: bfloat16 [256, 768], P('seq'), may hold values from -3 to 3
- class_table: bfloat16 [1024, 768], replicated, may hold values from -3 to 3
- ln1_gain: bfloat16 [1, 768], replicated, may hold values from 0.25 to 1.75
- ln1_bias: bfloat16 [1, 768], replicated, may hold values from -1.5 to 1.5
- qkv_weight: bfloat16 [1, 768, 2304], replicated, may hold values from -0.21875 to 0.21875
- out_weight: bfloat16 [1, 768, 768], replicated, may hold values from -0.875 to 0.875
- ln2_gain: bfloat16 [1, 768], replicated, may hold values from 0.25 to 1.75
- ln2_bias: bfloat16 [1, 768], replicated, may hold values from -1.5 to 1.5
- up_weight: bfloat16 [1, 768, 3072], replicated, may hold values from -0.21875 to 0.21875
- up_bias: bfloat16 [1, 3072], replicated, may hold values from -1.5 to 1.5
- down_weight: bfloat16 [1, 3072, 768], replicated, may hold values from -0.109375 to 0.109375
- head_weight: bfloat16 [768, 96], replicated, may hold values from -0.109375 to 0.109375
- head_bias: bfloat16 [96], replicated, may hold values from -1 to 1
- cot_latents: float32 [16, 256, 48], P('dp', 'seq'), may hold values from -6 to 6
- cot_logdet: float32 [16], P('dp'), may hold values from -4 to 4
Outputs:
- new_latents: float32 [16, 256, 48], P('dp', 'seq')
- logdet: float32 [16], P('dp')
- latents_grad: float32 [16, 256, 48], P('dp', 'seq')
- patch_weight_grad: float32 [48, 768], replicated
- pos_grad: float32 [256, 768], P('seq')
- class_grad: float32 [1024, 768], P('dp')
- ln1_gain_grad: float32 [1, 768], replicated
- ln1_bias_grad: float32 [1, 768], replicated
- qkv_grad: float32 [1, 768, 2304], replicated
- out_grad: float32 [1, 768, 768], replicated
- ln2_gain_grad: float32 [1, 768], replicated
- ln2_bias_grad: float32 [1, 768], replicated
- up_grad: float32 [1, 768, 3072], replicated
- up_bias_grad: float32 [1, 3072], replicated
- down_grad: float32 [1, 3072, 768], replicated
- head_weight_grad: float32 [768, 96], replicated
- head_bias_grad: float32 [96], replicated
Inputs may be any that keep to these rules, and one draw needn't show every extreme that they name: Each of 0 to 15 once; class_labels[group_perm] never falls.
All inputs are finite; a program needn't handle non-finite values. No bound on the sum of `valid` on one device may be relied on, other than what follows from the above.
Results may differ from a plain program's by a relative error of at most 0.023.
Values may be sent and summed in bfloat16 or wider, within the bound.
A program may use at most 320 MiB of HBM per device.

v0:
```python
import jax
import jax.numpy as jnp
from jax import lax
from jax.sharding import PartitionSpec as P

HEAD_DIM = 64


precise = lax.Precision.HIGHEST
norm_eps = 1e-05


def shifted_2(shard, axis, by):
    size = lax.axis_size(axis)
    pairs = [(i, i + by) for i in range(size) if 0 <= i + by < size]
    return lax.ppermute(shard, axis, pairs)


def layer_norm(values, norm_gain, norm_bias):
    center = values - jnp.mean(values, -1, keepdims=True)
    spread = jnp.mean(center * center, -1, keepdims=True)
    return center * lax.rsqrt(spread + norm_eps) * norm_gain + norm_bias


def matmul(left_side, weight_mat):
    return jnp.dot(left_side, weight_mat, preferred_element_type=jnp.float32)


def outer_sum(left_side, grad_side):
    left_flat = left_side.reshape(-1, left_side.shape[-1])
    grad_flat = grad_side.reshape(-1, grad_side.shape[-1])
    return lax.dot_general(
        left_flat, grad_flat, (((0,), (0,)), ((), ())), preferred_element_type=jnp.float32
    )


def transposed(grad_side, weight_mat):
    return lax.dot_general(
        grad_side,
        weight_mat,
        (((grad_side.ndim - 1,), (1,)), ((), ())),
        preferred_element_type=jnp.float32,
    )


def eight_rows(matrix):
    return matrix.reshape(8, -1)


def attention_mask(key_valid, patch_rows, seq_place):
    query_pos = seq_place * patch_rows + lax.iota(jnp.int32, patch_rows)
    key_pos = (seq_place - 1) * patch_rows + lax.iota(jnp.int32, 2 * patch_rows)
    earlier = (key_pos[None, :] < query_pos[:, None])[None] & (key_valid[:, None, :] > 0)
    return earlier | (key_pos[None, :] == query_pos[:, None])[None]


def masked_scores(query, keys, allowed):
    logits = jnp.einsum(
        "bqhd,bkhd->bhqk", query, keys, preferred_element_type=jnp.float32
    ) * HEAD_DIM ** (-0.5)
    return jnp.where(allowed[:, None], logits, -1e30)


def forward(latents, valid, class_rows, seq_place, weights):
    (
        patch_weight,
        pos_table,
        qkv_weight,
        out_weight,
        ln1_gain,
        ln1_bias,
        ln2_gain,
        ln2_bias,
        up_weight,
        up_bias,
        down_weight,
        head_weight,
        head_bias,
    ) = weights
    images, patch_rows, channels = latents.shape
    model_width = qkv_weight.shape[1]
    head_count = model_width // HEAD_DIM
    latent_low = latents.astype(jnp.bfloat16)
    hidden = (
        matmul(latent_low, patch_weight)
        + pos_table.astype(jnp.float32)[None]
        + class_rows[:, None, :]
    )
    own_mask = valid.astype(jnp.bfloat16)
    normed = layer_norm(
        hidden, ln1_gain[0].astype(jnp.float32), ln1_bias[0].astype(jnp.float32)
    ).astype(jnp.bfloat16)
    packed = matmul(normed, qkv_weight[0]).astype(jnp.bfloat16)
    query = packed[..., :model_width].reshape(images, patch_rows, head_count, HEAD_DIM)
    keys_own = packed[..., model_width : 2 * model_width]
    values_own = packed[..., 2 * model_width :]
    prior_keys, prior_values, prior_mask = shifted_2((keys_own, values_own, own_mask), "seq", 1)
    keys = jnp.concatenate((prior_keys, keys_own), 1).reshape(
        images, 2 * patch_rows, head_count, HEAD_DIM
    )
    values = jnp.concatenate((prior_values, values_own), 1).reshape(
        images, 2 * patch_rows, head_count, HEAD_DIM
    )
    allowed = attention_mask(jnp.concatenate((prior_mask, own_mask), 1), patch_rows, seq_place)
    logits = masked_scores(query, keys, allowed)
    row_peak = jnp.max(logits, -1, keepdims=True)
    log_total = row_peak + jnp.log(jnp.sum(jnp.exp(logits - row_peak), -1, keepdims=True))
    weights_soft = jnp.exp(logits - log_total).astype(jnp.bfloat16)
    attended = jnp.einsum(
        "bhqk,bkhd->bqhd", weights_soft, values, preferred_element_type=jnp.float32
    )
    attended = attended.astype(jnp.bfloat16).reshape(images, patch_rows, model_width)
    mid = hidden + matmul(attended, out_weight[0])
    second = layer_norm(
        mid, ln2_gain[0].astype(jnp.float32), ln2_bias[0].astype(jnp.float32)
    ).astype(jnp.bfloat16)
    preact = matmul(second, up_weight[0]) + up_bias[0].astype(jnp.float32)
    activated = jax.nn.gelu(preact, approximate=True).astype(jnp.bfloat16)
    saved = [
        (
            hidden,
            normed,
            query,
            keys,
            values,
            allowed,
            log_total,
            attended,
            mid,
            second,
            preact,
            activated,
        )
    ]
    hidden = mid + matmul(activated, down_weight[0])
    top_low = hidden.astype(jnp.bfloat16)
    head_out = matmul(top_low, head_weight) + head_bias.astype(jnp.float32)
    prior_row = shifted_2(head_out[:, patch_rows - 1, :], "seq", 1)
    shifted = jnp.concatenate((prior_row[:, None, :], head_out[:, : patch_rows - 1, :]), 1)
    shifted = shifted * valid.astype(jnp.float32)[..., None]
    alpha = shifted[..., :channels]
    shift_mean = shifted[..., channels:]
    factor = jnp.exp(-alpha)
    new_latents = (latents - shift_mean) * factor
    logdet_part = -jnp.sum(alpha, (1, 2))
    return (new_latents, logdet_part, factor, top_low, saved)


def local(
    latents,
    valid,
    class_labels,
    group_perm,
    patch_weight,
    pos_table,
    class_table,
    ln1_gain,
    ln1_bias,
    qkv_weight,
    out_weight,
    ln2_gain,
    ln2_bias,
    up_weight,
    up_bias,
    down_weight,
    head_weight,
    head_bias,
    cot_latents,
    cot_logdet,
):
    images, patch_rows, channels = latents.shape
    model_width = qkv_weight.shape[1]
    head_count = model_width // HEAD_DIM
    layer_total = qkv_weight.shape[0]
    seq_place = lax.axis_index("seq")
    picks = group_perm[:, None] == lax.iota(jnp.int32, class_labels.shape[0])[None, :]
    image_labels = jnp.sum(jnp.where(picks, class_labels[None, :], 0), 1)
    label_hot = image_labels[:, None] == lax.iota(jnp.int32, class_table.shape[0])[None, :]
    class_rows = matmul(label_hot.astype(jnp.bfloat16), class_table)
    weights = (
        patch_weight,
        pos_table,
        qkv_weight,
        out_weight,
        ln1_gain,
        ln1_bias,
        ln2_gain,
        ln2_bias,
        up_weight,
        up_bias,
        down_weight,
        head_weight,
        head_bias,
    )
    new_latents, logdet_part, factor, top_low, saved = forward(
        latents, valid, class_rows, seq_place, weights
    )
    latents_again, unused = lax.optimization_barrier((latents, new_latents))
    unused_a, unused_b, unused_c, unused_d, saved = forward(
        latents_again, valid, class_rows, seq_place, weights
    )
    valid_float = valid.astype(jnp.float32)
    d_alpha = -cot_latents * new_latents - cot_logdet[:, None, None]
    d_mean = -cot_latents * factor
    d_shifted = jnp.concatenate((d_alpha, d_mean), -1) * valid_float[..., None]
    next_row = shifted_2(d_shifted[:, 0, :], "seq", -1)
    d_head = jnp.concatenate((d_shifted[:, 1:, :], next_row[:, None, :]), 1).astype(jnp.bfloat16)
    head_weight_grad = outer_sum(top_low, d_head)
    head_bias_grad = jnp.sum(d_head.astype(jnp.float32), (0, 1))
    d_hidden = transposed(d_head, head_weight)
    grads_qkv, grads_out, grads_up, grads_down = ([], [], [], [])
    grads_g1, grads_b1, grads_g2, grads_b2, grads_ub = ([], [], [], [], [])
    for layer_index in reversed(range(layer_total)):
        (
            hidden,
            normed,
            query,
            keys,
            values,
            allowed,
            log_total,
            attended,
            mid,
            second,
            preact,
            activated,
        ) = saved[layer_index]
        d_down = d_hidden.astype(jnp.bfloat16)
        down_grad = outer_sum(activated, d_down)
        d_act = transposed(d_down, down_weight[layer_index])
        unused_gelu, gelu_pull = jax.vjp(lambda inner: jax.nn.gelu(inner, approximate=True), preact)
        d_pre = gelu_pull(d_act)[0].astype(jnp.bfloat16)
        up_bias_grad = jnp.sum(d_pre.astype(jnp.float32), (0, 1))
        up_grad = outer_sum(second, d_pre)
        d_second = transposed(d_pre, up_weight[layer_index])
        unused_norm, norm_pull = jax.vjp(
            layer_norm,
            mid,
            ln2_gain[layer_index].astype(jnp.float32),
            ln2_bias[layer_index].astype(jnp.float32),
        )
        d_mid_norm, ln2_gain_part, ln2_bias_part = norm_pull(d_second)
        d_mid = d_hidden + d_mid_norm
        d_proj = d_mid.astype(jnp.bfloat16)
        out_grad = outer_sum(attended, d_proj)
        d_attended = transposed(d_proj, out_weight[layer_index]).astype(jnp.bfloat16)
        d_attended = d_attended.reshape(images, patch_rows, head_count, HEAD_DIM)
        logits = masked_scores(query, keys, allowed)
        probs = jnp.exp(logits - log_total)
        d_probs = jnp.einsum(
            "bqhd,bkhd->bhqk", d_attended, values, preferred_element_type=jnp.float32
        )
        d_scores = (probs * (d_probs - jnp.sum(d_probs * probs, -1, keepdims=True))).astype(
            jnp.bfloat16
        )
        d_query = jnp.einsum(
            "bhqk,bkhd->bqhd", d_scores, keys, preferred_element_type=jnp.float32
        ) * HEAD_DIM ** (-0.5)
        d_keys = jnp.einsum(
            "bhqk,bqhd->bkhd", d_scores, query, preferred_element_type=jnp.float32
        ) * HEAD_DIM ** (-0.5)
        d_values = jnp.einsum(
            "bhqk,bqhd->bkhd",
            probs.astype(jnp.bfloat16),
            d_attended,
            preferred_element_type=jnp.float32,
        )
        d_keys = d_keys.reshape(images, 2 * patch_rows, model_width)
        d_values = d_values.reshape(images, 2 * patch_rows, model_width)
        back_keys, back_values = (
            shifted_2(d_keys[:, :patch_rows].astype(jnp.bfloat16), "seq", -1).astype(jnp.float32),
            shifted_2(d_values[:, :patch_rows].astype(jnp.bfloat16), "seq", -1).astype(jnp.float32),
        )
        d_packed = jnp.concatenate(
            (
                d_query.reshape(images, patch_rows, model_width),
                d_keys[:, patch_rows:] + back_keys,
                d_values[:, patch_rows:] + back_values,
            ),
            -1,
        ).astype(jnp.bfloat16)
        qkv_grad = outer_sum(normed, d_packed)
        d_normed = transposed(d_packed, qkv_weight[layer_index])
        unused_norm, norm_pull = jax.vjp(
            layer_norm,
            hidden,
            ln1_gain[layer_index].astype(jnp.float32),
            ln1_bias[layer_index].astype(jnp.float32),
        )
        d_input, ln1_gain_part, ln1_bias_part = norm_pull(d_normed)
        d_hidden = d_mid + d_input
        grads_qkv.insert(0, qkv_grad)
        grads_out.insert(0, out_grad)
        grads_up.insert(0, up_grad)
        grads_down.insert(0, down_grad)
        grads_g1.insert(0, ln1_gain_part)
        grads_b1.insert(0, ln1_bias_part)
        grads_g2.insert(0, ln2_gain_part)
        grads_b2.insert(0, ln2_bias_part)
        grads_ub.insert(0, up_bias_grad)
    d_embed_low = d_hidden.astype(jnp.bfloat16)
    patch_grad_part = outer_sum(latents.astype(jnp.bfloat16), d_embed_low)
    latents_grad = cot_latents * factor + transposed(d_embed_low, patch_weight)
    pos_part = jnp.sum(d_hidden, 0)
    class_part = jnp.sum(d_hidden, 1)
    logdet, class_sums = lax.psum((logdet_part, class_part), "seq")
    class_term = lax.dot_general(
        label_hot.astype(jnp.float32),
        class_sums,
        (((0,), (0,)), ((), ())),
        precision=precise,
        preferred_element_type=jnp.float32,
    )
    class_grad = lax.psum_scatter(class_term, "dp", scatter_dimension=0, tiled=True)
    pos_grad = lax.psum(pos_part, "dp")
    (
        patch_weight_grad,
        head_weight_grad,
        head_bias_grad,
        ln1_gain_grad,
        ln1_bias_grad,
        ln2_gain_grad,
        ln2_bias_grad,
        up_bias_grad,
    ) = lax.psum(
        (
            patch_grad_part,
            head_weight_grad,
            head_bias_grad,
            jnp.stack(grads_g1),
            jnp.stack(grads_b1),
            jnp.stack(grads_g2),
            jnp.stack(grads_b2),
            jnp.stack(grads_ub),
        ),
        ("dp", "seq"),
    )
    qkv_stack = jnp.stack(grads_qkv)
    out_stack = jnp.stack(grads_out)
    up_stack = jnp.stack(grads_up)
    down_stack = jnp.stack(grads_down)
    flat_parts = (
        lax.psum_scatter(eight_rows(qkv_stack), ("dp", "seq"), scatter_dimension=1, tiled=True),
        lax.psum_scatter(eight_rows(out_stack), ("dp", "seq"), scatter_dimension=1, tiled=True),
        lax.psum_scatter(eight_rows(up_stack), ("dp", "seq"), scatter_dimension=1, tiled=True),
        lax.psum_scatter(eight_rows(down_stack), ("dp", "seq"), scatter_dimension=1, tiled=True),
    )
    flat_qkv, flat_out, flat_up, flat_down = (
        lax.all_gather(
            flat_parts[0].astype(jnp.bfloat16), ("dp", "seq"), axis=1, tiled=True
        ).astype(jnp.float32),
        lax.all_gather(
            flat_parts[1].astype(jnp.bfloat16), ("dp", "seq"), axis=1, tiled=True
        ).astype(jnp.float32),
        lax.all_gather(
            flat_parts[2].astype(jnp.bfloat16), ("dp", "seq"), axis=1, tiled=True
        ).astype(jnp.float32),
        lax.all_gather(
            flat_parts[3].astype(jnp.bfloat16), ("dp", "seq"), axis=1, tiled=True
        ).astype(jnp.float32),
    )
    qkv_stack = flat_qkv.reshape(qkv_stack.shape)
    out_stack = flat_out.reshape(out_stack.shape)
    up_stack = flat_up.reshape(up_stack.shape)
    down_stack = flat_down.reshape(down_stack.shape)
    return (
        new_latents,
        logdet,
        latents_grad,
        patch_weight_grad,
        pos_grad,
        class_grad,
        ln1_gain_grad,
        ln1_bias_grad,
        qkv_stack,
        out_stack,
        ln2_gain_grad,
        ln2_bias_grad,
        up_stack,
        up_bias_grad,
        down_stack,
        head_weight_grad,
        head_bias_grad,
    )


def solution(mesh):
    in_specs = (
        P("dp", "seq", None),
        P("dp", "seq"),
        P(),
        P("dp"),
        P(),
        P("seq", None),
        P(),
        P(),
        P(),
        P(),
        P(),
        P(),
        P(),
        P(),
        P(),
        P(),
        P(),
        P(),
        P("dp", "seq", None),
        P("dp"),
    )
    out_specs = (
        P("dp", "seq", None),
        P("dp"),
        P("dp", "seq", None),
        P(),
        P("seq", None),
        P("dp", None),
        P(),
        P(),
        P(),
        P(),
        P(),
        P(),
        P(),
        P(),
        P(),
        P(),
        P(),
    )
    return jax.shard_map(local, mesh=mesh, in_specs=in_specs, out_specs=out_specs, check_vma=False)
```

profile of v0, /device:TPU:0, one launch (start us, length us, event | category | flops | bytes accessed | tf_op | source)
XLA Modules:
  0.0 1260.5 jit_solution(11902922079995836065)
XLA Ops:
  14.1 3.0 collective-permute-start.2
  17.6 1.9 collective-permute-start.1
  19.5 2.0 collective-permute-start
  31.4 1.9 copy.53
  38.9 1.9 copy.51
  40.9 2.1 convolution_convert_fusion.3
  44.9 6.5 fusion.57
  57.1 2.0 multiply_subtract_fusion
  64.6 2.9 collective-permute-start.6
  70.5 4.3 collective-permute-start.5
  74.8 2.0 fusion.109
  78.6 1.9 copy.58
  85.6 1.9 copy.56
  87.5 2.1 convolution_convert_fusion.2
  90.4 3.3 fusion.13
  93.8 5.5 convert_reduce_fusion
  99.3 2.3 multiply_reduce_fusion.1
  102.7 1.9 fusion.96
  104.6 3.5 reshape_stack.13
  108.2 2.6 fusion.60
  112.5 2.5 multiply_reduce_fusion
  122.5 4.2 fusion.76
  126.7 7.2 reshape_stack.12
  134.6 6.5 fusion.125
  141.1 9.2 reshape_stack.14
  150.4 6.8 fusion.66
  157.2 9.3 reshape_stack.15
  166.6 42.8 %reduce-scatter.10.cloned.1.call-done = f32[8,2304]{1,0:T(8,128)} async-done(((f32[8,73728]{1,0:T(8,128)}), f32[8,2304]{1,0:T(8,128)}) %reduce-scatter.10.cloned.1.call-update) | async-done | bytes 73744 | tf_op jit(solution)/shard_map/reduce_scatter | solution.py:344
  211.0 123.2 %reduce-scatter.8.cloned.1.call-done = f32[8,6912]{1,0:T(8,128)} async-done(((f32[8,221184]{1,0:T(8,128)}), f32[8,6912]{1,0:T(8,128)}) %reduce-scatter.8.cloned.1.call-update) | async-done | bytes 221200 | tf_op jit(solution)/shard_map/reduce_scatter | solution.py:343
  335.8 139.6 %reduce-scatter.12.cloned.1.call-done = f32[8,9216]{1,0:T(8,128)} async-done(((f32[8,294912]{1,0:T(8,128)}), f32[8,9216]{1,0:T(8,128)}) %reduce-scatter.12.cloned.1.call-update) | async-done | bytes 294928 | tf_op jit(solution)/shard_map/reduce_scatter | solution.py:345
  477.1 139.7 %reduce-scatter.14.cloned.1.call-done = f32[8,9216]{1,0:T(8,128)} async-done(((f32[8,294912]{1,0:T(8,128)}), f32[8,9216]{1,0:T(8,128)}) %reduce-scatter.14.cloned.1.call-update) | async-done | bytes 294928 | tf_op jit(solution)/shard_map/reduce_scatter | solution.py:346
  618.5 1.9 fusion.108
  620.5 3.4 multiply_reduce_fusion.2
  624.9 1.8 convolution_bitcast_fusion
  626.8 1.9 fusion.65
  630.6 3.6 all-reduce.2
  634.2 1.9 broadcast_multiply_fusion
  639.2 41.3 %all-reduce = (f32[1,768]{1,0:T(1,128)}, f32[1,768]{1,0:T(1,128)}, f32[1,768]{1,0:T(1,128)}, f32[1,768]{1,0:T(1,128)}, f32[1,3072]{1,0:T(1,128)}, /*index=5*/f32[96]{0:T(128)}) all-reduce(f32[1,768]{1,0:T(1,128)S(1)} %stack.15, f32[1,768]{1,0:T(1,128)S(1)} %stack.16, ...), channel_id=1, replica_groups=mesh['dp'=16,'seq'=2] {'dp','seq'}, use_global_device_ids=true, to_apply=%region_26.27 | all-reduce | flops 6240 | bytes 49920 | tf_op jit(solution)/shard_map/psum | solution.py:325
  680.5 3.1 reshape.960
  683.6 51.8 %all-gather.5.cloned.1.call-done = bf16[8,221184]{1,0:T(8,128)(2,1)} async-done(((bf16[8,6912]{1,0:T(8,128)(2,1)}), bf16[8,221184]{1,0:T(8,128)(2,1)}) %all-gather.5.cloned.1.call-update) | async-done | bytes 3538960 | tf_op jit(solution)/shard_map/all_gather | solution.py:349
  735.4 6.3 reshape.958
  741.8 59.6 %all-gather.9.cloned.1.call-done = bf16[8,294912]{1,0:T(8,128)(2,1)} async-done(((bf16[8,9216]{1,0:T(8,128)(2,1)}), bf16[8,294912]{1,0:T(8,128)(2,1)}) %all-gather.9.cloned.1.call-update) | async-done | bytes 4718608 | tf_op jit(solution)/shard_map/all_gather | solution.py:355
  801.4 7.9 reshape.962
  809.3 57.4 %all-gather.11.cloned.1.call-done = bf16[8,294912]{1,0:T(8,128)(2,1)} async-done(((bf16[8,9216]{1,0:T(8,128)(2,1)}), bf16[8,294912]{1,0:T(8,128)(2,1)}) %all-gather.11.cloned.1.call-update) | async-done | bytes 4718608 | tf_op jit(solution)/shard_map/all_gather | solution.py:358
  866.7 7.9 reshape.964
  874.6 123.7 %all-reduce.8.cloned.1.call-done = (f32[48,768]{1,0:T(8,128)}, f32[768,96]{0,1:T(8,128)}) async-done(((f32[48,768]{1,0:T(8,128)}, f32[768,96]{0,1:T(8,128)}), (f32[48,768]{1,0:T(8,128)}, f32[768,96]{0,1:T(8,128)})) %all-reduce.8.cloned.1.call-update) | async-done | bytes 442384 | tf_op jit(solution)/shard_map/psum | solution.py:325
  998.3 115.3 %all-reduce.6.cloned.1.call-done = f32[128,768]{1,0:T(8,128)} async-done(((f32[128,768]{1,0:T(8,128)}), f32[128,768]{1,0:T(8,128)}) %all-reduce.6.cloned.1.call-update) | async-done | bytes 393232 | tf_op jit(solution)/shard_map/psum | solution.py:315
  1113.7 135.2 %reduce-scatter.6.cloned.1.call-done = f32[64,768]{1,0:T(8,128)} async-done(((f32[1024,768]{1,0:T(8,128)}), f32[64,768]{1,0:T(8,128)}) %reduce-scatter.6.cloned.1.call-update) | async-done | bytes 196624 | tf_op jit(solution)/shard_map/reduce_scatter | solution.py:314
  (236 shorter events, 72.8 us)
Async XLA Ops:
  7.2 5.4 copy-start
  7.2 5.3 copy-start.51
  7.2 5.3 copy-start.50
  7.2 202.2 %reduce-scatter.10.cloned.1.call-start = ((), (), s32[]{:S(2)}) async-start(), calls=%async_computation.9 | async-start | bytes 2433024 | tf_op jit(solution)/shard_map/reduce_scatter | solution.py:344
  7.3 4.6 copy-start.23
  7.3 4.6 copy-start.27
  7.3 4.6 copy-start.29
  12.5 50.5 %copy-start.32 = (f32[768]{0:T(1024)}, f32[768]{0:T(1024)S(1)}, u32[]{:S(2)}) copy-start(f32[768]{0:T(1024)S(1)} %get-tuple-element.71) | copy-start | bytes 9220
  12.6 4.6 copy-start.55
  14.1 15.5 %collective-permute-start.2 = (bf16[1,128,768]{2,1,0:T(8,128)(2,1)}, bf16[1,128,768]{2,1,0:T(8,128)(2,1)}, u32[]{:S(2)}, u32[]{:S(2)}) collective-permute-start(bf16[1,128,768]{2,1,0:T(8,128)(2,1)} %get-tuple-element.46), channel_id=1, source_target_pairs={{0,1},{2,3},{4,5},{6,7},{8,9},{10,11},{12,13},{14,15},{16,17},{18,... | collective-permute-start | bytes 589832 | tf_op jit(solution)/shard_map/ppermute | solution.py:16
  17.6 9.9 collective-permute-start.1
  19.5 17.6 %collective-permute-start = (bf16[1,128,768]{2,1,0:T(8,128)(2,1)}, bf16[1,128,768]{2,1,0:T(8,128)(2,1)}, u32[]{:S(2)}, u32[]{:S(2)}) collective-permute-start(bf16[1,128,768]{2,1,0:T(8,128)(2,1)} %get-tuple-element.48), channel_id=1, source_target_pairs={{0,1},{2,3},{4,5},{6,7},{8,9},{10,11},{12,13},{14,15},{16,17},{18,... | collective-permute-start | bytes 589832 | tf_op jit(solution)/shard_map/ppermute | solution.py:16
  23.3 21.6 %copy-start.34 = (f32[768]{0:T(1024)}, f32[768]{0:T(1024)S(1)}, u32[]{:S(2)}) copy-start(f32[768]{0:T(1024)S(1)} %get-tuple-element.73) | copy-start | bytes 9220
  53.3 2.1 collective-permute-start.3
  59.7 2.8 copy-start.30
  64.6 12.2 collective-permute-start.6
  67.5 7.3 collective-permute-start.4
  70.5 13.3 %collective-permute-start.5 = (bf16[1,128,768]{2,1,0:T(8,128)(2,1)}, bf16[1,128,768]{2,1,0:T(8,128)(2,1)}, u32[]{:S(2)}, u32[]{:S(2)}) collective-permute-start(bf16[1,128,768]{2,1,0:T(8,128)(2,1)} %get-tuple-element.45), channel_id=1, source_target_pairs={{0,1},{2,3},{4,5},{6,7},{8,9},{10,11},{12,13},{14,15},{16,17},{18,... | collective-permute-start | bytes 589832 | tf_op jit(solution)/shard_map/ppermute | solution.py:16
  80.6 3.3 copy-start.22
  90.1 11.5 copy-start.7
  90.1 11.5 copy-start.39
  90.4 11.3 copy-start.46
  90.4 3.4 copy-start.17
  90.4 8.9 slice-start
  93.8 5.5 copy-start.11
  93.8 5.5 slice-start.1
  108.1 226.0 %reduce-scatter.8.cloned.1.call-start = ((), (), s32[]{:S(2)}) async-start(), calls=%async_computation.7 | async-start | bytes 7299072 | tf_op jit(solution)/shard_map/reduce_scatter | solution.py:343
  116.3 3.4 copy-start.16
  116.3 3.9 collective-permute-start.7
  118.3 4.3 copy-start.5
  118.3 4.3 copy-start.33
  118.3 4.2 copy-start.44
  118.3 4.2 copy-start.48
  118.3 3.5 collective-permute-start.8
  133.9 341.5 %reduce-scatter.12.cloned.1.call-start = ((), (), s32[]{:S(2)}) async-start(), calls=%async_computation.11 | async-start | bytes 9732096 | tf_op jit(solution)/shard_map/reduce_scatter | solution.py:345
  150.4 466.4 %reduce-scatter.14.cloned.1.call-start = ((), (), s32[]{:S(2)}) async-start(), calls=%async_computation.13 | async-start | bytes 9732096 | tf_op jit(solution)/shard_map/reduce_scatter | solution.py:346
  166.5 453.9 %copy-start.45 = (f32[128]{0:T(128)S(1)}, f32[128]{0:T(128)}, u32[]{:S(2)}) copy-start(f32[128]{0:T(128)} %copy-done.43) | copy-start | bytes 1540
  166.5 453.9 %copy-start.49 = (f32[128]{0:T(128)S(1)}, f32[128]{0:T(128)}, u32[]{:S(2)}) copy-start(f32[128]{0:T(128)} %copy-done.47) | copy-start | bytes 1540
  166.6 513.9 %all-gather.7.cloned.1.call-start = ((), (), s32[]{:S(2)}) async-start(), calls=%async_computation.10 | async-start | bytes 1216512 | tf_op jit(solution)/shard_map/all_gather | solution.py:352
  210.9 524.5 %all-gather.5.cloned.1.call-start = ((), (), s32[]{:S(2)}) async-start(), calls=%async_computation.8 | async-start | bytes 3649536 | tf_op jit(solution)/shard_map/all_gather | solution.py:349
  335.8 465.6 %all-gather.9.cloned.1.call-start = ((), (), s32[]{:S(2)}) async-start(), calls=%async_computation.12 | async-start | bytes 4866048 | tf_op jit(solution)/shard_map/all_gather | solution.py:355
  477.1 389.6 %all-gather.11.cloned.1.call-start = ((), (), s32[]{:S(2)}) async-start(), calls=%async_computation.14 | async-start | bytes 4866048 | tf_op jit(solution)/shard_map/all_gather | solution.py:358
  618.5 379.9 %all-reduce.8.cloned.1.call-start = ((), (), s32[]{:S(2)}) async-start(), calls=%async_computation.15 | async-start | bytes 884736 | tf_op jit(solution)/shard_map/psum | solution.py:325
  620.4 3.4 copy-start.53
  620.4 3.4 copy-start.6
  620.4 3.6 copy-start.15
  628.7 485.0 %all-reduce.6.cloned.1.call-start = ((), (), s32[]{:S(2)}) async-start(), calls=%async_computation.5 | async-start | bytes 786432 | tf_op jit(solution)/shard_map/psum | solution.py:315
  629.2 619.7 %reduce-scatter.6.cloned.1.call-start = ((), (), s32[]{:S(2)}) async-start(), calls=%async_computation.6 | async-start | bytes 3342336 | tf_op jit(solution)/shard_map/reduce_scatter | solution.py:314
  (30 other events, 40.5 us)
Sparse Core Ops, SparseCore 0:
  108.3 101.0 reduce-scatter.9
  216.0 118.1 reduce-scatter.7
  340.6 134.7 reduce-scatter.11
  482.2 134.5 reduce-scatter.13
  619.6 53.5 all-gather.6
  676.5 58.9 all-gather.4
  738.9 62.4 all-gather.8
  804.3 62.4 all-gather.10
  873.2 125.0 all-reduce.7
  1004.8 108.8 all-reduce.5
  1119.2 129.6 reduce-scatter.5
where the time goes:
time: 1260 us
  waiting for transfers between devices  991 us (79%)
  local copies, waits for them, and re-layouts  84.4 us (7%)
  matrix products  68.3 us (5%)
  blocking collectives  44.9 us (4%)
  other arithmetic  34.9 us (3%)
  starting transfers between devices  20.1 us (2%)
  between operations  17 us (1%)
    reduce_scatter x1, waiting for transfers between devices, local(): lax.psum_scatter(eight_rows(down_stack), ('dp', 'seq'), scatter_dimension...  140 us
    reduce_scatter x1, waiting for transfers between devices, local(): lax.psum_scatter(eight_rows(up_stack), ('dp', 'seq'), scatter_dimension=1...  140 us
    reduce_scatter x1, waiting for transfers between devices, local(): lax.psum_scatter(class_term, 'dp', scatter_dimension=0, tiled=True)  135 us
    psum x1, waiting for transfers between devices, local(): lax.psum((patch_grad_part, head_weight_grad, head_bias_grad, jnp.stack(gr...  124 us
    reduce_scatter x1, waiting for transfers between devices, local(): lax.psum_scatter(eight_rows(qkv_stack), ('dp', 'seq'), scatter_dimension=...  123 us
    psum x1, waiting for transfers between devices, local(): pos_grad = lax.psum(pos_part, 'dp')  115 us
    all_gather x1, waiting for transfers between devices, local(): lax.all_gather(flat_parts[2].astype(jnp.bfloat16), ('dp', 'seq'), axis=1,...  59.6 us
    all_gather x1, waiting for transfers between devices, local(): lax.all_gather(flat_parts[3].astype(jnp.bfloat16), ('dp', 'seq'), axis=1,...  57.4 us
  transfers between devices with their start and end apart: 20, of which 12 were waited for; matrix products, arithmetic and copies ran while one was open for 10% of the time, Pallas kernels for 0%

commit v1 on v0

--- a/solution.py
+++ b/solution.py
@@ -1,6 +1,8 @@
 import jax
 import jax.numpy as jnp
 from jax import lax
+from jax.experimental import pallas as pl
+from jax.experimental.pallas import tpu as pltpu
 from jax.sharding import PartitionSpec as P
 
 HEAD_DIM = 64
@@ -59,6 +61,501 @@
         "bqhd,bkhd->bhqk", query, keys, preferred_element_type=jnp.float32
     ) * HEAD_DIM ** (-0.5)
     return jnp.where(allowed[:, None], logits, -1e30)
+
+
+MESH = pl.DeviceIdType.MESH
+UNITS = 12
+ROWS = 256
+COLS = 384
+STAGES = 3
+f32 = jnp.float32
+bf16 = jnp.bfloat16
+
+
+def grads_kernel(
+    lt_ref, r_ref, pos_ref, small_ref,
+    down_hbm, up_hbm, out_hbm, qkv_hbm, pos_hbm, small_hbm,
+    stage, part, full, core_in, ab_in, c_in, send_sem, recv_sem, local_sem,
+):
+    dp = lax.axis_index("dp")
+    core = lax.axis_index("seq")
+    x, y, z = dp % 2, (dp // 2) % 2, dp // 4
+    side = z // 2
+    inner = ((z + 1) // 2) % 2 == 1
+    outer = ((z + 1) // 2) % 2 == 0
+    to_core = (dp, 1 - core)
+    to_x = (dp + 1 - 2 * x, core)
+    to_y = (dp + 2 - 4 * y, core)
+    to_mate = (dp + 4 - 8 * (z % 2), core)
+    to_inner = ((dp + 12 - 8 * z + 16) % 16, core)
+
+    def rows_at(start, count):
+        return pl.ds(pl.multiple_of(start, 16), count)
+
+    barrier = pltpu.get_barrier_semaphore()
+    for target in (to_core, to_x, to_y, to_mate):
+        pl.semaphore_signal(barrier, inc=1, device_id=target, device_id_type=MESH)
+
+    @pl.when(inner)
+    def _():
+        pl.semaphore_signal(barrier, inc=1, device_id=to_inner, device_id_type=MESH)
+        pl.semaphore_wait(barrier, 5)
+
+    @pl.when(outer)
+    def _():
+        pl.semaphore_wait(barrier, 4)
+
+    def copy(u, k, src, dst, target):
+        return pltpu.make_async_remote_copy(
+            src_ref=src, dst_ref=dst, send_sem=send_sem.at[u, k], recv_sem=recv_sem.at[u, k],
+            device_id=target, device_id_type=MESH,
+        )
+
+    def arrived(u, k, dst):
+        copy(u, k, dst, dst, to_core).wait_recv()
+
+    def added(dst, left, right):
+        dst[...] = (left[...].astype(f32) + right[...].astype(f32)).astype(bf16)
+
+    first = (x, y)
+    second = (y, x)
+    to_first = (to_x, to_y)
+    to_second = (to_y, to_x)
+
+    def out_rows(u, t, start, count):
+        return full.at[u, rows_at(t * ROWS + start, count)]
+
+    def part_rows(u, t, start, count):
+        return part.at[u, rows_at(t * ROWS + start, count)]
+
+    def left_index(u):
+        return jnp.minimum(u, 4) + jnp.minimum(jnp.maximum(u - 7, 0), 2)
+
+    def right_index(u):
+        return jnp.maximum(u - 3, 0)
+
+    small_rows = (slice(128, 256), slice(384, 512))
+
+    def core_first(u):
+        return copy(u, 0, stage.at[u % STAGES], core_in.at[u], to_core)
+
+    def small_first(t):
+        return copy(UNITS, 25 + t, small_ref.at[1 - core, t], core_in.at[UNITS, small_rows[t]], to_core)
+
+    def produce(u):
+        @pl.when(jnp.logical_and(u >= STAGES, u < UNITS))
+        def _():
+            core_first(u - STAGES).wait_send()
+
+        @pl.when(u < UNITS)
+        def _():
+            right = r_ref[right_index(u), 1 - core]
+            for t in range(3):
+                product = jnp.dot(
+                    lt_ref[left_index(u), t * ROWS : (t + 1) * ROWS], right, preferred_element_type=f32
+                )
+                stage[u % STAGES, t * ROWS : (t + 1) * ROWS] = product.astype(bf16)
+            core_first(u).start()
+
+        @pl.when(u == UNITS)
+        def _():
+            for t in range(2):
+                small_first(t).start()
+
+    def begin(u):
+        @pl.when(u < UNITS)
+        def _():
+            arrived(u, 0, core_in.at[u])
+            right = r_ref[right_index(u), core]
+            for t in range(3):
+                rows = slice(t * ROWS, (t + 1) * ROWS)
+                product = jnp.dot(lt_ref[left_index(u), rows], right, preferred_element_type=f32)
+                part[u, rows] = (product + core_in[u, rows].astype(f32)).astype(bf16)
+                if t < 2:
+                    ab_first(u, t).start()
+
+            @pl.when(outer)
+            def _():
+                c_z1(u).start()
+
+        @pl.when(u == UNITS)
+        def _():
+            for t in range(2):
+                arrived(UNITS, 25 + t, core_in.at[UNITS, small_rows[t]])
+                part[UNITS, t * ROWS : t * ROWS + 128] = pos_ref[t]
+                part[UNITS, small_rows[t]] = (
+                    small_ref[core, t].astype(f32) + core_in[UNITS, small_rows[t]].astype(f32)
+                ).astype(bf16)
+                ab_first(u, t).start()
+
+    def ab_first(u, t):
+        return copy(u, 1 + t, part_rows(u, t, (1 - first[t]) * 128, 128), ab_in.at[u, t, 0:128], to_first[t])
+
+    def ab_second(u, t):
+        row = first[t] * 128 + (1 - second[t]) * 64
+        return copy(u, 3 + t, part_rows(u, t, row, 64), ab_in.at[u, t, 128:192], to_second[t])
+
+    def ab_base(t):
+        return first[t] * 128 + second[t] * 64
+
+    def ab_z1(u, t):
+        return copy(u, 5 + t, part_rows(u, t, ab_base(t), 64), ab_in.at[u, t, 192:256], to_mate)
+
+    def ab_z2(u, t):
+        return copy(
+            u, 7 + t, part_rows(u, t, ab_base(t) + (2 - z) * 32, 32), ab_in.at[u, t, 256:288], to_inner
+        )
+
+    def ab_z3(u, t, row):
+        block = out_rows(u, t, row, 32)
+        return copy(u, 9 + t, block, block, to_inner)
+
+    def ab_z4(u, t):
+        block = out_rows(u, t, ab_base(t), 64)
+        return copy(u, 11 + t, block, block, to_mate)
+
+    def ab_back2(u, t, row):
+        block = out_rows(u, t, row, 64)
+        return copy(u, 13 + t, block, block, to_second[t])
+
+    def ab_back1(u, t, row):
+        block = out_rows(u, t, row, 128)
+        return copy(u, 15 + t, block, block, to_first[t])
+
+    def ab1(u):
+        for t in range(2):
+            arrived(u, 1 + t, ab_in.at[u, t, 0:128])
+            kept = part_rows(u, t, first[t] * 128, 128)
+            added(kept, kept, ab_in.at[u, t, 0:128])
+            ab_second(u, t).start()
+
+    def ab2(u):
+        for t in range(2):
+            arrived(u, 3 + t, ab_in.at[u, t, 128:192])
+            kept = part_rows(u, t, ab_base(t), 64)
+            added(kept, kept, ab_in.at[u, t, 128:192])
+
+        @pl.when(outer)
+        def _():
+            for t in range(2):
+                ab_z1(u, t).start()
+
+    def ab3_inner(u):
+        for t in range(2):
+            arrived(u, 5 + t, ab_in.at[u, t, 192:256])
+            kept = part_rows(u, t, ab_base(t), 64)
+            added(kept, kept, ab_in.at[u, t, 192:256])
+            ab_z2(u, t).start()
+
+    def ab4_inner(u):
+        for t in range(2):
+            arrived(u, 7 + t, ab_in.at[u, t, 256:288])
+            row = ab_base(t) + (z - 1) * 32
+            added(out_rows(u, t, row, 32), part_rows(u, t, row, 32), ab_in.at[u, t, 256:288])
+            ab_z3(u, t, row).start()
+
+    def ab5_inner(u):
+        for t in range(2):
+            arrived(u, 9 + t, out_rows(u, t, ab_base(t) + (2 - z) * 32, 32))
+            ab_z4(u, t).start()
+            ab_back2(u, t, ab_base(t)).start()
+
+    def ab5_outer(u):
+        for t in range(2):
+            arrived(u, 11 + t, out_rows(u, t, ab_base(t), 64))
+            ab_back2(u, t, ab_base(t)).start()
+
+    def ab6(u):
+        for t in range(2):
+            arrived(u, 13 + t, out_rows(u, t, first[t] * 128 + (1 - second[t]) * 64, 64))
+            ab_back1(u, t, first[t] * 128).start()
+
+    def place(u, h, row, count, act):
+        def columns(base):
+            return pl.ds(pl.multiple_of(base + h * COLS, 128), COLS)
+
+        @pl.when(u < 4)
+        def _():
+            act(down_hbm.at[pl.ds(pl.multiple_of(u * 768 + row, 16), count), columns(0)])
+
+        @pl.when(jnp.logical_and(u >= 4, u < 8))
+        def _():
+            act(up_hbm.at[row : row + count, columns((u - 4) * 768)])
+
+        @pl.when(u == 8)
+        def _():
+            act(out_hbm.at[row : row + count, columns(0)])
+
+        @pl.when(jnp.logical_and(u >= 9, u < UNITS))
+        def _():
+            act(qkv_hbm.at[row : row + count, columns((u - 9) * 768)])
+
+    def to_other(u, k, row, count):
+        return lambda dst: copy(u, k, full.at[u, row : row + count], dst, to_core)
+
+    def to_own(u, k, row, count):
+        return lambda dst: pltpu.make_async_copy(full.at[u, row : row + count], dst, local_sem.at[u, k])
+
+    def spread_ab(u):
+        place(u, core, 0, 512, lambda dst: to_other(u, 27, 0, 512)(dst).start())
+        place(u, core, 0, 512, lambda dst: to_own(u, 0, 0, 512)(dst).start())
+
+    def spread_c(u):
+        place(u, core, 512, 256, lambda dst: to_other(u, 28, 512, 256)(dst).start())
+        place(u, core, 512, 256, lambda dst: to_own(u, 1, 512, 256)(dst).start())
+
+    def small_out(h, t):
+        return small_hbm.at[pl.ds(pl.multiple_of(h * 128, 128), 128), t * COLS : (t + 1) * COLS]
+
+    def small_other(t):
+        return copy(UNITS, 27 + t, full.at[UNITS, small_rows[t]], small_out(core, t), to_core)
+
+    def small_own(t):
+        return pltpu.make_async_copy(
+            full.at[UNITS, small_rows[t]], small_out(core, t), local_sem.at[UNITS, t]
+        )
+
+    def pos_own(t):
+        return pltpu.make_async_copy(
+            full.at[UNITS, t * ROWS : t * ROWS + 128],
+            pos_hbm.at[:, t * COLS : (t + 1) * COLS],
+            local_sem.at[UNITS, 2 + t],
+        )
+
+    def ab7(u):
+        for t in range(2):
+            arrived(u, 15 + t, out_rows(u, t, (1 - first[t]) * 128, 128))
+        spread_ab(u)
+
+        @pl.when(u == UNITS)
+        def _():
+            for t in range(2):
+                small_other(t).start()
+                small_own(t).start()
+                pos_own(t).start()
+
+    far = 64 * (1 - side)
+    own_end = 192 * side
+    shard = z * 64
+    half = shard + x * 32
+    mine = half + y * 16
+
+    def c_z1(u):
+        return copy(u, 17, part_rows(u, 2, far, 192), c_in.at[u, 0:192], to_mate)
+
+    def c_z2(u):
+        return copy(u, 18, part_rows(u, 2, (1 - side) * 128, 128), c_in.at[u, 192:320], to_inner)
+
+    def c_z3(u):
+        return copy(u, 19, part_rows(u, 2, own_end, 64), c_in.at[u, 320:384], to_mate)
+
+    def c_x(u):
+        return copy(u, 20, part_rows(u, 2, shard + (1 - x) * 32, 32), c_in.at[u, 384:416], to_x)
+
+    def c_y(u):
+        return copy(u, 21, part_rows(u, 2, half + (1 - y) * 16, 16), c_in.at[u, 416:432], to_y)
+
+    def c_back_y(u, row):
+        block = out_rows(u, 2, row, 16)
+        return copy(u, 22, block, block, to_y)
+
+    def c_back_x(u, row):
+        block = out_rows(u, 2, row, 32)
+        return copy(u, 23, block, block, to_x)
+
+    def c_z4(u):
+        block = out_rows(u, 2, own_end, 64)
+        return copy(u, 24, block, block, to_mate)
+
+    def c_z5(u, row):
+        block = out_rows(u, 2, row, 128)
+        return copy(u, 25, block, block, to_inner)
+
+    def c_z6(u):
+        block = out_rows(u, 2, far, 192)
+        return copy(u, 26, block, block, to_mate)
+
+    def c1_inner(u):
+        arrived(u, 17, c_in.at[u, 0:192])
+        kept = part_rows(u, 2, far, 192)
+        added(kept, kept, c_in.at[u, 0:192])
+        c_z2(u).start()
+
+    def c2_inner(u):
+        arrived(u, 18, c_in.at[u, 192:320])
+        kept = part_rows(u, 2, side * 128, 128)
+        added(kept, kept, c_in.at[u, 192:320])
+        c_z3(u).start()
+        c_x(u).start()
+
+    def c3_outer(u):
+        arrived(u, 19, c_in.at[u, 320:384])
+        kept = part_rows(u, 2, shard, 64)
+        added(kept, kept, c_in.at[u, 320:384])
+        c_x(u).start()
+
+    def c4(u):
+        arrived(u, 20, c_in.at[u, 384:416])
+        kept = part_rows(u, 2, half, 32)
+        added(kept, kept, c_in.at[u, 384:416])
+        c_y(u).start()
+
+    def c5(u):
+        arrived(u, 21, c_in.at[u, 416:432])
+        added(out_rows(u, 2, mine, 16), part_rows(u, 2, mine, 16), c_in.at[u, 416:432])
+        c_back_y(u, mine).start()
+
+    def c6(u):
+        arrived(u, 22, out_rows(u, 2, half + (1 - y) * 16, 16))
+        c_back_x(u, half).start()
+
+    def c7(u):
+        arrived(u, 23, out_rows(u, 2, shard + (1 - x) * 32, 32))
+
+    def c7_outer(u):
+        c7(u)
+        c_z4(u).start()
+
+    def c8_inner(u):
+        arrived(u, 24, out_rows(u, 2, own_end, 64))
+        c_z5(u, side * 128).start()
+
+    def c9_inner(u):
+        arrived(u, 25, out_rows(u, 2, (1 - side) * 128, 128))
+        c_z6(u).start()
+        spread_c(u)
+
+    def c10_outer(u):
+        arrived(u, 26, out_rows(u, 2, far, 192))
+        spread_c(u)
+
+    everyone, inners, outers = None, inner, outer
+    events = [
+        (0, UNITS + 1, everyone, produce),
+        (1, UNITS + 1, everyone, begin),
+        (2, UNITS + 1, everyone, ab1),
+        (2, UNITS, inners, c1_inner),
+        (3, UNITS, inners, c2_inner),
+        (3, UNITS + 1, everyone, ab2),
+        (4, UNITS, outers, c3_outer),
+        (4, UNITS + 1, inners, ab3_inner),
+        (4, UNITS, inners, c4),
+        (5, UNITS, outers, c4),
+        (5, UNITS + 1, inners, ab4_inner),
+        (5, UNITS, inners, c5),
+        (6, UNITS, outers, c5),
+        (6, UNITS + 1, inners, ab5_inner),
+        (6, UNITS, inners, c6),
+        (7, UNITS, outers, c6),
+        (7, UNITS + 1, outers, ab5_outer),
+        (7, UNITS, inners, c7),
+        (8, UNITS, outers, c7_outer),
+        (8, UNITS + 1, everyone, ab6),
+        (9, UNITS, inners, c8_inner),
+        (9, UNITS + 1, everyone, ab7),
+        (10, UNITS, inners, c9_inner),
+        (11, UNITS, outers, c10_outer),
+    ]
+
+    def step(t, carried):
+        for lag, count, who, event in events:
+            u = t - lag
+            now = jnp.logical_and(u >= 0, u < count)
+            if who is not None:
+                now = jnp.logical_and(now, who)
+            pl.when(now)(lambda event=event, u=u: event(u))
+        return carried
+
+    lax.fori_loop(0, UNITS + 11, step, 0)
+
+    def drain(u, carried):
+        @pl.when(u < UNITS)
+        def _():
+            place(u, core, 0, 512, lambda dst: to_other(u, 27, 0, 512)(dst).wait_send())
+            place(u, core, 0, 512, lambda dst: to_own(u, 0, 0, 512)(dst).wait())
+            place(u, 1 - core, 0, 512, lambda dst: to_other(u, 27, 0, 512)(dst).wait_recv())
+            place(u, core, 512, 256, lambda dst: to_other(u, 28, 512, 256)(dst).wait_send())
+            place(u, core, 512, 256, lambda dst: to_own(u, 1, 512, 256)(dst).wait())
+            place(u, 1 - core, 512, 256, lambda dst: to_other(u, 28, 512, 256)(dst).wait_recv())
+            c_x(u).wait_send()
+            c_y(u).wait_send()
+            c_back_y(u, mine).wait_send()
+            c_back_x(u, half).wait_send()
+
+            @pl.when(outer)
+            def _():
+                c_z1(u).wait_send()
+                c_z4(u).wait_send()
+
+            @pl.when(inner)
+            def _():
+                c_z2(u).wait_send()
+                c_z3(u).wait_send()
+                c_z5(u, side * 128).wait_send()
+                c_z6(u).wait_send()
+
+        for t in range(2):
+            ab_first(u, t).wait_send()
+            ab_second(u, t).wait_send()
+            ab_back2(u, t, ab_base(t)).wait_send()
+            ab_back1(u, t, first[t] * 128).wait_send()
+
+        @pl.when(outer)
+        def _():
+            for t in range(2):
+                ab_z1(u, t).wait_send()
+
+        @pl.when(inner)
+        def _():
+            for t in range(2):
+                ab_z2(u, t).wait_send()
+                ab_z3(u, t, ab_base(t) + (z - 1) * 32).wait_send()
+                ab_z4(u, t).wait_send()
+
+        return carried
+
+    lax.fori_loop(0, UNITS + 1, drain, 0)
+    for u in range(UNITS - STAGES, UNITS):
+        core_first(u).wait_send()
+    for t in range(2):
+        small_first(t).wait_send()
+        small_other(t).wait_send()
+        arrived(UNITS, 27 + t, small_out(1 - core, t))
+        small_own(t).wait()
+        pos_own(t).wait()
+
+
+def summed_grads(lt, r, pos, small):
+    vmem = pl.BlockSpec(memory_space=pltpu.VMEM)
+    hbm = pl.BlockSpec(memory_space=pl.ANY)
+    return pl.pallas_call(
+        grads_kernel,
+        out_shape=(
+            jax.ShapeDtypeStruct((3072, 768), bf16),
+            jax.ShapeDtypeStruct((768, 3072), bf16),
+            jax.ShapeDtypeStruct((768, 768), bf16),
+            jax.ShapeDtypeStruct((768, 2304), bf16),
+            jax.ShapeDtypeStruct((128, 768), bf16),
+            jax.ShapeDtypeStruct((256, 768), bf16),
+        ),
+        in_specs=[vmem] * 4,
+        out_specs=(hbm,) * 6,
+        scratch_shapes=[
+            pltpu.VMEM((STAGES, 3 * ROWS, COLS), bf16),
+            pltpu.VMEM((UNITS + 1, 3 * ROWS, COLS), bf16),
+            pltpu.VMEM((UNITS + 1, 3 * ROWS, COLS), bf16),
+            pltpu.VMEM((UNITS + 1, 3 * ROWS, COLS), bf16),
+            pltpu.VMEM((UNITS + 1, 2, 288, COLS), bf16),
+            pltpu.VMEM((UNITS, 432, COLS), bf16),
+            pltpu.SemaphoreType.DMA((UNITS + 1, 29)),
+            pltpu.SemaphoreType.DMA((UNITS + 1, 29)),
+            pltpu.SemaphoreType.DMA((UNITS + 1, 4)),
+        ],
+        compiler_params=pltpu.CompilerParams(
+            collective_id=0, has_side_effects=True, vmem_limit_bytes=58 << 20
+        ),
+        name="grads",
+    )(lt, r, pos, small)
 
 
 def forward(latents, valid, class_rows, seq_place, weights):
@@ -195,10 +692,6 @@
     new_latents, logdet_part, factor, top_low, saved = forward(
         latents, valid, class_rows, seq_place, weights
     )
-    latents_again, unused = lax.optimization_barrier((latents, new_latents))
-    unused_a, unused_b, unused_c, unused_d, saved = forward(
-        latents_again, valid, class_rows, seq_place, weights
-    )
     valid_float = valid.astype(jnp.float32)
     d_alpha = -cot_latents * new_latents - cot_logdet[:, None, None]
     d_mean = -cot_latents * factor
@@ -226,12 +719,12 @@
             activated,
         ) = saved[layer_index]
         d_down = d_hidden.astype(jnp.bfloat16)
-        down_grad = outer_sum(activated, d_down)
+        down_grad = (activated, d_down)
         d_act = transposed(d_down, down_weight[layer_index])
         unused_gelu, gelu_pull = jax.vjp(lambda inner: jax.nn.gelu(inner, approximate=True), preact)
         d_pre = gelu_pull(d_act)[0].astype(jnp.bfloat16)
         up_bias_grad = jnp.sum(d_pre.astype(jnp.float32), (0, 1))
-        up_grad = outer_sum(second, d_pre)
+        up_grad = (second, d_pre)
         d_second = transposed(d_pre, up_weight[layer_index])
         unused_norm, norm_pull = jax.vjp(
             layer_norm,
@@ -242,7 +735,7 @@
         d_mid_norm, ln2_gain_part, ln2_bias_part = norm_pull(d_second)
         d_mid = d_hidden + d_mid_norm
         d_proj = d_mid.astype(jnp.bfloat16)
-        out_grad = outer_sum(attended, d_proj)
+        out_grad = (attended, d_proj)
         d_attended = transposed(d_proj, out_weight[layer_index]).astype(jnp.bfloat16)
         d_attended = d_attended.reshape(images, patch_rows, head_count, HEAD_DIM)
         logits = masked_scores(query, keys, allowed)
@@ -279,7 +772,7 @@
             ),
             -1,
         ).astype(jnp.bfloat16)
-        qkv_grad = outer_sum(normed, d_packed)
+        qkv_grad = (normed, d_packed)
         d_normed = transposed(d_packed, qkv_weight[layer_index])
         unused_norm, norm_pull = jax.vjp(
             layer_norm,
@@ -303,6 +796,110 @@
     latents_grad = cot_latents * factor + transposed(d_embed_low, patch_weight)
     pos_part = jnp.sum(d_hidden, 0)
     class_part = jnp.sum(d_hidden, 1)
+    small_parts = (
+        patch_grad_part,
+        head_weight_grad,
+        head_bias_grad,
+        grads_g1[0],
+        grads_b1[0],
+        grads_g2[0],
+        grads_b2[0],
+        grads_ub[0],
+    )
+    if lax.axis_size("dp") == 16 and lax.axis_size("seq") == 2:
+        return (new_latents,) + kernel_sums(
+            logdet_part, latents_grad, pos_part, class_part, label_hot, class_labels, small_parts,
+            grads_qkv[0], grads_out[0], grads_up[0], grads_down[0],
+        )
+    return (new_latents,) + plain_sums(
+        logdet_part, latents_grad, pos_part, class_part, label_hot, small_parts,
+        grads_qkv[0], grads_out[0], grads_up[0], grads_down[0],
+    )
+
+
+def kernel_sums(
+    logdet_part, latents_grad, pos_part, class_part, label_hot, class_labels, small_parts, qkv, out, up, down
+):
+    dp = lax.axis_index("dp")
+    count = lax.axis_size("dp")
+    patch, head, head_bias, g1, b1, g2, b2, ub = small_parts
+    model_width = 768
+
+    def columns(matrix):
+        width = matrix.shape[-1] // model_width
+        return matrix.reshape(128, width, model_width).transpose(1, 0, 2)
+
+    lefts = jnp.concatenate(
+        (columns(down[0][0]), columns(up[0][0]), columns(out[0][0]), columns(qkv[0][0]))
+    ).transpose(0, 2, 1)
+    rights = jnp.concatenate(
+        (columns(down[1][0]), columns(up[1][0]), columns(out[1][0]), columns(qkv[1][0]))
+    )
+    rights = rights.reshape(9, 128, 2, COLS).transpose(0, 2, 1, 3)
+    slot = (lax.iota(jnp.int32, count) == dp).astype(f32)
+    misc = jnp.concatenate(
+        (head_bias, slot * logdet_part[0], jnp.zeros((model_width - head_bias.shape[0] - count,), f32))
+    )
+    small = jnp.concatenate(
+        (
+            patch,
+            head.T,
+            slot[:, None] * class_part,
+            g1[None],
+            b1[None],
+            g2[None],
+            b2[None],
+            ub.reshape(4, model_width),
+            misc[None],
+            jnp.zeros((256 - 169, model_width), f32),
+        )
+    ).astype(bf16)
+    small = small.reshape(2, 128, 2, COLS).transpose(0, 2, 1, 3)
+    pos = pos_part.astype(bf16).reshape(128, 2, COLS).transpose(1, 0, 2)
+    down_sum, up_sum, out_sum, qkv_sum, pos_sum, small_sum = summed_grads(lefts, rights, pos, small)
+    pos_grad = pos_sum.astype(f32)
+    sums = small_sum.astype(f32)
+    class_rows = sums[144:160]
+    misc = sums[168]
+    owned = label_hot.shape[1] // count
+    own_rows = dp * owned + lax.iota(jnp.int32, owned)
+    own = (stored_labels(class_labels)[:, None] == own_rows[None, :]).astype(f32)
+    class_grad = lax.dot_general(
+        own, class_rows, (((0,), (0,)), ((), ())), precision=precise, preferred_element_type=f32
+    )
+    logdet = lax.dynamic_slice_in_dim(misc, head_bias.shape[0] + dp, 1)
+
+    return (
+        logdet,
+        latents_grad,
+        sums[:48],
+        pos_grad,
+        class_grad,
+        sums[160:161],
+        sums[161:162],
+        qkv_sum.astype(f32)[None],
+        out_sum.astype(f32)[None],
+        sums[162:163],
+        sums[163:164],
+        up_sum.astype(f32)[None],
+        sums[164:168].reshape(1, -1),
+        down_sum.astype(f32)[None],
+        sums[48:144].T,
+        misc[: head_bias.shape[0]],
+    )
+
+
+def stored_labels(class_labels):
+    place = lax.iota(jnp.int32, class_labels.shape[0])
+    less = class_labels[:, None] < class_labels[None, :]
+    tie = (class_labels[:, None] == class_labels[None, :]) & (place[:, None] < place[None, :])
+    rank = jnp.sum((less | tie).astype(jnp.int32), 0)
+    return jnp.sum(jnp.where(rank[:, None] == place[None, :], class_labels[:, None], 0), 0)
+
+
+def plain_sums(
+    logdet_part, latents_grad, pos_part, class_part, label_hot, small_parts, qkv, out, up, down
+):
     logdet, class_sums = lax.psum((logdet_part, class_part), "seq")
     class_term = lax.dot_general(
         label_hot.astype(jnp.float32),
@@ -313,74 +910,31 @@
     )
     class_grad = lax.psum_scatter(class_term, "dp", scatter_dimension=0, tiled=True)
     pos_grad = lax.psum(pos_part, "dp")
-    (
-        patch_weight_grad,
-        head_weight_grad,
-        head_bias_grad,
-        ln1_gain_grad,
-        ln1_bias_grad,
-        ln2_gain_grad,
-        ln2_bias_grad,
-        up_bias_grad,
-    ) = lax.psum(
-        (
-            patch_grad_part,
-            head_weight_grad,
-            head_bias_grad,
-            jnp.stack(grads_g1),
-            jnp.stack(grads_b1),
-            jnp.stack(grads_g2),
-            jnp.stack(grads_b2),
-            jnp.stack(grads_ub),
-        ),
-        ("dp", "seq"),
-    )
-    qkv_stack = jnp.stack(grads_qkv)
-    out_stack = jnp.stack(grads_out)
-    up_stack = jnp.stack(grads_up)
-    down_stack = jnp.stack(grads_down)
-    flat_parts = (
-        lax.psum_scatter(eight_rows(qkv_stack), ("dp", "seq"), scatter_dimension=1, tiled=True),
-        lax.psum_scatter(eight_rows(out_stack), ("dp", "seq"), scatter_dimension=1, tiled=True),
-        lax.psum_scatter(eight_rows(up_stack), ("dp", "seq"), scatter_dimension=1, tiled=True),
-        lax.psum_scatter(eight_rows(down_stack), ("dp", "seq"), scatter_dimension=1, tiled=True),
-    )
-    flat_qkv, flat_out, flat_up, flat_down = (
-        lax.all_gather(
-            flat_parts[0].astype(jnp.bfloat16), ("dp", "seq"), axis=1, tiled=True
-        ).astype(jnp.float32),
-        lax.all_gather(
-            flat_parts[1].astype(jnp.bfloat16), ("dp", "seq"), axis=1, tiled=True
-        ).astype(jnp.float32),
-        lax.all_gather(
-            flat_parts[2].astype(jnp.bfloat16), ("dp", "seq"), axis=1, tiled=True
-        ).astype(jnp.float32),
-        lax.all_gather(
-            flat_parts[3].astype(jnp.bfloat16), ("dp", "seq"), axis=1, tiled=True
-        ).astype(jnp.float32),
-    )
-    qkv_stack = flat_qkv.reshape(qkv_stack.shape)
-    out_stack = flat_out.reshape(out_stack.shape)
-    up_stack = flat_up.reshape(up_stack.shape)
-    down_stack = flat_down.reshape(down_stack.shape)
+    patch, head, head_bias, g1, b1, g2, b2, ub = lax.psum(small_parts, ("dp", "seq"))
+
+    def gathered(pair):
+        grad = outer_sum(*pair)
+        share = lax.psum_scatter(eight_rows(grad), ("dp", "seq"), scatter_dimension=1, tiled=True)
+        every = lax.all_gather(share.astype(jnp.bfloat16), ("dp", "seq"), axis=1, tiled=True)
+        return every.astype(jnp.float32).reshape((1,) + grad.shape)
+
     return (
-        new_latents,
         logdet,
         latents_grad,
-        patch_weight_grad,
+        patch,
         pos_grad,
         class_grad,
-        ln1_gain_grad,
-        ln1_bias_grad,
-        qkv_stack,
-        out_stack,
-        ln2_gain_grad,
-        ln2_bias_grad,
-        up_stack,
-        up_bias_grad,
-        down_stack,
-        head_weight_grad,
-        head_bias_grad,
+        g1[None],
+        b1[None],
+        gathered(qkv),
+        gathered(out),
+        g2[None],
+        b2[None],
+        gathered(up),
+        ub[None],
+        gathered(down),
+        head,
+        head_bias,
     )
 
 

time: 1260 us -> 299 us (0.24)
  waiting for transfers between devices: 991 us -> 0.8 us
  Pallas kernels: 0 us -> 132 us
  blocking collectives: 44.9 us -> 0 us
  local copies, waits for them, and re-layouts: 84.4 us -> 48.8 us
  matrix products: 68.3 us -> 42.6 us
  other arithmetic: 34.9 us -> 56.8 us
  between operations: 17 us -> 3.69 us
    reduce_scatter x5 -> x0, waiting for transfers between devices: 580 us -> none  [the longest x1 140 us: local(): lax.psum_scatter(eight_rows(down_stack), ('dp', 'seq'), scatter_dimension...]
    psum x2 -> x0, waiting for transfers between devices: 239 us -> none  [the longest x1 124 us: local(): lax.psum((patch_grad_part, head_weight_grad, head_bias_grad, jnp.stack(gr...]
    all_gather x4 -> x0, waiting for transfers between devices: 169 us -> none  [the longest x1 59.6 us: local(): lax.all_gather(flat_parts[2].astype(jnp.bfloat16), ('dp', 'seq'), axis=1,...]
    pallas_call x0 -> x1, Pallas kernels: none -> 132 us  [summed_grads(): pl.pallas_call(grads_kernel, out_shape=(jax.ShapeDtypeStruct((3072, 768),...]
    psum x2 -> x0, blocking collectives: 44.9 us -> none  [the longest x1 41.3 us: local(): lax.psum((patch_grad_part, head_weight_grad, head_bias_grad, jnp.stack(gr...]
    another operation x8 -> x1, local copies, waits for them, and re-layouts: 29.9 us -> 2.32 us  [columns(): return matrix.reshape(128, width, model_width).transpose(1, 0, 2)]
    reshape x4 -> x1, local copies, waits for them, and re-layouts: 25.3 us -> 1.29 us  [kernel_sums(): ub.reshape(4, model_width)]
    dot_general x6 -> x2, matrix products: 23.1 us -> 2.1 us  [outer_sum(): lax.dot_general(left_flat, grad_flat, (((0,), (0,)), ((), ())), preferred...]
  transfers between devices with their start and end apart: 20 -> 7, of which waited for: 12 -> 1; matrix products, arithmetic and copies ran while one was open for 10% -> 11% of each run, Pallas kernels for 0% -> 0%
where the time goes in v1:
time: 299 us; the launch traced here: 298 us
  Pallas kernels  132 us (44%)
  other arithmetic  56.8 us (19%)
  local copies, waits for them, and re-layouts  48.8 us (16%)
  matrix products  42.6 us (14%)
  starting transfers between devices  12.6 us (4%)
  between operations  3.69 us (1%)
    pallas_call x1, Pallas kernels, summed_grads(): pl.pallas_call(grads_kernel, out_shape=(jax.ShapeDtypeStruct((3072, 768),...  132 us
    dot_general x6, matrix products, transposed(): lax.dot_general(grad_side, weight_mat, (((grad_side.ndim - 1,), (1,)), ((...  16.5 us
    ppermute x7, starting transfers between devices, shifted_2(): return lax.ppermute(shard, axis, pairs)  12.6 us
    dot_general x7, matrix products, matmul(): return jnp.dot(left_side, weight_mat, preferred_element_type=jnp.float32)  12.6 us
    unnamed x169, local copies, waits for them, and re-layouts  7.21 us
    broadcast_in_dim x1, other arithmetic, kernel_sums(): down_sum.astype(f32)[None]  7.21 us
    concatenate x4, local copies, waits for them, and re-layouts, kernel_sums(): jnp.concatenate((columns(down[1][0]), columns(up[1][0]), columns(out[1][0...  6.06 us
  transfers between devices with their start and end apart: 7, of which 1 were waited for; matrix products, arithmetic and copies ran while one was open for 11% of the time, Pallas kernels for 0%

profile of v1, /device:TPU:0, one launch (start us, length us, event | category | flops | bytes accessed | tf_op | source)
XLA Modules:
  0.0 297.6 jit_solution(1404244405948032694)
XLA Ops:
  0.7 1.9 copy.81
  5.3 1.7 convolution_reduce_fusion
  9.7 3.0 %collective-permute-start.2 = (bf16[1,128,768]{2,1,0:T(8,128)(2,1)}, bf16[1,128,768]{2,1,0:T(8,128)(2,1)}, u32[]{:S(2)}, u32[]{:S(2)}) collective-permute-start(bf16[1,128,768]{2,1,0:T(8,128)(2,1)} %get-tuple-element.39), channel_id=1, source_target_pairs={{0,1},{2,3},{4,5},{6,7},{8,9},{10,11},{12,13},{14,15},{16,17},{18,... | collective-permute-start | bytes 589832 | tf_op jit(solution)/shard_map/ppermute | solution.py:18
  13.3 1.9 collective-permute-start.1
  15.1 2.0 collective-permute-start
  17.7 1.7 copy.84
  27.3 1.4 compare_or_fusion
  28.7 1.8 pad_maximum_fusion.2
  30.5 1.9 copy.85
  32.4 1.6 fusion.86
  35.7 1.8 pad_maximum_fusion.1
  37.5 1.9 copy.83
  39.4 2.1 convolution_convert_fusion.1
  42.8 4.8 %multiply_convert_fusion.1 = (bf16[128,3072]{1,0:T(8,128)(2,1)S(1)}, f32[128,3072]{1,0:T(8,128)}) fusion(f32[3072]{0:T(1024)S(1)} %bitcast.208, bf16[1,768,3072]{2,1,0:T(8,128)(2,1)} %param.33, f32[128,768]{0,1:T(8,128)S(1)} %get-tuple-element.60, f32[768]{0:T(1024)S(1)} %copy-done.47, f32[768]{0:T(1024)S(1)} %get-tuple-element.76, f32[128]{0:T(128)S(1)} %fusion.73, ...), kind=kOutput, calls=%fused_computation.29 | convolution fusion | flops 608403456 | bytes 7490560 | tf_op jit(solution)/shard_map/dot_general | solution.py:28
  47.6 4.2 %fusion.34 = bf16[128,768]{0,1:T(8,128)(2,1)S(1)} fusion(f32[128,768]{0,1:T(8,128)S(1)} %get-tuple-element.60, bf16[128,3072]{1,0:T(8,128)(2,1)S(1)} %get-tuple-element.61, bf16[1,3072,768]{2,1,0:T(8,128)(2,1)} %param.35), kind=kOutput, calls=%fused_computation.45 | convolution fusion | flops 604176384 | bytes 6094848 | tf_op jit(solution)/shard_map/dot_general | solution.py:28
  53.2 1.8 collective-permute-start.3
  55.0 2.3 copy.89
  60.1 2.0 multiply_subtract_fusion
  64.7 1.5 collective-permute-start.4
  68.1 2.2 fusion.88
  70.2 5.5 %fusion.91 = (bf16[3072]{0:T(1024)(128)(2,1)}, bf16[128,3072]{1,0:T(8,128)(2,1)S(1)}) fusion(f32[128,3072]{1,0:T(8,128)} %get-tuple-element.62, bf16[128,768]{1,0:T(8,128)(2,1)S(1)} %get-tuple-element.63, bf16[1,3072,768]{2,1,0:T(8,128)(2,1)} %param.35), kind=kOutput, calls=%fused_computation.165 | convolution fusion | flops 612234240 | bytes 7280640 | tf_op jit(solution)/shard_map/dot_general | solution.py:40
  75.7 3.0 %fusion.90 = (bf16[768]{0:T(1024)(128)(2,1)}, f32[128,768]{1,0:T(8,128)}) fusion(bf16[128,3072]{1,0:T(8,128)(2,1)S(1)} %get-tuple-element.72, bf16[1,768,3072]{2,1,0:T(8,128)(2,1)S(1)} %bitcast.178), kind=kOutput, calls=%fused_computation.164 | convolution fusion | flops 604077312 | bytes 5899776 | tf_op jit(solution)/shard_map/dot_general | solution.py:40
  78.7 1.9 copy.93
  80.7 2.0 multiply_reduce_fusion.1
  83.3 2.2 fusion.81
  85.5 1.9 copy.94
  89.2 2.5 fusion.37
  91.7 1.7 copy.95
  93.5 2.5 multiply_reduce_fusion
  100.5 2.3 copy.108
  102.8 1.7 copy.91
  104.6 1.4 reduce.48
  107.9 1.7 slice.153
  110.9 1.7 slice.152
  116.4 1.7 copy.98
  118.1 2.3 copy.97
  120.4 1.7 copy.96
  122.1 1.9 convolution_convert_fusion.2
  126.3 2.6 fusion.89
  135.4 1.5 maximum_bitcast_fusion.r_ref
  138.2 132.2 %grads.1 = (bf16[3072,768]{1,0:T(8,128)(2,1)}, bf16[768,3072]{1,0:T(8,128)(2,1)}, bf16[768,768]{1,0:T(8,128)(2,1)}, bf16[768,2304]{1,0:T(8,128)(2,1)}, bf16[128,...) custom-call(bf16[7,768,128]{2,1,0:T(8,128)(2,1)} %maximum_bitcast_fusion.1.lt_ref, ...), custom_call_target="tpu_custom_call" | custom-call | tf_op jit(solution)/shard_map/grads/pallas_call | solution.py:531
  272.8 1.6 slice.113
  274.4 1.5 fusion.84
  276.6 7.2 %bitcast_convert_fusion = f32[1,3072,768]{2,1,0:T(8,128)} fusion(bf16[3072,768]{1,0:T(8,128)(2,1)} %get-tuple-element.28), kind=kLoop, calls=%fused_computation | loop fusion | flops 2359296 | bytes 14155776 | tf_op jit(solution)/shard_map/broadcast_in_dim | solution.py:886
  283.8 5.0 %bitcast_convert_fusion.1 = f32[1,768,3072]{2,1,0:T(8,128)} fusion(bf16[768,3072]{1,0:T(8,128)(2,1)S(1)} %bitcast.180), kind=kLoop, calls=%fused_computation.1 | loop fusion | flops 2359296 | bytes 14155776 | tf_op jit(solution)/shard_map/broadcast_in_dim | solution.py:884
  288.9 3.5 %bitcast_convert_fusion.2 = f32[1,768,2304]{2,1,0:T(8,128)} fusion(bf16[768,2304]{1,0:T(8,128)(2,1)S(1)} %copy-done.13), kind=kLoop, calls=%fused_computation.12 | loop fusion | flops 1769472 | bytes 10616832 | tf_op jit(solution)/shard_map/broadcast_in_dim | solution.py:880
  292.4 1.6 bitcast_convert_fusion.3
  295.4 1.7 fusion.56
  (254 shorter events, 52.6 us)
Async XLA Ops:
  0.7 7.4 %copy-start = (bf16[1,768,2304]{2,1,0:T(8,128)(2,1)S(1)}, bf16[1,768,2304]{2,1,0:T(8,128)(2,1)}, u32[]{:S(2)}) copy-start(bf16[1,768,2304]{2,1,0:T(8,128)(2,1)} %param.29) | copy-start | bytes 10616836
  0.7 6.8 %copy-start.63 = (bf16[1,768]{1,0:T(2,128)(2,1)S(1)}, bf16[1,768]{1,0:T(2,128)(2,1)}, u32[]{:S(2)}) copy-start(bf16[1,768]{1,0:T(2,128)(2,1)} %param.27) | copy-start | bytes 4612
  0.7 6.8 %copy-start.62 = (bf16[1,768]{1,0:T(2,128)(2,1)S(1)}, bf16[1,768]{1,0:T(2,128)(2,1)}, u32[]{:S(2)}) copy-start(bf16[1,768]{1,0:T(2,128)(2,1)} %param.28) | copy-start | bytes 4612
  2.6 4.4 %copy-start.31 = (bf16[128,768]{0,1:T(8,128)(2,1)S(1)}, bf16[128,768]{0,1:T(8,128)(2,1)}, u32[]{:S(2)}) copy-start(bf16[128,768]{0,1:T(8,128)(2,1)} %copy.81) | copy-start | bytes 589828
  2.6 4.4 %copy-start.40 = (bf16[48,768]{1,0:T(8,128)(2,1)S(1)}, bf16[48,768]{1,0:T(8,128)(2,1)}, u32[]{:S(2)}) copy-start(bf16[48,768]{1,0:T(8,128)(2,1)} %param.24) | copy-start | bytes 221188
  2.6 4.4 %copy-start.42 = (f32[1,128,48]{1,2,0:T(8,128)S(1)}, f32[1,128,48]{1,2,0:T(8,128)}, u32[]{:S(2)}) copy-start(f32[1,128,48]{1,2,0:T(8,128)} %param.20) | copy-start | bytes 73732
  8.0 4.7 %copy-start.77 = (s32[1,128]{1,0:T(1,128)S(1)}, s32[1,128]{1,0:T(1,128)}, u32[]{:S(2)}) copy-start(s32[1,128]{1,0:T(1,128)} %param.21) | copy-start | bytes 1540
  8.1 9.1 %copy-start.78 = (s32[16]{0:T(128)S(1)}, s32[16]{0:T(128)}, u32[]{:S(2)}) copy-start(s32[16]{0:T(128)} %param.22) | copy-start | bytes 196
  8.9 14.0 %copy-start.64 = (bf16[1,768]{1,0:T(2,128)(2,1)S(1)}, bf16[1,768]{1,0:T(2,128)(2,1)}, u32[]{:S(2)}) copy-start(bf16[1,768]{1,0:T(2,128)(2,1)} %param.32) | copy-start | bytes 4612
  8.9 14.0 %copy-start.65 = (bf16[1,768]{1,0:T(2,128)(2,1)S(1)}, bf16[1,768]{1,0:T(2,128)(2,1)}, u32[]{:S(2)}) copy-start(bf16[1,768]{1,0:T(2,128)(2,1)} %param.31) | copy-start | bytes 4612
  9.7 19.0 %collective-permute-start.2 = (bf16[1,128,768]{2,1,0:T(8,128)(2,1)}, bf16[1,128,768]{2,1,0:T(8,128)(2,1)}, u32[]{:S(2)}, u32[]{:S(2)}) collective-permute-start(bf16[1,128,768]{2,1,0:T(8,128)(2,1)} %get-tuple-element.39), channel_id=1, source_target_pairs={{0,1},{2,3},{4,5},{6,7},{8,9},{10,11},{12,13},{14,15},{16,17},{18,... | collective-permute-start | bytes 589832 | tf_op jit(solution)/shard_map/ppermute | solution.py:18
  13.3 13.3 %collective-permute-start.1 = (bf16[1,128]{1,0:T(2,128)(2,1)}, bf16[1,128]{1,0:T(2,128)(2,1)}, u32[]{:S(2)}, u32[]{:S(2)}) collective-permute-start(bf16[1,128]{1,0:T(2,128)(2,1)} %get-tuple-element.54), channel_id=1, source_target_pairs={{0,1},{2,3},{4,5},{6,7},{8,9},{10,11},{12,13},{14,15},{16,17},{18,... | collective-permute-start | bytes 776 | tf_op jit(solution)/shard_map/ppermute | solution.py:18
  15.1 20.5 %collective-permute-start = (bf16[1,128,768]{2,1,0:T(8,128)(2,1)}, bf16[1,128,768]{2,1,0:T(8,128)(2,1)}, u32[]{:S(2)}, u32[]{:S(2)}) collective-permute-start(bf16[1,128,768]{2,1,0:T(8,128)(2,1)} %get-tuple-element.41), channel_id=1, source_target_pairs={{0,1},{2,3},{4,5},{6,7},{8,9},{10,11},{12,13},{14,15},{16,17},{18,... | collective-permute-start | bytes 589832 | tf_op jit(solution)/shard_map/ppermute | solution.py:18
  42.1 5.5 %copy-start.7 = (f32[128,768]{0,1:T(8,128)}, f32[128,768]{0,1:T(8,128)S(1)}, u32[]{:S(2)}) copy-start(f32[128,768]{0,1:T(8,128)S(1)} %get-tuple-element.60) | copy-start | bytes 1179652
  42.1 5.4 %copy-start.58 = (f32[128]{0:T(128)}, f32[128]{0:T(128)S(1)}, u32[]{:S(2)}) copy-start(f32[128]{0:T(128)S(1)} %broadcast_multiply_fusion) | copy-start | bytes 1540
  42.3 5.3 %copy-start.61 = (f32[128]{0:T(128)}, f32[128]{0:T(128)S(1)}, u32[]{:S(2)}) copy-start(f32[128]{0:T(128)S(1)} %fusion.73) | copy-start | bytes 1540
  47.6 4.3 %copy-start.8 = (bf16[128,3072]{1,0:T(8,128)(2,1)}, bf16[128,3072]{1,0:T(8,128)(2,1)S(1)}, u32[]{:S(2)}) copy-start(bf16[128,3072]{1,0:T(8,128)(2,1)S(1)} %get-tuple-element.61) | copy-start | bytes 2359300
  47.6 4.3 %copy-start.36 = (bf16[768,96]{0,1:T(8,128)(2,1)S(1)}, bf16[768,96]{0,1:T(8,128)(2,1)}, u32[]{:S(2)}) copy-start(bf16[768,96]{0,1:T(8,128)(2,1)} %param.36) | copy-start | bytes 442372
  47.6 4.3 %copy-start.76 = (f32[96]{0:T(128)S(1)}, f32[96]{0:T(128)}, u32[]{:S(2)}) copy-start(f32[96]{0:T(128)} %convert_element_type.233) | copy-start | bytes 1156
  53.2 4.0 %collective-permute-start.3 = (f32[1,96]{1,0:T(1,128)}, f32[1,96]{1,0:T(1,128)}, u32[]{:S(2)}, u32[]{:S(2)}) collective-permute-start(f32[1,96]{1,0:T(1,128)} %bitcast.79), channel_id=1, source_target_pairs={{0,1},{2,3},{4,5},{6,7},{8,9},{10,11},{12,13},{14,15},{16,17},{18,... | collective-permute-start | bytes 1160 | tf_op jit(solution)/shard_map/ppermute | solution.py:18
  64.7 3.4 %collective-permute-start.4 = (bf16[1,96]{0,1:T(8,128)(2,1)}, bf16[1,96]{0,1:T(8,128)(2,1)}, u32[]{:S(2)}, u32[]{:S(2)}) collective-permute-start(bf16[1,96]{0,1:T(8,128)(2,1)} %slice_bitcast_fusion.1), channel_id=1, source_target_pairs={{1,0},{3,2},{5,4},{7,6},{9,8},{11,10},{13,12},{15,14},{17,16},{19,... | collective-permute-start | bytes 584 | tf_op jit(solution)/shard_map/ppermute | solution.py:18
  68.1 7.6 %slice-start = ((s8[4718592]{0:T(1024)(128)(4,1)}), s8[4194304]{0:T(1024)(128)(4,1)S(1)}, s32[]{:S(2)}) async-start(s8[4718592]{0:T(1024)(128)(4,1)} %bitcast.177), calls=%async_computation | async-start | bytes 8388608
  70.2 5.5 %copy-start.30 = (bf16[128,768]{1,0:T(8,128)(2,1)}, bf16[128,768]{1,0:T(8,128)(2,1)S(1)}, u32[]{:S(2)}) copy-start(bf16[128,768]{1,0:T(8,128)(2,1)S(1)} %get-tuple-element.63) | copy-start | bytes 589828
  70.2 5.5 %slice-start.1 = ((s8[4718592]{0:T(1024)(128)(4,1)}), s8[524288]{0:T(1024)(128)(4,1)S(1)}, s32[]{:S(2)}) async-start(s8[4718592]{0:T(1024)(128)(4,1)} %bitcast.177), calls=%async_computation.1 | async-start | bytes 1048576
  75.7 3.0 %copy-start.16 = (bf16[128,3072]{1,0:T(8,128)(2,1)}, bf16[128,3072]{1,0:T(8,128)(2,1)S(1)}, u32[]{:S(2)}) copy-start(bf16[128,3072]{1,0:T(8,128)(2,1)S(1)} %get-tuple-element.72) | copy-start | bytes 2359300
  85.5 6.3 %copy-start.66 = (f32[128]{0:T(128)}, f32[128]{0:T(128)S(1)}, u32[]{:S(2)}) copy-start(f32[128]{0:T(128)S(1)} %negate_multiply_fusion.2) | copy-start | bytes 1540
  100.5 5.4 %copy-start.75 = (bf16[96]{0:T(256)(128)(2,1)S(1)}, bf16[96]{0:T(256)(128)(2,1)}, u32[]{:S(2)}) copy-start(bf16[96]{0:T(256)(128)(2,1)} %get-tuple-element.51) | copy-start | bytes 580
  100.5 13.4 %copy-start.57 = (bf16[768]{0:T(1024)(128)(2,1)S(1)}, bf16[768]{0:T(1024)(128)(2,1)}, u32[]{:S(2)}) copy-start(bf16[768]{0:T(1024)(128)(2,1)} %get-tuple-element.31) | copy-start | bytes 4612
  100.5 14.0 %copy-start.56 = (bf16[768]{0:T(1024)(128)(2,1)S(1)}, bf16[768]{0:T(1024)(128)(2,1)}, u32[]{:S(2)}) copy-start(bf16[768]{0:T(1024)(128)(2,1)} %get-tuple-element.69) | copy-start | bytes 4612
  109.6 14.4 %collective-permute-start.5 = (bf16[1,128,768]{1,2,0:T(8,128)(2,1)}, bf16[1,128,768]{1,2,0:T(8,128)(2,1)}, u32[]{:S(2)}, u32[]{:S(2)}) collective-permute-start(bf16[1,128,768]{1,2,0:T(8,128)(2,1)} %slice.153), channel_id=1, source_target_pairs={{1,0},{3,2},{5,4},{7,6},{9,8},{11,10},{13,12},{15,14},{17,16},{19,... | collective-permute-start | bytes 589832 | tf_op jit(solution)/shard_map/ppermute | solution.py:18
  112.6 12.5 %collective-permute-start.6 = (bf16[1,128,768]{1,2,0:T(8,128)(2,1)}, bf16[1,128,768]{1,2,0:T(8,128)(2,1)}, u32[]{:S(2)}, u32[]{:S(2)}) collective-permute-start(bf16[1,128,768]{1,2,0:T(8,128)(2,1)} %slice.152), channel_id=1, source_target_pairs={{1,0},{3,2},{5,4},{7,6},{9,8},{11,10},{13,12},{15,14},{17,16},{19,... | collective-permute-start | bytes 589832 | tf_op jit(solution)/shard_map/ppermute | solution.py:18
  122.1 4.2 %copy-start.32 = (bf16[12,64,128]{2,1,0:T(8,128)(2,1)S(1)}, bf16[12,64,128]{2,1,0:T(8,128)(2,1)}, u32[]{:S(2)}) copy-start(bf16[12,64,128]{2,1,0:T(8,128)(2,1)} %fusion.40) | copy-start | bytes 589828
  125.1 3.8 %copy-start.26 = (bf16[1,128,768]{1,2,0:T(8,128)(2,1)}, bf16[1,128,768]{1,2,0:T(8,128)(2,1)S(1)}, u32[]{:S(2)}) copy-start(bf16[1,128,768]{1,2,0:T(8,128)(2,1)S(1)} %fusion.50) | copy-start | bytes 589828
  126.3 4.0 %copy-start.52 = (f32[128]{0:T(128)S(1)}, f32[128]{0:T(128)}, u32[]{:S(2)}) copy-start(f32[128]{0:T(128)} %copy-done.51) | copy-start | bytes 1540
  129.0 2.9 copy-start.10
  129.0 2.9 copy-start.11
  129.0 2.9 copy-start.49
  129.0 2.9 copy-start.67
  270.4 5.4 %copy-start.39 = (f32[1,128,96]{1,2,0:T(8,128)S(1)}, f32[1,128,96]{1,2,0:T(8,128)}, u32[]{:S(2)}) copy-start(f32[1,128,96]{1,2,0:T(8,128)} %copy-done.38) | copy-start | bytes 147460
  270.4 5.4 %copy-start.41 = (bf16[48,768]{1,0:T(8,128)(2,1)S(1)}, bf16[48,768]{1,0:T(8,128)(2,1)}, u32[]{:S(2)}) copy-start(bf16[48,768]{1,0:T(8,128)(2,1)} %param.24) | copy-start | bytes 221188
  270.4 5.4 %copy-start.45 = (f32[1,128,48]{1,2,0:T(8,128)S(1)}, f32[1,128,48]{1,2,0:T(8,128)}, u32[]{:S(2)}) copy-start(f32[1,128,48]{1,2,0:T(8,128)} %param.38) | copy-start | bytes 73732
  275.8 8.0 %slice-start.2 = ((s8[4718592]{0:T(1024)(128)(4,1)}), s8[4194304]{0:T(1024)(128)(4,1)S(1)}, s32[]{:S(2)}) async-start(s8[4718592]{0:T(1024)(128)(4,1)} %bitcast.179), calls=%async_computation.2 | async-start | bytes 8388608
  276.6 7.2 %slice-start.3 = ((s8[4718592]{0:T(1024)(128)(4,1)}), s8[524288]{0:T(1024)(128)(4,1)S(1)}, s32[]{:S(2)}) async-start(s8[4718592]{0:T(1024)(128)(4,1)} %bitcast.179), calls=%async_computation.3 | async-start | bytes 1048576
  283.8 5.1 %copy-start.13 = (bf16[768,2304]{1,0:T(8,128)(2,1)S(1)}, bf16[768,2304]{1,0:T(8,128)(2,1)}, u32[]{:S(2)}) copy-start(bf16[768,2304]{1,0:T(8,128)(2,1)} %get-tuple-element.25) | copy-start | bytes 10616836
  288.9 3.5 %copy-start.23 = (bf16[768,768]{1,0:T(8,128)(2,1)S(1)}, bf16[768,768]{1,0:T(8,128)(2,1)}, u32[]{:S(2)}) copy-start(bf16[768,768]{1,0:T(8,128)(2,1)} %get-tuple-element.26) | copy-start | bytes 3538948
  292.4 5.3 %copy-start.1 = (bf16[1,768,2304]{2,1,0:T(8,128)(2,1)S(1)}, bf16[1,768,2304]{2,1,0:T(8,128)(2,1)}, u32[]{:S(2)}) copy-start(bf16[1,768,2304]{2,1,0:T(8,128)(2,1)} %param.29) | copy-start | bytes 10616836
  292.4 3.0 %copy-start.69 = (s32[64]{0:T(128)S(1)}, s32[64]{0:T(128)}, u32[]{:S(2)}) copy-start(s32[64]{0:T(128)} %iota_add_fusion.1) | copy-start | bytes 772
  292.4 3.0 %copy-start.70 = (s32[16]{0:T(128)S(1)}, s32[16]{0:T(128)}, u32[]{:S(2)}) copy-start(s32[16]{0:T(128)} %select_reduce_fusion) | copy-start | bytes 196
  (42 other events, 61.2 us)

commit v2 on v1

--- a/solution.py
+++ b/solution.py
@@ -68,14 +68,25 @@
 ROWS = 256
 COLS = 384
 STAGES = 3
+CHUNK = 32
+GELU_A = (2.0 / 3.141592653589793) ** 0.5
+GELU_B = 0.044715
 f32 = jnp.float32
 bf16 = jnp.bfloat16
 
 
-def grads_kernel(
-    lt_ref, r_ref, pos_ref, small_ref,
-    down_hbm, up_hbm, out_hbm, qkv_hbm, pos_hbm, small_hbm,
+def flow_kernel(
+    labels_sm, perm_sm, cot_logdet_sm,
+    latents_ref, valid_ref, patch_ref, pos_table_ref, g1_ref, b1_ref, g2_ref, b2_ref,
+    up_bias_ref, head_w_ref, head_b_ref, cot_ref,
+    class_hbm, qkv_any, out_any, up_any, down_any,
+    down_hbm, up_hbm, out_hbm, qkv_hbm, pos_hbm, small_hbm, latents_hbm,
     stage, part, full, core_in, ab_in, c_in, send_sem, recv_sem, local_sem,
+    qkv_w, out_w, up_w, down_w, load_sem,
+    lat_pad, cot_pad, patch_pad, head_pad, hidden, mid, xhat1, xhat2, scale1, scale2,
+    keys, values, query, attended, bias, prior_mask, mask_row, probs, slope, d_hidden, d_second, d_att, d_keys, d_values,
+    d_prior, d_back, row_out, row_in, grad_out, grad_in, lat_out,
+    lt_ref, r_ref, pos_ref, small_ref, ub_grad, low_top, exch_send, exch_recv, lat_sem,
 ):
     dp = lax.axis_index("dp")
     core = lax.axis_index("seq")
@@ -91,6 +102,17 @@
 
     def rows_at(start, count):
         return pl.ds(pl.multiple_of(start, 16), count)
+
+    sources = [class_hbm.at[r : r + n, h * COLS : (h + 1) * COLS] for h in range(2) for r, n in ((0, 768), (768, 256))]
+    targets = [part.at[2 * h + i, 0:n] for h in range(2) for i, n in ((0, 768), (1, 256))]
+    sources += [qkv_any.at[0], out_any.at[0], up_any.at[0], down_any.at[0]]
+    targets += [qkv_w, out_w, up_w, down_w]
+
+    def load(i):
+        return pltpu.make_async_copy(sources[i], targets[i], load_sem.at[i])
+
+    for i in range(8):
+        load(i).start()
 
     barrier = pltpu.get_barrier_semaphore()
     for target in (to_core, to_x, to_y, to_mate):
@@ -466,7 +488,328 @@
             pl.when(now)(lambda event=event, u=u: event(u))
         return carried
 
+    mm_nt = (((1,), (1,)), ((), ()))
+    mm_tn = (((0,), (0,)), ((), ()))
+
+    def nt(left, right):
+        return lax.dot_general(left, right, mm_nt, preferred_element_type=f32)
+
+    def tn(left, right):
+        return lax.dot_general(left, right, mm_tn, preferred_element_type=f32)
+
+    def nn(left, right):
+        return jnp.dot(left, right, preferred_element_type=f32)
+
+    def exchange(k, src, dst):
+        return pltpu.make_async_remote_copy(
+            src_ref=src, dst_ref=dst, send_sem=exch_send.at[k], recv_sem=exch_recv.at[k],
+            device_id=to_core, device_id_type=MESH,
+        )
+
+    chunks = [slice(r, r + CHUNK) for r in range(0, 128, CHUNK)]
+    lane = lax.broadcasted_iota(jnp.int32, (128, 128), 1)
+    row = lax.broadcasted_iota(jnp.int32, (128, 128), 0)
+    eye = row == lane
+    low_half = lane < 64
+    valid_row = valid_ref[...].astype(f32)
+    valid_col = jnp.sum(jnp.where(eye, valid_row, 0.0), axis=1, keepdims=True)
+    mask_row[...] = jnp.broadcast_to(valid_row, (8, 128))
+    lat_pad[...] = jnp.zeros((128, 128), f32)
+    lat_pad[:, 0:48] = latents_ref[0]
+    cot_pad[...] = jnp.zeros((128, 128), f32)
+    cot_pad[:, 0:48] = cot_ref[0]
+    patch_pad[...] = jnp.zeros((128, 768), bf16)
+    patch_pad[0:48] = patch_ref[...]
+    head_pad[...] = jnp.zeros((768, 128), bf16)
+    head_pad[:, 0:96] = head_w_ref[...]
+    head_bias = jnp.concatenate((head_b_ref[...].astype(f32), jnp.zeros((1, 32), f32)), 1)
+
+    @pl.when(core == 0)
+    def _():
+        keys[0:128] = jnp.zeros((128, 768), bf16)
+        values[0:128] = jnp.zeros((128, 768), bf16)
+        prior_mask[...] = jnp.zeros((8, 128), f32)
+        row_in[...] = jnp.zeros((8, 128), f32)
+
+    @pl.when(core == 1)
+    def _():
+        grad_in[...] = jnp.zeros((8, 128), f32)
+        d_back[...] = jnp.zeros((2, 128, 768), bf16)
+
+    @pl.when(core == 0)
+    def _():
+        exchange(2, mask_row, prior_mask).start()
+
+    def normalize(src, hat, scale, gain, shift, put):
+        for r in chunks:
+            v = src[r]
+            center = v - jnp.mean(v, -1, keepdims=True)
+            inv = lax.rsqrt(jnp.mean(center * center, -1, keepdims=True) + norm_eps)
+            scaled = center * inv
+            hat[r] = scaled
+            scale[r] = inv
+            put(r, scaled * gain + shift)
+
+    label = labels_sm[perm_sm[0]]
+    hot = jnp.where(lax.broadcasted_iota(jnp.int32, (16, 1024), 1) == label, 1.0, 0.0).astype(bf16)
+    for i in range(4):
+        load(i).wait()
+    class_row = jnp.concatenate(
+        [nn(hot[:, 0:768], part[2 * h]) + nn(hot[:, 768:1024], part[2 * h + 1, 0:256]) for h in range(2)], 1
+    )[0:1]
+    hidden[...] = (
+        nn(lat_pad[...].astype(bf16), patch_pad[...]) + pos_table_ref[...].astype(f32) + class_row
+    )
+
+    def put_low(r, v):
+        low_top[r] = v.astype(bf16)
+
+    normalize(hidden, xhat1, scale1, g1_ref[...].astype(f32), b1_ref[...].astype(f32), put_low)
+    load(4).wait()
+    normed = low_top[...]
+    keys[128:256] = nn(normed, qkv_w[:, 768:1536]).astype(bf16)
+
+    @pl.when(core == 0)
+    def _():
+        exchange(0, keys.at[128:256], keys.at[0:128]).start()
+
+    values[128:256] = nn(normed, qkv_w[:, 1536:2304]).astype(bf16)
+
+    @pl.when(core == 0)
+    def _():
+        exchange(1, values.at[128:256], values.at[0:128]).start()
+
+    query[...] = nn(normed, qkv_w[:, 0:768]).astype(bf16)
+    lt_ref[6] = normed.astype(f32).T.astype(bf16)
+
+    @pl.when(core == 1)
+    def _():
+        exchange(2, mask_row, prior_mask).wait_recv()
+        exchange(0, keys.at[128:256], keys.at[0:128]).wait_recv()
+        exchange(1, values.at[128:256], values.at[0:128]).wait_recv()
+
+    bias[:, 0:128] = jnp.where(jnp.broadcast_to(prior_mask[0:1], (128, 128)) > 0.5, 0.0, -1e30)
+    bias[:, 128:256] = jnp.where(((lane < row) & (valid_row > 0.5)) | eye, 0.0, -1e30)
+
+    def columns128(p):
+        return pl.ds(pl.multiple_of(p * 128, 128), 128)
+
+    def attend(p, carried):
+        cols = columns128(p)
+        q_pair = query[:, cols]
+        k_pair = keys[:, cols]
+        v_pair = values[:, cols]
+        outs = []
+        for i in range(2):
+            q_one = jnp.where(low_half if i == 0 else lane >= 64, q_pair, jnp.zeros_like(q_pair))
+            scores = nt(q_one, k_pair) * 0.125 + bias[...]
+            top = jnp.max(scores, -1, keepdims=True)
+            powers = jnp.exp(scores - top)
+            soft = powers * (1.0 / jnp.sum(powers, -1, keepdims=True))
+            probs[2 * p + i] = soft
+            outs.append(nn(soft.astype(bf16), v_pair))
+        attended[:, cols] = jnp.where(low_half, outs[0], outs[1]).astype(bf16)
+        return carried
+
+    lax.fori_loop(0, 6, attend, 0)
+    load(5).wait()
+    mid[...] = hidden[...] + nn(attended[...], out_w[...])
+    lt_ref[5] = attended[...].astype(f32).T.astype(bf16)
+    normalize(mid, xhat2, scale2, g2_ref[...].astype(f32), b2_ref[...].astype(f32), put_low)
+    lt_ref[4] = low_top[...].astype(f32).T.astype(bf16)
+    load(6).wait()
+    load(7).wait()
+    d_hidden[...] = mid[...]
+
+    def rows768(j):
+        return pl.ds(pl.multiple_of(j * 768, 128), 768)
+
+    def feed(j, carried):
+        d_second[...] = nn(low_top[...], up_w[:, rows768(j)])
+        shift = up_bias_ref[:, rows768(j)].astype(f32)
+        for r in chunks:
+            pre = d_second[r] + shift
+            square = pre * pre
+            bend = jnp.tanh(pre * (GELU_A + (GELU_A * GELU_B) * square))
+            left = 0.5 * (1.0 + bend)
+            slope[j, r] = left + 0.5 * pre * (1.0 - bend * bend) * (GELU_A + (3.0 * GELU_A * GELU_B) * square)
+            d_second[r] = pre * left
+        act = d_second[...]
+        lt_ref[j] = act.T.astype(bf16)
+        d_hidden[...] += nn(act.astype(bf16), down_w[rows768(j)])
+        return carried
+
+    lax.fori_loop(0, 4, feed, 0)
+    low_top[...] = d_hidden[...].astype(bf16)
+    row_out[...] = nn(low_top[...], head_pad[...]) + head_bias
+
+    @pl.when(core == 0)
+    def _():
+        exchange(3, row_out.at[120:128], row_in).start()
+
+    rolled = pltpu.roll(row_out[...], 1, 0)
+
+    @pl.when(core == 1)
+    def _():
+        exchange(3, row_out.at[120:128], row_in).wait_recv()
+
+    shifted = jnp.where(row == 0, jnp.broadcast_to(row_in[7:8], (128, 128)), rolled) * valid_col
+    inside = lane < 48
+    alpha = jnp.where(inside, shifted, 0.0)
+    shift_mean = jnp.where(inside, pltpu.roll(shifted, 80, 1), 0.0)
+    factor = jnp.exp(-alpha)
+    new_latents = (lat_pad[...] - shift_mean) * factor
+    lat_out[0] = new_latents
+    logdet = -jnp.sum(jnp.sum(alpha, 1, keepdims=True), 0, keepdims=True)
+    d_alpha = -cot_pad[...] * new_latents - cot_logdet_sm[0]
+    direct = cot_pad[...] * factor
+    lat_out[1] = direct
+    grad_out[...] = (
+        jnp.where(inside, d_alpha, pltpu.roll(jnp.where(inside, -direct, 0.0), 48, 1)) * valid_col
+    )
+
+    @pl.when(core == 1)
+    def _():
+        exchange(4, grad_out.at[0:8], grad_in).start()
+
+    rolled_back = pltpu.roll(grad_out[...], 127, 0)
+
+    @pl.when(core == 0)
+    def _():
+        exchange(4, grad_out.at[0:8], grad_in).wait_recv()
+
+    d_head = jnp.where(row == 127, jnp.broadcast_to(grad_in[0:1], (128, 128)), rolled_back).astype(bf16)
+    head_grad = tn(d_head, low_top[...])
+    head_bias_grad = jnp.sum(d_head.astype(f32), 0, keepdims=True)
+    d_hidden[...] = nt(d_head, head_pad[...])
+    low_top[...] = d_hidden[...].astype(bf16)
+    for h in range(2):
+        r_ref[0, h] = low_top[:, h * COLS : (h + 1) * COLS]
+
+    def put(first_row, value):
+        h, r = first_row // 128, first_row % 128
+        for t in range(2):
+            small_ref[h, t, r : r + value.shape[0]] = value[:, t * COLS : (t + 1) * COLS].astype(bf16)
+
+    put(0, head_grad[0:96])
+
+    d_second[...] = jnp.zeros((128, 768), f32)
+
+    def feed_back(j, carried):
+        d_keys[...] = nt(low_top[...], down_w[rows768(j)])
+        total = jnp.zeros((1, 768), f32)
+        for r in chunks:
+            d_pre = (slope[j, r] * d_keys[r]).astype(bf16)
+            d_att[r] = d_pre
+            total += jnp.sum(d_pre.astype(f32), 0, keepdims=True)
+            for h in range(2):
+                r_ref[1 + j, h, r] = d_pre[:, h * COLS : (h + 1) * COLS]
+        ub_grad[pl.ds(j, 1)] = total
+        d_second[...] += nt(d_att[...], up_w[:, rows768(j)])
+        return carried
+
+    lax.fori_loop(0, 4, feed_back, 0)
+
+    def norm_back(grad, hat, scale, gain, base, out):
+        gain_total = jnp.zeros((1, 768), f32)
+        shift_total = jnp.zeros((1, 768), f32)
+        for r in chunks:
+            d = grad[r]
+            scaled = hat[r]
+            e = d * gain
+            v = e - jnp.mean(e, -1, keepdims=True) - scaled * jnp.mean(e * scaled, -1, keepdims=True)
+            out[r] = base[r] + scale[r] * v
+            gain_total += jnp.sum(d * scaled, 0, keepdims=True)
+            shift_total += jnp.sum(d, 0, keepdims=True)
+        return gain_total, shift_total
+
+    g2_grad, b2_grad = norm_back(d_second, xhat2, scale2, g2_ref[...].astype(f32), d_hidden, mid)
+    low_top[...] = mid[...].astype(bf16)
+    for h in range(2):
+        r_ref[5, h] = low_top[:, h * COLS : (h + 1) * COLS]
+    d_att[...] = nt(low_top[...], out_w[...]).astype(bf16)
+
+    def attend_back(p, carried):
+        cols = columns128(p)
+        q_pair = query[:, cols]
+        k_pair = keys[:, cols]
+        v_pair = values[:, cols]
+        a_pair = d_att[:, cols]
+        dq, dk, dv = [], [], []
+        for i in range(2):
+            own = low_half if i == 0 else lane >= 64
+            a_one = jnp.where(own, a_pair, jnp.zeros_like(a_pair))
+            q_one = jnp.where(own, q_pair, jnp.zeros_like(q_pair))
+            soft = probs[2 * p + i]
+            d_soft = nt(a_one, v_pair)
+            weighted = d_soft * soft
+            d_score = weighted - soft * jnp.sum(weighted, -1, keepdims=True)
+            d_low = d_score.astype(bf16)
+            dq.append(nn(d_low, k_pair))
+            dk.append(tn(d_low, q_one))
+            dv.append(tn(soft.astype(bf16), a_one))
+        h, local = p // 3, pl.ds(pl.multiple_of((p % 3) * 128, 128), 128)
+        r_ref[6, h, :, local] = (jnp.where(low_half, dq[0], dq[1]) * 0.125).astype(bf16)
+        dk_pair = (dk[0] + dk[1]) * 0.125
+        dv_pair = dv[0] + dv[1]
+        d_prior[0, :, cols] = dk_pair[0:128].astype(bf16)
+        d_prior[1, :, cols] = dv_pair[0:128].astype(bf16)
+        d_keys[:, cols] = dk_pair[128:256]
+        d_values[:, cols] = dv_pair[128:256]
+        return carried
+
+    lax.fori_loop(0, 6, attend_back, 0)
+
+    @pl.when(core == 1)
+    def _():
+        exchange(5, d_prior, d_back).start()
+
+    @pl.when(core == 0)
+    def _():
+        exchange(5, d_prior, d_back).wait_recv()
+
+    for h in range(2):
+        cols = slice(h * COLS, (h + 1) * COLS)
+        r_ref[7, h] = (d_keys[:, cols] + d_back[0, :, cols].astype(f32)).astype(bf16)
+        r_ref[8, h] = (d_values[:, cols] + d_back[1, :, cols].astype(f32)).astype(bf16)
+    d_second[...] = sum(
+        nt(r_ref[6 + j, h], qkv_w[:, j * 768 + h * COLS : j * 768 + (h + 1) * COLS])
+        for j in range(3)
+        for h in range(2)
+    )
+    g1_grad, b1_grad = norm_back(d_second, xhat1, scale1, g1_ref[...].astype(f32), mid, d_hidden)
+    low_top[...] = d_hidden[...].astype(bf16)
+    for t in range(2):
+        pos_ref[t] = low_top[:, t * COLS : (t + 1) * COLS]
+    patch_grad = tn(lat_pad[...].astype(bf16), low_top[...])
+    lat_out[1] += nt(low_top[...], patch_pad[...])
+    lat_copy = pltpu.make_async_copy(lat_out, latents_hbm, lat_sem)
+    lat_copy.start()
+    class_grad = jnp.sum(d_hidden[...], 0, keepdims=True)
+    put(96, patch_grad[0:32])
+    put(128, patch_grad[32:48])
+    line = lax.broadcasted_iota(jnp.int32, (16, 768), 0)
+    put(144, jnp.where(line == dp, class_grad, 0.0))
+    lane1 = lax.broadcasted_iota(jnp.int32, (1, 128), 1)
+    high = logdet.astype(bf16).astype(f32)
+    slot = lane1 == core * 16 + dp
+    misc = jnp.concatenate(
+        (
+            head_bias_grad,
+            jnp.where(slot, high, 0.0),
+            jnp.where(slot, logdet - high, 0.0),
+            jnp.zeros((1, 384), f32),
+        ),
+        1,
+    )
+    lines = [g1_grad, b1_grad, g2_grad, b2_grad] + [ub_grad[j : j + 1] for j in range(4)] + [misc]
+    block = jnp.zeros((16, 768), f32)
+    for i, one in enumerate(lines):
+        block = jnp.where(line == i, one, block)
+    put(160, block)
+    put(176, jnp.zeros((80, 768), f32))
     lax.fori_loop(0, UNITS + 11, step, 0)
+
 
     def drain(u, carried):
         @pl.when(u < UNITS)
@@ -523,13 +866,32 @@
         arrived(UNITS, 27 + t, small_out(1 - core, t))
         small_own(t).wait()
         pos_own(t).wait()
-
-
-def summed_grads(lt, r, pos, small):
+    lat_copy.wait()
+
+    @pl.when(core == 0)
+    def _():
+        exchange(2, mask_row, prior_mask).wait_send()
+        exchange(0, keys.at[128:256], keys.at[0:128]).wait_send()
+        exchange(1, values.at[128:256], values.at[0:128]).wait_send()
+        exchange(3, row_out.at[120:128], row_in).wait_send()
+
+    @pl.when(core == 1)
+    def _():
+        exchange(4, grad_out.at[0:8], grad_in).wait_send()
+        exchange(5, d_prior, d_back).wait_send()
+
+
+def flow(
+    class_labels, group_perm, cot_logdet, latents, valid, patch_weight, pos_table, ln1_gain, ln1_bias,
+    ln2_gain, ln2_bias, up_bias, head_weight, head_bias, cot_latents, class_table,
+    qkv_weight, out_weight, up_weight, down_weight,
+):
+    smem = pl.BlockSpec(memory_space=pltpu.SMEM)
     vmem = pl.BlockSpec(memory_space=pltpu.VMEM)
     hbm = pl.BlockSpec(memory_space=pl.ANY)
+    wide = (128, 768)
     return pl.pallas_call(
-        grads_kernel,
+        flow_kernel,
         out_shape=(
             jax.ShapeDtypeStruct((3072, 768), bf16),
             jax.ShapeDtypeStruct((768, 3072), bf16),
@@ -537,9 +899,10 @@
             jax.ShapeDtypeStruct((768, 2304), bf16),
             jax.ShapeDtypeStruct((128, 768), bf16),
             jax.ShapeDtypeStruct((256, 768), bf16),
+            jax.ShapeDtypeStruct((2, 128, 128), f32),
         ),
-        in_specs=[vmem] * 4,
-        out_specs=(hbm,) * 6,
+        in_specs=[smem] * 3 + [vmem] * 12 + [hbm] * 5,
+        out_specs=(hbm,) * 7,
         scratch_shapes=[
             pltpu.VMEM((STAGES, 3 * ROWS, COLS), bf16),
             pltpu.VMEM((UNITS + 1, 3 * ROWS, COLS), bf16),
@@ -550,12 +913,154 @@
             pltpu.SemaphoreType.DMA((UNITS + 1, 29)),
             pltpu.SemaphoreType.DMA((UNITS + 1, 29)),
             pltpu.SemaphoreType.DMA((UNITS + 1, 4)),
+            pltpu.VMEM((768, 2304), bf16),
+            pltpu.VMEM((768, 768), bf16),
+            pltpu.VMEM((768, 3072), bf16),
+            pltpu.VMEM((3072, 768), bf16),
+            pltpu.SemaphoreType.DMA((8,)),
+            pltpu.VMEM((128, 128), f32),
+            pltpu.VMEM((128, 128), f32),
+            pltpu.VMEM(wide, bf16),
+            pltpu.VMEM((768, 128), bf16),
+            pltpu.VMEM(wide, f32),
+            pltpu.VMEM(wide, f32),
+            pltpu.VMEM(wide, f32),
+            pltpu.VMEM(wide, f32),
+            pltpu.VMEM((128, 1), f32),
+            pltpu.VMEM((128, 1), f32),
+            pltpu.VMEM((256, 768), bf16),
+            pltpu.VMEM((256, 768), bf16),
+            pltpu.VMEM(wide, bf16),
+            pltpu.VMEM(wide, bf16),
+            pltpu.VMEM((128, 256), f32),
+            pltpu.VMEM((8, 128), f32),
+            pltpu.VMEM((8, 128), f32),
+            pltpu.VMEM((12, 128, 256), f32),
+            pltpu.VMEM((4, 128, 768), f32),
+            pltpu.VMEM(wide, f32),
+            pltpu.VMEM(wide, f32),
+            pltpu.VMEM(wide, bf16),
+            pltpu.VMEM(wide, f32),
+            pltpu.VMEM(wide, f32),
+            pltpu.VMEM((2, 128, 768), bf16),
+            pltpu.VMEM((2, 128, 768), bf16),
+            pltpu.VMEM((128, 128), f32),
+            pltpu.VMEM((8, 128), f32),
+            pltpu.VMEM((128, 128), f32),
+            pltpu.VMEM((8, 128), f32),
+            pltpu.VMEM((2, 128, 128), f32),
+            pltpu.VMEM((7, 768, 128), bf16),
+            pltpu.VMEM((9, 2, 128, COLS), bf16),
+            pltpu.VMEM((2, 128, COLS), bf16),
+            pltpu.VMEM((2, 2, 128, COLS), bf16),
+            pltpu.VMEM((8, 768), f32),
+            pltpu.VMEM(wide, bf16),
+            pltpu.SemaphoreType.DMA((6,)),
+            pltpu.SemaphoreType.DMA((6,)),
+            pltpu.SemaphoreType.DMA,
         ],
         compiler_params=pltpu.CompilerParams(
-            collective_id=0, has_side_effects=True, vmem_limit_bytes=58 << 20
+            collective_id=0, has_side_effects=True, vmem_limit_bytes=62 << 20
         ),
-        name="grads",
-    )(lt, r, pos, small)
+        name="flow",
+    )(
+        class_labels, group_perm, cot_logdet, latents, valid, patch_weight, pos_table, ln1_gain, ln1_bias,
+        ln2_gain, ln2_bias, up_bias, head_weight, head_bias, cot_latents, class_table,
+        qkv_weight, out_weight, up_weight, down_weight,
+    )
+
+
+def finish_kernel(
+    labels_ref, down_ref, up_ref, out_ref, qkv_ref, pos_ref, small_ref, lat_ref,
+    new_latents, logdet, latents_grad, patch, pos, classes, g1, b1, qkv, out, g2, b2, up, ub, down, head, hb,
+):
+    dp = lax.axis_index("dp")
+    down[0] = down_ref[...].astype(f32)
+    up[0] = up_ref[...].astype(f32)
+    out[0] = out_ref[...].astype(f32)
+    qkv[0] = qkv_ref[...].astype(f32)
+
+    @pl.when(pl.program_id(0) == 0)
+    def _():
+        new_latents[0] = lat_ref[0, :, 0:48]
+        latents_grad[0] = lat_ref[1, :, 0:48]
+        pos[...] = pos_ref[...].astype(f32)
+        patch[...] = small_ref[96:144].astype(f32)
+        head[...] = small_ref[0:128].astype(f32).T[:, 0:96]
+        block = small_ref[160:176].astype(f32)
+        for i, one in enumerate((g1, b1, g2, b2)):
+            one[...] = block[i : i + 1]
+        for i in range(4):
+            ub[:, i * 768 : (i + 1) * 768] = block[4 + i : 5 + i]
+        hb[...] = block[8:9, 0:96]
+        count = labels_ref.shape[1]
+        terms = block[8:9, 128:256] + block[8:9, 256:384]
+        lane = lax.broadcasted_iota(jnp.int32, (1, 128), 1)
+        mine = jnp.logical_or(lane == dp, lane == count + dp)
+        logdet[...] = jnp.sum(jnp.where(mine, terms, 0.0), 1, keepdims=True)
+        by_lane = jnp.broadcast_to(labels_ref[...], (count, count)).astype(f32)
+        first = lax.broadcasted_iota(jnp.int32, (count, count), 0)
+        second = lax.broadcasted_iota(jnp.int32, (count, count), 1)
+        by_row = jnp.sum(jnp.where(first == second, by_lane, 0.0), 1, keepdims=True)
+        before = (by_lane < by_row) | ((by_lane == by_row) & (second < first))
+        rank = jnp.sum(jnp.where(before, 1.0, 0.0), 1, keepdims=True)
+        stored = jnp.sum(jnp.where(rank == second.astype(f32), by_row, 0.0), 0, keepdims=True)
+        owned = classes.shape[0]
+        wanted = (dp * owned + lax.broadcasted_iota(jnp.int32, (owned, count), 0)).astype(f32)
+        hot = jnp.where(stored == wanted, 1.0, 0.0).astype(bf16)
+        classes[...] = jnp.dot(hot, small_ref[144:160], preferred_element_type=f32)
+
+
+def finish(class_labels, down, up, out, qkv, pos, small, lat):
+    steps = 16
+
+    def blocked(rows, width):
+        return pl.BlockSpec((rows // steps, width), lambda i: (i, 0))
+
+    def blocked_out(rows, width):
+        return pl.BlockSpec((1, rows // steps, width), lambda i: (0, i, 0))
+
+    def kept(*shape):
+        return pl.BlockSpec(shape, lambda i: (0,) * len(shape))
+
+    count = class_labels.shape[1]
+    owned = 1024 // count
+    shapes = [
+        (1, 128, 48), (1, 1), (1, 128, 48), (48, 768), (128, 768), (owned, 768), (1, 768), (1, 768),
+        (1, 768, 2304), (1, 768, 768), (1, 768), (1, 768), (1, 768, 3072), (1, 3072), (1, 3072, 768),
+        (768, 96), (1, 96),
+    ]
+    specs = [kept(*shape) for shape in shapes]
+    specs[8], specs[9] = blocked_out(768, 2304), blocked_out(768, 768)
+    specs[12], specs[14] = blocked_out(768, 3072), blocked_out(3072, 768)
+    return pl.pallas_call(
+        finish_kernel,
+        grid=(steps,),
+        out_shape=[jax.ShapeDtypeStruct(shape, f32) for shape in shapes],
+        in_specs=[
+            kept(1, count), blocked(3072, 768), blocked(768, 3072), blocked(768, 768), blocked(768, 2304),
+            kept(128, 768), kept(256, 768), kept(2, 128, 128),
+        ],
+        out_specs=specs,
+        compiler_params=pltpu.CompilerParams(vmem_limit_bytes=40 << 20),
+        name="finish",
+    )(class_labels, down, up, out, qkv, pos, small, lat)
+
+
+def fast_local(
+    latents, valid, class_labels, group_perm, patch_weight, pos_table, class_table, ln1_gain, ln1_bias,
+    qkv_weight, out_weight, ln2_gain, ln2_bias, up_weight, up_bias, down_weight, head_weight, head_bias,
+    cot_latents, cot_logdet,
+):
+    sums = flow(
+        class_labels, group_perm, cot_logdet, latents, valid, patch_weight, pos_table, ln1_gain, ln1_bias,
+        ln2_gain, ln2_bias, up_bias, head_weight, head_bias[None], cot_latents, class_table,
+        qkv_weight, out_weight, up_weight, down_weight,
+    )
+    results = list(finish(class_labels[None], *sums))
+    results[1] = results[1].reshape(1)
+    results[16] = results[16].reshape(96)
+    return tuple(results)
 
 
 def forward(latents, valid, class_rows, seq_place, weights):
@@ -719,12 +1224,12 @@
             activated,
         ) = saved[layer_index]
         d_down = d_hidden.astype(jnp.bfloat16)
-        down_grad = (activated, d_down)
+        down_grad = outer_sum(activated, d_down)
         d_act = transposed(d_down, down_weight[layer_index])
         unused_gelu, gelu_pull = jax.vjp(lambda inner: jax.nn.gelu(inner, approximate=True), preact)
         d_pre = gelu_pull(d_act)[0].astype(jnp.bfloat16)
         up_bias_grad = jnp.sum(d_pre.astype(jnp.float32), (0, 1))
-        up_grad = (second, d_pre)
+        up_grad = outer_sum(second, d_pre)
         d_second = transposed(d_pre, up_weight[layer_index])
         unused_norm, norm_pull = jax.vjp(
             layer_norm,
@@ -735,7 +1240,7 @@
         d_mid_norm, ln2_gain_part, ln2_bias_part = norm_pull(d_second)
         d_mid = d_hidden + d_mid_norm
         d_proj = d_mid.astype(jnp.bfloat16)
-        out_grad = (attended, d_proj)
+        out_grad = outer_sum(attended, d_proj)
         d_attended = transposed(d_proj, out_weight[layer_index]).astype(jnp.bfloat16)
         d_attended = d_attended.reshape(images, patch_rows, head_count, HEAD_DIM)
         logits = masked_scores(query, keys, allowed)
@@ -772,7 +1277,7 @@
             ),
             -1,
         ).astype(jnp.bfloat16)
-        qkv_grad = (normed, d_packed)
+        qkv_grad = outer_sum(normed, d_packed)
         d_normed = transposed(d_packed, qkv_weight[layer_index])
         unused_norm, norm_pull = jax.vjp(
             layer_norm,
@@ -796,110 +1301,6 @@
     latents_grad = cot_latents * factor + transposed(d_embed_low, patch_weight)
     pos_part = jnp.sum(d_hidden, 0)
     class_part = jnp.sum(d_hidden, 1)
-    small_parts = (
-        patch_grad_part,
-        head_weight_grad,
-        head_bias_grad,
-        grads_g1[0],
-        grads_b1[0],
-        grads_g2[0],
-        grads_b2[0],
-        grads_ub[0],
-    )
-    if lax.axis_size("dp") == 16 and lax.axis_size("seq") == 2:
-        return (new_latents,) + kernel_sums(
-            logdet_part, latents_grad, pos_part, class_part, label_hot, class_labels, small_parts,
-            grads_qkv[0], grads_out[0], grads_up[0], grads_down[0],
-        )
-    return (new_latents,) + plain_sums(
-        logdet_part, latents_grad, pos_part, class_part, label_hot, small_parts,
-        grads_qkv[0], grads_out[0], grads_up[0], grads_down[0],
-    )
-
-
-def kernel_sums(
-    logdet_part, latents_grad, pos_part, class_part, label_hot, class_labels, small_parts, qkv, out, up, down
-):
-    dp = lax.axis_index("dp")
-    count = lax.axis_size("dp")
-    patch, head, head_bias, g1, b1, g2, b2, ub = small_parts
-    model_width = 768
-
-    def columns(matrix):
-        width = matrix.shape[-1] // model_width
-        return matrix.reshape(128, width, model_width).transpose(1, 0, 2)
-
-    lefts = jnp.concatenate(
-        (columns(down[0][0]), columns(up[0][0]), columns(out[0][0]), columns(qkv[0][0]))
-    ).transpose(0, 2, 1)
-    rights = jnp.concatenate(
-        (columns(down[1][0]), columns(up[1][0]), columns(out[1][0]), columns(qkv[1][0]))
-    )
-    rights = rights.reshape(9, 128, 2, COLS).transpose(0, 2, 1, 3)
-    slot = (lax.iota(jnp.int32, count) == dp).astype(f32)
-    misc = jnp.concatenate(
-        (head_bias, slot * logdet_part[0], jnp.zeros((model_width - head_bias.shape[0] - count,), f32))
-    )
-    small = jnp.concatenate(
-        (
-            patch,
-            head.T,
-            slot[:, None] * class_part,
-            g1[None],
-            b1[None],
-            g2[None],
-            b2[None],
-            ub.reshape(4, model_width),
-            misc[None],
-            jnp.zeros((256 - 169, model_width), f32),
-        )
-    ).astype(bf16)
-    small = small.reshape(2, 128, 2, COLS).transpose(0, 2, 1, 3)
-    pos = pos_part.astype(bf16).reshape(128, 2, COLS).transpose(1, 0, 2)
-    down_sum, up_sum, out_sum, qkv_sum, pos_sum, small_sum = summed_grads(lefts, rights, pos, small)
-    pos_grad = pos_sum.astype(f32)
-    sums = small_sum.astype(f32)
-    class_rows = sums[144:160]
-    misc = sums[168]
-    owned = label_hot.shape[1] // count
-    own_rows = dp * owned + lax.iota(jnp.int32, owned)
-    own = (stored_labels(class_labels)[:, None] == own_rows[None, :]).astype(f32)
-    class_grad = lax.dot_general(
-        own, class_rows, (((0,), (0,)), ((), ())), precision=precise, preferred_element_type=f32
-    )
-    logdet = lax.dynamic_slice_in_dim(misc, head_bias.shape[0] + dp, 1)
-
-    return (
-        logdet,
-        latents_grad,
-        sums[:48],
-        pos_grad,
-        class_grad,
-        sums[160:161],
-        sums[161:162],
-        qkv_sum.astype(f32)[None],
-        out_sum.astype(f32)[None],
-        sums[162:163],
-        sums[163:164],
-        up_sum.astype(f32)[None],
-        sums[164:168].reshape(1, -1),
-        down_sum.astype(f32)[None],
-        sums[48:144].T,
-        misc[: head_bias.shape[0]],
-    )
-
-
-def stored_labels(class_labels):
-    place = lax.iota(jnp.int32, class_labels.shape[0])
-    less = class_labels[:, None] < class_labels[None, :]
-    tie = (class_labels[:, None] == class_labels[None, :]) & (place[:, None] < place[None, :])
-    rank = jnp.sum((less | tie).astype(jnp.int32), 0)
-    return jnp.sum(jnp.where(rank[:, None] == place[None, :], class_labels[:, None], 0), 0)
-
-
-def plain_sums(
-    logdet_part, latents_grad, pos_part, class_part, label_hot, small_parts, qkv, out, up, down
-):
     logdet, class_sums = lax.psum((logdet_part, class_part), "seq")
     class_term = lax.dot_general(
         label_hot.astype(jnp.float32),
@@ -910,31 +1311,74 @@
     )
     class_grad = lax.psum_scatter(class_term, "dp", scatter_dimension=0, tiled=True)
     pos_grad = lax.psum(pos_part, "dp")
-    patch, head, head_bias, g1, b1, g2, b2, ub = lax.psum(small_parts, ("dp", "seq"))
-
-    def gathered(pair):
-        grad = outer_sum(*pair)
-        share = lax.psum_scatter(eight_rows(grad), ("dp", "seq"), scatter_dimension=1, tiled=True)
-        every = lax.all_gather(share.astype(jnp.bfloat16), ("dp", "seq"), axis=1, tiled=True)
-        return every.astype(jnp.float32).reshape((1,) + grad.shape)
-
+    (
+        patch_weight_grad,
+        head_weight_grad,
+        head_bias_grad,
+        ln1_gain_grad,
+        ln1_bias_grad,
+        ln2_gain_grad,
+        ln2_bias_grad,
+        up_bias_grad,
+    ) = lax.psum(
+        (
+            patch_grad_part,
+            head_weight_grad,
+            head_bias_grad,
+            jnp.stack(grads_g1),
+            jnp.stack(grads_b1),
+            jnp.stack(grads_g2),
+            jnp.stack(grads_b2),
+            jnp.stack(grads_ub),
+        ),
+        ("dp", "seq"),
+    )
+    qkv_stack = jnp.stack(grads_qkv)
+    out_stack = jnp.stack(grads_out)
+    up_stack = jnp.stack(grads_up)
+    down_stack = jnp.stack(grads_down)
+    flat_parts = (
+        lax.psum_scatter(eight_rows(qkv_stack), ("dp", "seq"), scatter_dimension=1, tiled=True),
+        lax.psum_scatter(eight_rows(out_stack), ("dp", "seq"), scatter_dimension=1, tiled=True),
+        lax.psum_scatter(eight_rows(up_stack), ("dp", "seq"), scatter_dimension=1, tiled=True),
+        lax.psum_scatter(eight_rows(down_stack), ("dp", "seq"), scatter_dimension=1, tiled=True),
+    )
+    flat_qkv, flat_out, flat_up, flat_down = (
+        lax.all_gather(
+            flat_parts[0].astype(jnp.bfloat16), ("dp", "seq"), axis=1, tiled=True
+        ).astype(jnp.float32),
+        lax.all_gather(
+            flat_parts[1].astype(jnp.bfloat16), ("dp", "seq"), axis=1, tiled=True
+        ).astype(jnp.float32),
+        lax.all_gather(
+            flat_parts[2].astype(jnp.bfloat16), ("dp", "seq"), axis=1, tiled=True
+        ).astype(jnp.float32),
+        lax.all_gather(
+            flat_parts[3].astype(jnp.bfloat16), ("dp", "seq"), axis=1, tiled=True
+        ).astype(jnp.float32),
+    )
+    qkv_stack = flat_qkv.reshape(qkv_stack.shape)
+    out_stack = flat_out.reshape(out_stack.shape)
+    up_stack = flat_up.reshape(up_stack.shape)
+    down_stack = flat_down.reshape(down_stack.shape)
     return (
+        new_latents,
         logdet,
         latents_grad,
-        patch,
+        patch_weight_grad,
         pos_grad,
         class_grad,
-        g1[None],
-        b1[None],
-        gathered(qkv),
-        gathered(out),
-        g2[None],
-        b2[None],
-        gathered(up),
-        ub[None],
-        gathered(down),
-        head,
-        head_bias,
+        ln1_gain_grad,
+        ln1_bias_grad,
+        qkv_stack,
+        out_stack,
+        ln2_gain_grad,
+        ln2_bias_grad,
+        up_stack,
+        up_bias_grad,
+        down_stack,
+        head_weight_grad,
+        head_bias_grad,
     )
 
 
@@ -980,4 +1424,5 @@
         P(),
         P(),
     )
-    return jax.shard_map(local, mesh=mesh, in_specs=in_specs, out_specs=out_specs, check_vma=False)
+    body = fast_local if mesh.shape["dp"] == 16 and mesh.shape["seq"] == 2 else local
+    return jax.shard_map(body, mesh=mesh, in_specs=in_specs, out_specs=out_specs, check_vma=False)

time: 299 us -> 186 us (0.62)
  other arithmetic: 56.8 us -> 0 us
  matrix products: 42.6 us -> 0 us
  Pallas kernels: 132 us -> 168 us
  local copies, waits for them, and re-layouts: 48.8 us -> 15.3 us
  starting transfers between devices: 12.6 us -> 0 us
    dot_general x22 -> x0, matrix products: 42.6 us -> none  [the longest x6 16.5 us: transposed(): lax.dot_general(grad_side, weight_mat, (((grad_side.ndim - 1,), (1,)), ((...]
    pallas_call x1 -> x2, Pallas kernels: 132 us -> 168 us  [the longest x1 153 us: flow(): pl.pallas_call(flow_kernel, out_shape=(jax.ShapeDtypeStruct((3072, 768),...]
    broadcast_in_dim x4 -> x0, other arithmetic: 17.3 us -> none  [the longest x1 7.21 us: kernel_sums(): down_sum.astype(f32)[None]]
    ppermute x7 -> x0, starting transfers between devices: 12.6 us -> none  [shifted_2(): return lax.ppermute(shard, axis, pairs)]
    reduce_sum x13 -> x0, other arithmetic: 11.9 us -> none  [the longest x3 3.48 us: layer_norm(): return center * lax.rsqrt(spread + norm_eps) * norm_gain + norm_bias]
    concatenate x8 -> x0, local copies, waits for them, and re-layouts: 11.6 us -> none  [the longest x4 6.06 us: kernel_sums(): jnp.concatenate((columns(down[1][0]), columns(up[1][0]), columns(out[1][0...]
    slice x8 -> x0, local copies, waits for them, and re-layouts: 10.1 us -> none  [the longest x1 1.73 us: forward(): packed[..., :model_width].reshape(images, patch_rows, head_count, HEAD_DIM)]
    unnamed x169 -> x20, local copies, waits for them, and re-layouts: 7.21 us -> 15.3 us
  transfers between devices with their start and end apart: 7 -> 0, of which waited for: 1 -> 0; matrix products, arithmetic and copies ran while one was open for 11% -> 0% of each run, Pallas kernels for 0% -> 0%
where the time goes in v2:
time: 186 us; the launch traced here: 185 us
  Pallas kernels  168 us (90%)
  local copies, waits for them, and re-layouts  15.3 us (8%)
  between operations  1.98 us (1%)
    pallas_call x1, Pallas kernels, flow(): pl.pallas_call(flow_kernel, out_shape=(jax.ShapeDtypeStruct((3072, 768),...  153 us
    unnamed x20, local copies, waits for them, and re-layouts  15.3 us
    pallas_call x1, Pallas kernels, finish(): pl.pallas_call(finish_kernel, grid=(steps,), out_shape=[jax.ShapeDtypeStr...  14.9 us

profile of v2, /device:TPU:0, one launch (start us, length us, event | category | flops | bytes accessed | tf_op | source)
XLA Modules:
  0.0 185.2 jit_solution(1646718410363856442)
XLA Ops:
  1.9 1.5 copy.37.latents_ref
  3.4 1.5 copy.39.cot_ref
  4.9 1.7 copy.38.head_w_ref
  6.6 0.0 copy-start.6
  6.6 153.0 %flow.1 = (bf16[3072,768]{1,0:T(8,128)(2,1)}, bf16[768,3072]{1,0:T(8,128)(2,1)}, bf16[768,768]{1,0:T(8,128)(2,1)}, bf16[768,2304]{1,0:T(8,128)(2,1)}, bf16[128,7...) custom-call(s32[16]{0:T(128)} %labels_sm.1, s32[1]{0:T(128)S(6)} %copy.43.perm_sm, ...), custom_call_target="tpu_custom_call" | custom-call | tf_op jit(solution)/shard_map/flow/pallas_call | solution.py:893
  159.6 0.0 copy-done.6
  159.6 0.0 copy-start
  159.6 2.3 %copy-done = bf16[3072,768]{1,0:T(8,128)(2,1)S(1)} copy-done((bf16[3072,768]{1,0:T(8,128)(2,1)S(1)}, bf16[3072,768]{1,0:T(8,128)(2,1)}, u32[]{:S(2)}) %copy-start) | copy-done | bytes 4718616
  161.9 0.0 copy-start.1
  161.9 2.0 %copy-done.1 = bf16[768,2304]{1,0:T(8,128)(2,1)S(1)} copy-done((bf16[768,2304]{1,0:T(8,128)(2,1)S(1)}, bf16[768,2304]{1,0:T(8,128)(2,1)}, u32[]{:S(2)}) %copy-start.1) | copy-done | bytes 3538968
  163.9 0.0 copy-start.2
  163.9 1.3 copy-done.2
  165.2 0.0 copy-start.3
  165.2 1.0 copy-done.3
  166.2 0.0 copy-start.4
  166.2 0.9 copy-done.4
  167.1 0.0 copy-start.5
  167.1 0.9 copy-done.5
  168.0 14.9 %finish.1 = (f32[1,128,48]{2,1,0:T(8,128)S(1)}, f32[1,1]{1,0:T(1,128)}, f32[1,128,48]{2,1,0:T(8,128)S(1)}, f32[48,768]{1,0:T(8,128)}, f32[128,768]{1,0:T(8,128)}...) custom-call(s32[1,16]{1,0:T(1,128)S(1)} %bitcast.4, ...), custom_call_target="tpu_custom_call" | custom-call | tf_op jit(solution)/shard_map/finish/pallas_call | solution.py:1036
  182.9 0.7 copy.40
  183.6 0.7 copy.41
  184.3 0.9 copy.42
Async XLA Ops:
  6.6 153.0 %copy-start.6 = (s32[16]{0:T(128)S(1)}, s32[16]{0:T(128)}, u32[]{:S(2)}) copy-start(s32[16]{0:T(128)} %labels_sm.1) | copy-start | bytes 196
  159.6 2.3 %copy-start = (bf16[3072,768]{1,0:T(8,128)(2,1)S(1)}, bf16[3072,768]{1,0:T(8,128)(2,1)}, u32[]{:S(2)}) copy-start(bf16[3072,768]{1,0:T(8,128)(2,1)} %get-tuple-element.41.down_ref) | copy-start | bytes 14155780
  161.9 2.0 %copy-start.1 = (bf16[768,2304]{1,0:T(8,128)(2,1)S(1)}, bf16[768,2304]{1,0:T(8,128)(2,1)}, u32[]{:S(2)}) copy-start(bf16[768,2304]{1,0:T(8,128)(2,1)} %get-tuple-element.44.qkv_ref) | copy-start | bytes 10616836
  163.9 1.3 copy-start.2
  165.2 1.0 copy-start.3
  166.2 0.9 copy-start.4
  167.1 0.9 copy-start.5

commit v3 on v2

--- a/solution.py
+++ b/solution.py
@@ -64,8 +64,13 @@
 
 
 MESH = pl.DeviceIdType.MESH
-UNITS = 12
-ROWS = 256
+UNITS = 24
+LAST = 25
+TURNS = 13
+SLAB = 128
+TABLE_ROWS = ((0, 384), (384, 384), (768, 256))
+FINISH_ROWS = 768
+AHEAD = 6
 COLS = 384
 STAGES = 3
 CHUNK = 32
@@ -80,13 +85,14 @@
     latents_ref, valid_ref, patch_ref, pos_table_ref, g1_ref, b1_ref, g2_ref, b2_ref,
     up_bias_ref, head_w_ref, head_b_ref, cot_ref,
     class_hbm, qkv_any, out_any, up_any, down_any,
-    down_hbm, up_hbm, out_hbm, qkv_hbm, pos_hbm, small_hbm, latents_hbm,
-    stage, part, full, core_in, ab_in, c_in, send_sem, recv_sem, local_sem,
+    down_hbm, up_hbm, out_hbm, qkv_hbm, pos_hbm, small_hbm, latents_hbm, lines_hbm,
+    stage, part, full, core_in, small_in, ab_in, c_in, send_sem, recv_sem, stage_sem, back_sem, local_sem,
     qkv_w, out_w, up_w, down_w, load_sem,
     lat_pad, cot_pad, patch_pad, head_pad, hidden, mid, xhat1, xhat2, scale1, scale2,
     keys, values, query, attended, bias, prior_mask, mask_row, probs, slope, d_hidden, d_second, d_att, d_keys, d_values,
-    d_prior, d_back, row_out, row_in, grad_out, grad_in, lat_out,
-    lt_ref, r_ref, pos_ref, small_ref, ub_grad, low_top, exch_send, exch_recv, lat_sem,
+    d_prior, d_back, row_out, row_in, grad_out, grad_in, factor, lat_out,
+    lines, line_sum, line_in, line_send, line_recv, line_sem,
+    lt_ref, r_ref, pos_ref, small_ref, low_top, exch_send, exch_recv, lat_sem,
 ):
     dp = lax.axis_index("dp")
     core = lax.axis_index("seq")
@@ -103,15 +109,15 @@
     def rows_at(start, count):
         return pl.ds(pl.multiple_of(start, 16), count)
 
-    sources = [class_hbm.at[r : r + n, h * COLS : (h + 1) * COLS] for h in range(2) for r, n in ((0, 768), (768, 256))]
-    targets = [part.at[2 * h + i, 0:n] for h in range(2) for i, n in ((0, 768), (1, 256))]
+    sources = [class_hbm.at[r : r + n, h * COLS : (h + 1) * COLS] for h in range(2) for r, n in TABLE_ROWS]
+    targets = [part.at[3 * h + i, 0:n] for h in range(2) for i, (r, n) in enumerate(TABLE_ROWS)]
     sources += [qkv_any.at[0], out_any.at[0], up_any.at[0], down_any.at[0]]
     targets += [qkv_w, out_w, up_w, down_w]
 
     def load(i):
         return pltpu.make_async_copy(sources[i], targets[i], load_sem.at[i])
 
-    for i in range(8):
+    for i in range(10):
         load(i).start()
 
     barrier = pltpu.get_barrier_semaphore()
@@ -129,7 +135,7 @@
 
     def copy(u, k, src, dst, target):
         return pltpu.make_async_remote_copy(
-            src_ref=src, dst_ref=dst, send_sem=send_sem.at[u, k], recv_sem=recv_sem.at[u, k],
+            src_ref=src, dst_ref=dst, send_sem=send_sem.at[u], recv_sem=recv_sem.at[k, u % TURNS],
             device_id=target, device_id_type=MESH,
         )
 
@@ -145,24 +151,56 @@
     to_second = (to_y, to_x)
 
     def out_rows(u, t, start, count):
-        return full.at[u, rows_at(t * ROWS + start, count)]
+        return full.at[u, rows_at(t * SLAB + start, count)]
 
     def part_rows(u, t, start, count):
-        return part.at[u, rows_at(t * ROWS + start, count)]
+        return part.at[u, rows_at(t * SLAB + start, count)]
 
     def left_index(u):
-        return jnp.minimum(u, 4) + jnp.minimum(jnp.maximum(u - 7, 0), 2)
+        return jnp.minimum(u // 2, 4) + jnp.minimum(jnp.maximum(u // 2 - 7, 0), 2)
 
     def right_index(u):
-        return jnp.maximum(u - 3, 0)
-
-    small_rows = (slice(128, 256), slice(384, 512))
+        return jnp.maximum(u // 2 - 3, 0)
+
+    def product(u, t, half):
+        rows = pl.ds(pl.multiple_of((u % 2) * 384 + t * SLAB, 128), SLAB)
+        return jnp.dot(lt_ref[left_index(u), rows], r_ref[right_index(u), half], preferred_element_type=f32)
 
     def core_first(u):
-        return copy(u, 0, stage.at[u % STAGES], core_in.at[u], to_core)
-
-    def small_first(t):
-        return copy(UNITS, 25 + t, small_ref.at[1 - core, t], core_in.at[UNITS, small_rows[t]], to_core)
+        return pltpu.make_async_remote_copy(
+            src_ref=stage.at[u % STAGES], dst_ref=core_in.at[u], send_sem=stage_sem.at[u % STAGES],
+            recv_sem=recv_sem.at[0, u % TURNS], device_id=to_core, device_id_type=MESH,
+        )
+
+    def small_first():
+        return pltpu.make_async_remote_copy(
+            src_ref=small_ref.at[1 - core], dst_ref=small_in, send_sem=stage_sem.at[STAGES],
+            recv_sem=recv_sem.at[0, LAST % TURNS], device_id=to_core, device_id_type=MESH,
+        )
+
+    def line_copy(k, src, dst, target):
+        return pltpu.make_async_remote_copy(
+            src_ref=src, dst_ref=dst, send_sem=line_send.at[k], recv_sem=line_recv.at[k],
+            device_id=target, device_id_type=MESH,
+        )
+
+    line_steps = (
+        (lines, line_in.at[0], to_core),
+        (line_sum.at[0], line_in.at[1], to_x),
+        (line_sum.at[1], line_in.at[2], to_y),
+        (line_sum.at[2], line_in.at[3], to_mate),
+        (line_sum.at[3], line_in.at[4], to_inner),
+        (line_sum.at[4], line_sum.at[4], to_mate),
+    )
+
+    def line_go(k):
+        return line_copy(k, *line_steps[k])
+
+    def line_add(k):
+        line_go(k).wait_recv()
+        line_sum[k] = line_steps[k][0][...] + line_in[k]
+
+    line_out = pltpu.make_async_copy(line_sum.at[4], lines_hbm, line_sem)
 
     def produce(u):
         @pl.when(jnp.logical_and(u >= STAGES, u < UNITS))
@@ -171,322 +209,298 @@
 
         @pl.when(u < UNITS)
         def _():
-            right = r_ref[right_index(u), 1 - core]
             for t in range(3):
-                product = jnp.dot(
-                    lt_ref[left_index(u), t * ROWS : (t + 1) * ROWS], right, preferred_element_type=f32
-                )
-                stage[u % STAGES, t * ROWS : (t + 1) * ROWS] = product.astype(bf16)
+                stage[u % STAGES, t * SLAB : (t + 1) * SLAB] = product(u, t, 1 - core).astype(bf16)
             core_first(u).start()
 
-        @pl.when(u == UNITS)
-        def _():
-            for t in range(2):
-                small_first(t).start()
+        @pl.when(u == LAST)
+        def _():
+            small_first().start()
+            line_go(0).start()
 
     def begin(u):
         @pl.when(u < UNITS)
         def _():
             arrived(u, 0, core_in.at[u])
-            right = r_ref[right_index(u), core]
             for t in range(3):
-                rows = slice(t * ROWS, (t + 1) * ROWS)
-                product = jnp.dot(lt_ref[left_index(u), rows], right, preferred_element_type=f32)
-                part[u, rows] = (product + core_in[u, rows].astype(f32)).astype(bf16)
+                rows = slice(t * SLAB, (t + 1) * SLAB)
+                part[u, rows] = (product(u, t, core) + core_in[u, rows].astype(f32)).astype(bf16)
                 if t < 2:
                     ab_first(u, t).start()
-
-            @pl.when(outer)
-            def _():
-                c_z1(u).start()
+            pl.when(outer)(lambda: c_z1(u).start())
 
         @pl.when(u == UNITS)
         def _():
+            part[UNITS, 0:256] = pos_ref[...]
             for t in range(2):
-                arrived(UNITS, 25 + t, core_in.at[UNITS, small_rows[t]])
-                part[UNITS, t * ROWS : t * ROWS + 128] = pos_ref[t]
-                part[UNITS, small_rows[t]] = (
-                    small_ref[core, t].astype(f32) + core_in[UNITS, small_rows[t]].astype(f32)
-                ).astype(bf16)
                 ab_first(u, t).start()
 
+        @pl.when(u == LAST)
+        def _():
+            small_first().wait_recv()
+            part[LAST, 0:256] = (small_ref[core].astype(f32) + small_in[...].astype(f32)).astype(bf16)
+            for t in range(2):
+                ab_first(u, t).start()
+            line_add(0)
+            line_go(1).start()
+
+    def ab_base(t):
+        return first[t] * 64 + second[t] * 32
+
     def ab_first(u, t):
-        return copy(u, 1 + t, part_rows(u, t, (1 - first[t]) * 128, 128), ab_in.at[u, t, 0:128], to_first[t])
+        return copy(u, 1, part_rows(u, t, (1 - first[t]) * 64, 64), ab_in.at[u, t, 0:64], to_first[t])
 
     def ab_second(u, t):
-        row = first[t] * 128 + (1 - second[t]) * 64
-        return copy(u, 3 + t, part_rows(u, t, row, 64), ab_in.at[u, t, 128:192], to_second[t])
-
-    def ab_base(t):
-        return first[t] * 128 + second[t] * 64
+        row = first[t] * 64 + (1 - second[t]) * 32
+        return copy(u, 2, part_rows(u, t, row, 32), ab_in.at[u, t, 64:96], to_second[t])
 
     def ab_z1(u, t):
-        return copy(u, 5 + t, part_rows(u, t, ab_base(t), 64), ab_in.at[u, t, 192:256], to_mate)
+        return copy(u, 3, part_rows(u, t, ab_base(t), 32), ab_in.at[u, t, 96:128], to_mate)
 
     def ab_z2(u, t):
-        return copy(
-            u, 7 + t, part_rows(u, t, ab_base(t) + (2 - z) * 32, 32), ab_in.at[u, t, 256:288], to_inner
-        )
-
-    def ab_z3(u, t, row):
-        block = out_rows(u, t, row, 32)
-        return copy(u, 9 + t, block, block, to_inner)
-
-    def ab_z4(u, t):
-        block = out_rows(u, t, ab_base(t), 64)
-        return copy(u, 11 + t, block, block, to_mate)
-
-    def ab_back2(u, t, row):
-        block = out_rows(u, t, row, 64)
-        return copy(u, 13 + t, block, block, to_second[t])
-
-    def ab_back1(u, t, row):
-        block = out_rows(u, t, row, 128)
-        return copy(u, 15 + t, block, block, to_first[t])
+        return copy(u, 4, part_rows(u, t, ab_base(t), 32), ab_in.at[u, t, 128:160], to_inner)
+
+    def ab_z3(u, t):
+        block = out_rows(u, t, ab_base(t), 32)
+        return copy(u, 3, block, block, to_mate)
+
+    def ab_back2(u, t):
+        block = out_rows(u, t, ab_base(t), 32)
+        return copy(u, 5, block, block, to_second[t])
+
+    def ab_back1(u, t):
+        block = out_rows(u, t, first[t] * 64, 64)
+        return copy(u, 6, block, block, to_first[t])
 
     def ab1(u):
+        arrived(u, 1, ab_in.at[u, :, 0:64])
         for t in range(2):
-            arrived(u, 1 + t, ab_in.at[u, t, 0:128])
-            kept = part_rows(u, t, first[t] * 128, 128)
-            added(kept, kept, ab_in.at[u, t, 0:128])
+            kept = part_rows(u, t, first[t] * 64, 64)
+            added(kept, kept, ab_in.at[u, t, 0:64])
             ab_second(u, t).start()
 
+        @pl.when(u == LAST)
+        def _():
+            line_add(1)
+            line_go(2).start()
+
     def ab2(u):
+        arrived(u, 2, ab_in.at[u, :, 64:96])
         for t in range(2):
-            arrived(u, 3 + t, ab_in.at[u, t, 128:192])
-            kept = part_rows(u, t, ab_base(t), 64)
-            added(kept, kept, ab_in.at[u, t, 128:192])
-
-        @pl.when(outer)
-        def _():
-            for t in range(2):
-                ab_z1(u, t).start()
+            kept = part_rows(u, t, ab_base(t), 32)
+            added(kept, kept, ab_in.at[u, t, 64:96])
+            pl.when(outer)(lambda: ab_z1(u, t).start())
+
+        @pl.when(u == LAST)
+        def _():
+            line_add(2)
+            pl.when(outer)(line_go(3).start)
 
     def ab3_inner(u):
+        arrived(u, 3, ab_in.at[u, :, 96:128])
         for t in range(2):
-            arrived(u, 5 + t, ab_in.at[u, t, 192:256])
-            kept = part_rows(u, t, ab_base(t), 64)
-            added(kept, kept, ab_in.at[u, t, 192:256])
+            kept = part_rows(u, t, ab_base(t), 32)
+            added(kept, kept, ab_in.at[u, t, 96:128])
             ab_z2(u, t).start()
 
+        @pl.when(u == LAST)
+        def _():
+            line_add(3)
+            line_go(4).start()
+
     def ab4_inner(u):
+        arrived(u, 4, ab_in.at[u, :, 128:160])
         for t in range(2):
-            arrived(u, 7 + t, ab_in.at[u, t, 256:288])
-            row = ab_base(t) + (z - 1) * 32
-            added(out_rows(u, t, row, 32), part_rows(u, t, row, 32), ab_in.at[u, t, 256:288])
-            ab_z3(u, t, row).start()
-
-    def ab5_inner(u):
+            added(out_rows(u, t, ab_base(t), 32), part_rows(u, t, ab_base(t), 32), ab_in.at[u, t, 128:160])
+            ab_z3(u, t).start()
+            ab_back2(u, t).start()
+
+        @pl.when(u == LAST)
+        def _():
+            line_add(4)
+            line_go(5).start()
+            line_out.start()
+
+    def ab5_outer(u):
+        arrived(u, 3, full.at[u, 0:64])
         for t in range(2):
-            arrived(u, 9 + t, out_rows(u, t, ab_base(t) + (2 - z) * 32, 32))
-            ab_z4(u, t).start()
-            ab_back2(u, t, ab_base(t)).start()
-
-    def ab5_outer(u):
+            ab_back2(u, t).start()
+
+        @pl.when(u == LAST)
+        def _():
+            line_go(5).wait_recv()
+            line_out.start()
+
+    def ab6(u):
+        arrived(u, 5, full.at[u, 0:64])
         for t in range(2):
-            arrived(u, 11 + t, out_rows(u, t, ab_base(t), 64))
-            ab_back2(u, t, ab_base(t)).start()
-
-    def ab6(u):
-        for t in range(2):
-            arrived(u, 13 + t, out_rows(u, t, first[t] * 128 + (1 - second[t]) * 64, 64))
-            ab_back1(u, t, first[t] * 128).start()
+            ab_back1(u, t).start()
 
     def place(u, h, row, count, act):
         def columns(base):
             return pl.ds(pl.multiple_of(base + h * COLS, 128), COLS)
 
-        @pl.when(u < 4)
-        def _():
-            act(down_hbm.at[pl.ds(pl.multiple_of(u * 768 + row, 16), count), columns(0)])
-
-        @pl.when(jnp.logical_and(u >= 4, u < 8))
-        def _():
-            act(up_hbm.at[row : row + count, columns((u - 4) * 768)])
-
-        @pl.when(u == 8)
-        def _():
-            act(out_hbm.at[row : row + count, columns(0)])
-
-        @pl.when(jnp.logical_and(u >= 9, u < UNITS))
-        def _():
-            act(qkv_hbm.at[row : row + count, columns((u - 9) * 768)])
-
-    def to_other(u, k, row, count):
-        return lambda dst: copy(u, k, full.at[u, row : row + count], dst, to_core)
-
-    def to_own(u, k, row, count):
-        return lambda dst: pltpu.make_async_copy(full.at[u, row : row + count], dst, local_sem.at[u, k])
-
-    def spread_ab(u):
-        place(u, core, 0, 512, lambda dst: to_other(u, 27, 0, 512)(dst).start())
-        place(u, core, 0, 512, lambda dst: to_own(u, 0, 0, 512)(dst).start())
-
-    def spread_c(u):
-        place(u, core, 512, 256, lambda dst: to_other(u, 28, 512, 256)(dst).start())
-        place(u, core, 512, 256, lambda dst: to_own(u, 1, 512, 256)(dst).start())
+        block, top = u // 2, (u % 2) * 384 + row
+
+        @pl.when(block < 4)
+        def _():
+            act(down_hbm.at[rows_at(block * 768 + top, count), columns(0)])
+
+        @pl.when(jnp.logical_and(block >= 4, block < 8))
+        def _():
+            act(up_hbm.at[rows_at(top, count), columns((block - 4) * 768)])
+
+        @pl.when(block == 8)
+        def _():
+            act(out_hbm.at[rows_at(top, count), columns(0)])
+
+        @pl.when(jnp.logical_and(block >= 9, block < 12))
+        def _():
+            act(qkv_hbm.at[rows_at(top, count), columns((block - 9) * 768)])
+
+    def to_other(u, src, dst):
+        return pltpu.make_async_remote_copy(
+            src_ref=src, dst_ref=dst, send_sem=send_sem.at[u], recv_sem=back_sem.at[u],
+            device_id=to_core, device_id_type=MESH,
+        )
+
+    def to_own(u, src, dst):
+        return pltpu.make_async_copy(src, dst, local_sem.at[u])
+
+    def both_ways(u, src, dst):
+        to_other(u, src, dst).start()
+        to_own(u, src, dst).start()
+
+    def spread(u, row, count):
+        place(u, core, row, count, lambda dst: both_ways(u, full.at[u, row : row + count], dst))
 
     def small_out(h, t):
         return small_hbm.at[pl.ds(pl.multiple_of(h * 128, 128), 128), t * COLS : (t + 1) * COLS]
 
-    def small_other(t):
-        return copy(UNITS, 27 + t, full.at[UNITS, small_rows[t]], small_out(core, t), to_core)
-
-    def small_own(t):
-        return pltpu.make_async_copy(
-            full.at[UNITS, small_rows[t]], small_out(core, t), local_sem.at[UNITS, t]
-        )
-
-    def pos_own(t):
-        return pltpu.make_async_copy(
-            full.at[UNITS, t * ROWS : t * ROWS + 128],
-            pos_hbm.at[:, t * COLS : (t + 1) * COLS],
-            local_sem.at[UNITS, 2 + t],
-        )
-
     def ab7(u):
-        for t in range(2):
-            arrived(u, 15 + t, out_rows(u, t, (1 - first[t]) * 128, 128))
-        spread_ab(u)
+        arrived(u, 6, full.at[u, 0:128])
+        spread(u, 0, 2 * SLAB)
 
         @pl.when(u == UNITS)
         def _():
             for t in range(2):
-                small_other(t).start()
-                small_own(t).start()
-                pos_own(t).start()
-
-    far = 64 * (1 - side)
-    own_end = 192 * side
-    shard = z * 64
-    half = shard + x * 32
-    mine = half + y * 16
+                to_own(
+                    UNITS, full.at[UNITS, t * 128 : (t + 1) * 128], pos_hbm.at[:, t * COLS : (t + 1) * COLS]
+                ).start()
+
+        @pl.when(u == LAST)
+        def _():
+            for t in range(2):
+                both_ways(LAST, full.at[LAST, t * 128 : (t + 1) * 128], small_out(core, t))
+
+    far = 32 * (1 - side)
+    own_end = 96 * side
+    shard = z * 32
+    half = shard + x * 16
 
     def c_z1(u):
-        return copy(u, 17, part_rows(u, 2, far, 192), c_in.at[u, 0:192], to_mate)
+        return copy(u, 7, part_rows(u, 2, far, 96), c_in.at[u, 0:96], to_mate)
 
     def c_z2(u):
-        return copy(u, 18, part_rows(u, 2, (1 - side) * 128, 128), c_in.at[u, 192:320], to_inner)
+        return copy(u, 8, part_rows(u, 2, (1 - side) * 64, 64), c_in.at[u, 96:160], to_inner)
 
     def c_z3(u):
-        return copy(u, 19, part_rows(u, 2, own_end, 64), c_in.at[u, 320:384], to_mate)
+        return copy(u, 7, part_rows(u, 2, own_end, 32), c_in.at[u, 160:192], to_mate)
 
     def c_x(u):
-        return copy(u, 20, part_rows(u, 2, shard + (1 - x) * 32, 32), c_in.at[u, 384:416], to_x)
+        return copy(u, 9, part_rows(u, 2, shard + (1 - x) * 16, 16), c_in.at[u, 192:208], to_x)
 
     def c_y(u):
-        return copy(u, 21, part_rows(u, 2, half + (1 - y) * 16, 16), c_in.at[u, 416:432], to_y)
-
-    def c_back_y(u, row):
-        block = out_rows(u, 2, row, 16)
-        return copy(u, 22, block, block, to_y)
-
-    def c_back_x(u, row):
-        block = out_rows(u, 2, row, 32)
-        return copy(u, 23, block, block, to_x)
+        return copy(u, 10, part_rows(u, 2, half, 16), c_in.at[u, 208:224], to_y)
+
+    def c_back_x(u):
+        block = out_rows(u, 2, half, 16)
+        return copy(u, 11, block, block, to_x)
 
     def c_z4(u):
-        block = out_rows(u, 2, own_end, 64)
-        return copy(u, 24, block, block, to_mate)
-
-    def c_z5(u, row):
-        block = out_rows(u, 2, row, 128)
-        return copy(u, 25, block, block, to_inner)
+        block = out_rows(u, 2, own_end, 32)
+        return copy(u, 12, block, block, to_mate)
+
+    def c_z5(u):
+        block = out_rows(u, 2, side * 64, 64)
+        return copy(u, 13, block, block, to_inner)
 
     def c_z6(u):
-        block = out_rows(u, 2, far, 192)
-        return copy(u, 26, block, block, to_mate)
+        block = out_rows(u, 2, far, 96)
+        return copy(u, 12, block, block, to_mate)
 
     def c1_inner(u):
-        arrived(u, 17, c_in.at[u, 0:192])
-        kept = part_rows(u, 2, far, 192)
-        added(kept, kept, c_in.at[u, 0:192])
+        arrived(u, 7, c_in.at[u, 0:96])
+        kept = part_rows(u, 2, far, 96)
+        added(kept, kept, c_in.at[u, 0:96])
         c_z2(u).start()
 
     def c2_inner(u):
-        arrived(u, 18, c_in.at[u, 192:320])
-        kept = part_rows(u, 2, side * 128, 128)
-        added(kept, kept, c_in.at[u, 192:320])
+        arrived(u, 8, c_in.at[u, 96:160])
+        kept = part_rows(u, 2, side * 64, 64)
+        added(kept, kept, c_in.at[u, 96:160])
         c_z3(u).start()
         c_x(u).start()
 
     def c3_outer(u):
-        arrived(u, 19, c_in.at[u, 320:384])
-        kept = part_rows(u, 2, shard, 64)
-        added(kept, kept, c_in.at[u, 320:384])
+        arrived(u, 7, c_in.at[u, 160:192])
+        kept = part_rows(u, 2, shard, 32)
+        added(kept, kept, c_in.at[u, 160:192])
         c_x(u).start()
 
     def c4(u):
-        arrived(u, 20, c_in.at[u, 384:416])
-        kept = part_rows(u, 2, half, 32)
-        added(kept, kept, c_in.at[u, 384:416])
+        arrived(u, 9, c_in.at[u, 192:208])
+        kept = part_rows(u, 2, half, 16)
+        added(kept, kept, c_in.at[u, 192:208])
         c_y(u).start()
 
     def c5(u):
-        arrived(u, 21, c_in.at[u, 416:432])
-        added(out_rows(u, 2, mine, 16), part_rows(u, 2, mine, 16), c_in.at[u, 416:432])
-        c_back_y(u, mine).start()
-
-    def c6(u):
-        arrived(u, 22, out_rows(u, 2, half + (1 - y) * 16, 16))
-        c_back_x(u, half).start()
+        arrived(u, 10, c_in.at[u, 208:224])
+        added(out_rows(u, 2, half, 16), part_rows(u, 2, half, 16), c_in.at[u, 208:224])
+        c_back_x(u).start()
 
     def c7(u):
-        arrived(u, 23, out_rows(u, 2, shard + (1 - x) * 32, 32))
-
-    def c7_outer(u):
-        c7(u)
-        c_z4(u).start()
+        arrived(u, 11, out_rows(u, 2, shard + (1 - x) * 16, 16))
+        pl.when(outer)(lambda: c_z4(u).start())
 
     def c8_inner(u):
-        arrived(u, 24, out_rows(u, 2, own_end, 64))
-        c_z5(u, side * 128).start()
+        arrived(u, 12, out_rows(u, 2, own_end, 32))
+        c_z5(u).start()
 
     def c9_inner(u):
-        arrived(u, 25, out_rows(u, 2, (1 - side) * 128, 128))
+        arrived(u, 13, out_rows(u, 2, (1 - side) * 64, 64))
         c_z6(u).start()
-        spread_c(u)
+        spread(u, 2 * SLAB, SLAB)
 
     def c10_outer(u):
-        arrived(u, 26, out_rows(u, 2, far, 192))
-        spread_c(u)
+        arrived(u, 12, out_rows(u, 2, far, 96))
+        spread(u, 2 * SLAB, SLAB)
 
     everyone, inners, outers = None, inner, outer
     events = [
-        (0, UNITS + 1, everyone, produce),
-        (1, UNITS + 1, everyone, begin),
-        (2, UNITS + 1, everyone, ab1),
+        (1, LAST + 1, everyone, begin),
+        (2, LAST + 1, everyone, ab1),
+        (3, LAST + 1, everyone, ab2),
         (2, UNITS, inners, c1_inner),
         (3, UNITS, inners, c2_inner),
-        (3, UNITS + 1, everyone, ab2),
         (4, UNITS, outers, c3_outer),
-        (4, UNITS + 1, inners, ab3_inner),
+        (4, LAST + 1, inners, ab3_inner),
+        (5, LAST + 1, inners, ab4_inner),
+        (6, LAST + 1, outers, ab5_outer),
         (4, UNITS, inners, c4),
         (5, UNITS, outers, c4),
-        (5, UNITS + 1, inners, ab4_inner),
         (5, UNITS, inners, c5),
         (6, UNITS, outers, c5),
-        (6, UNITS + 1, inners, ab5_inner),
-        (6, UNITS, inners, c6),
-        (7, UNITS, outers, c6),
-        (7, UNITS + 1, outers, ab5_outer),
-        (7, UNITS, inners, c7),
-        (8, UNITS, outers, c7_outer),
-        (8, UNITS + 1, everyone, ab6),
-        (9, UNITS, inners, c8_inner),
-        (9, UNITS + 1, everyone, ab7),
-        (10, UNITS, inners, c9_inner),
-        (11, UNITS, outers, c10_outer),
+        (6, UNITS, inners, c7),
+        (7, UNITS, outers, c7),
+        (6, LAST + 1, inners, ab6),
+        (7, LAST + 1, outers, ab6),
+        (7, LAST + 1, inners, ab7),
+        (8, LAST + 1, outers, ab7),
+        (8, UNITS, inners, c8_inner),
+        (9, UNITS, inners, c9_inner),
+        (10, UNITS, outers, c10_outer),
     ]
-
-    def step(t, carried):
-        for lag, count, who, event in events:
-            u = t - lag
-            now = jnp.logical_and(u >= 0, u < count)
-            if who is not None:
-                now = jnp.logical_and(now, who)
-            pl.when(now)(lambda event=event, u=u: event(u))
-        return carried
 
     mm_nt = (((1,), (1,)), ((), ()))
     mm_tn = (((0,), (0,)), ((), ()))
@@ -515,13 +529,15 @@
     valid_col = jnp.sum(jnp.where(eye, valid_row, 0.0), axis=1, keepdims=True)
     mask_row[...] = jnp.broadcast_to(valid_row, (8, 128))
     lat_pad[...] = jnp.zeros((128, 128), f32)
-    lat_pad[:, 0:48] = latents_ref[0]
+    lat_pad[0:48] = latents_ref[0]
+    lat_pad[...] = lat_pad[...].T
     cot_pad[...] = jnp.zeros((128, 128), f32)
-    cot_pad[:, 0:48] = cot_ref[0]
+    cot_pad[0:48] = cot_ref[0]
+    cot_pad[...] = cot_pad[...].T
     patch_pad[...] = jnp.zeros((128, 768), bf16)
     patch_pad[0:48] = patch_ref[...]
-    head_pad[...] = jnp.zeros((768, 128), bf16)
-    head_pad[:, 0:96] = head_w_ref[...]
+    head_pad[...] = jnp.zeros((128, 768), bf16)
+    head_pad[0:96] = head_w_ref[...]
     head_bias = jnp.concatenate((head_b_ref[...].astype(f32), jnp.zeros((1, 32), f32)), 1)
 
     @pl.when(core == 0)
@@ -552,10 +568,14 @@
 
     label = labels_sm[perm_sm[0]]
     hot = jnp.where(lax.broadcasted_iota(jnp.int32, (16, 1024), 1) == label, 1.0, 0.0).astype(bf16)
-    for i in range(4):
+    for i in range(6):
         load(i).wait()
     class_row = jnp.concatenate(
-        [nn(hot[:, 0:768], part[2 * h]) + nn(hot[:, 768:1024], part[2 * h + 1, 0:256]) for h in range(2)], 1
+        [
+            sum(nn(hot[:, r : r + n], part[3 * h + i, 0:n]) for i, (r, n) in enumerate(TABLE_ROWS))
+            for h in range(2)
+        ],
+        1,
     )[0:1]
     hidden[...] = (
         nn(lat_pad[...].astype(bf16), patch_pad[...]) + pos_table_ref[...].astype(f32) + class_row
@@ -565,7 +585,7 @@
         low_top[r] = v.astype(bf16)
 
     normalize(hidden, xhat1, scale1, g1_ref[...].astype(f32), b1_ref[...].astype(f32), put_low)
-    load(4).wait()
+    load(6).wait()
     normed = low_top[...]
     keys[128:256] = nn(normed, qkv_w[:, 768:1536]).astype(bf16)
 
@@ -612,13 +632,13 @@
         return carried
 
     lax.fori_loop(0, 6, attend, 0)
-    load(5).wait()
+    load(7).wait()
     mid[...] = hidden[...] + nn(attended[...], out_w[...])
     lt_ref[5] = attended[...].astype(f32).T.astype(bf16)
     normalize(mid, xhat2, scale2, g2_ref[...].astype(f32), b2_ref[...].astype(f32), put_low)
     lt_ref[4] = low_top[...].astype(f32).T.astype(bf16)
-    load(6).wait()
-    load(7).wait()
+    load(8).wait()
+    load(9).wait()
     d_hidden[...] = mid[...]
 
     def rows768(j):
@@ -641,7 +661,7 @@
 
     lax.fori_loop(0, 4, feed, 0)
     low_top[...] = d_hidden[...].astype(bf16)
-    row_out[...] = nn(low_top[...], head_pad[...]) + head_bias
+    row_out[...] = nt(low_top[...], head_pad[...]) + head_bias
 
     @pl.when(core == 0)
     def _():
@@ -657,13 +677,12 @@
     inside = lane < 48
     alpha = jnp.where(inside, shifted, 0.0)
     shift_mean = jnp.where(inside, pltpu.roll(shifted, 80, 1), 0.0)
-    factor = jnp.exp(-alpha)
-    new_latents = (lat_pad[...] - shift_mean) * factor
-    lat_out[0] = new_latents
+    factor[...] = jnp.exp(-alpha)
+    new_latents = (lat_pad[...] - shift_mean) * factor[...]
+    lat_out[0] = new_latents.T
     logdet = -jnp.sum(jnp.sum(alpha, 1, keepdims=True), 0, keepdims=True)
     d_alpha = -cot_pad[...] * new_latents - cot_logdet_sm[0]
-    direct = cot_pad[...] * factor
-    lat_out[1] = direct
+    direct = cot_pad[...] * factor[...]
     grad_out[...] = (
         jnp.where(inside, d_alpha, pltpu.roll(jnp.where(inside, -direct, 0.0), 48, 1)) * valid_col
     )
@@ -681,7 +700,7 @@
     d_head = jnp.where(row == 127, jnp.broadcast_to(grad_in[0:1], (128, 128)), rolled_back).astype(bf16)
     head_grad = tn(d_head, low_top[...])
     head_bias_grad = jnp.sum(d_head.astype(f32), 0, keepdims=True)
-    d_hidden[...] = nt(d_head, head_pad[...])
+    d_hidden[...] = nn(d_head, head_pad[...])
     low_top[...] = d_hidden[...].astype(bf16)
     for h in range(2):
         r_ref[0, h] = low_top[:, h * COLS : (h + 1) * COLS]
@@ -689,13 +708,18 @@
     def put(first_row, value):
         h, r = first_row // 128, first_row % 128
         for t in range(2):
-            small_ref[h, t, r : r + value.shape[0]] = value[:, t * COLS : (t + 1) * COLS].astype(bf16)
+            small_ref[h, t * 128 + r : t * 128 + r + value.shape[0]] = value[:, t * COLS : (t + 1) * COLS].astype(bf16)
 
     put(0, head_grad[0:96])
 
+    lines[...] = jnp.zeros((16, 768), f32)
+    lane1 = lax.broadcasted_iota(jnp.int32, (1, 128), 1)
+    lines[8:9, 0:128] = head_bias_grad
+    lines[8:9, 128:256] = jnp.where(lane1 == dp, logdet, 0.0)
+
     d_second[...] = jnp.zeros((128, 768), f32)
 
-    def feed_back(j, carried):
+    def feed_back(j):
         d_keys[...] = nt(low_top[...], down_w[rows768(j)])
         total = jnp.zeros((1, 768), f32)
         for r in chunks:
@@ -704,13 +728,10 @@
             total += jnp.sum(d_pre.astype(f32), 0, keepdims=True)
             for h in range(2):
                 r_ref[1 + j, h, r] = d_pre[:, h * COLS : (h + 1) * COLS]
-        ub_grad[pl.ds(j, 1)] = total
+        lines[pl.ds(4 + j, 1)] = total
         d_second[...] += nt(d_att[...], up_w[:, rows768(j)])
-        return carried
-
-    lax.fori_loop(0, 4, feed_back, 0)
-
-    def norm_back(grad, hat, scale, gain, base, out):
+
+    def norm_back(grad, hat, scale, gain, base, out, line):
         gain_total = jnp.zeros((1, 768), f32)
         shift_total = jnp.zeros((1, 768), f32)
         for r in chunks:
@@ -721,15 +742,17 @@
             out[r] = base[r] + scale[r] * v
             gain_total += jnp.sum(d * scaled, 0, keepdims=True)
             shift_total += jnp.sum(d, 0, keepdims=True)
-        return gain_total, shift_total
-
-    g2_grad, b2_grad = norm_back(d_second, xhat2, scale2, g2_ref[...].astype(f32), d_hidden, mid)
-    low_top[...] = mid[...].astype(bf16)
-    for h in range(2):
-        r_ref[5, h] = low_top[:, h * COLS : (h + 1) * COLS]
-    d_att[...] = nt(low_top[...], out_w[...]).astype(bf16)
-
-    def attend_back(p, carried):
+        lines[line : line + 1] = gain_total
+        lines[line + 1 : line + 2] = shift_total
+
+    def feed_norm_back():
+        norm_back(d_second, xhat2, scale2, g2_ref[...].astype(f32), d_hidden, mid, 2)
+        low_top[...] = mid[...].astype(bf16)
+        for h in range(2):
+            r_ref[5, h] = low_top[:, h * COLS : (h + 1) * COLS]
+        d_att[...] = nt(low_top[...], out_w[...]).astype(bf16)
+
+    def attend_back(p):
         cols = columns128(p)
         q_pair = query[:, cols]
         k_pair = keys[:, cols]
@@ -756,117 +779,110 @@
         d_prior[1, :, cols] = dv_pair[0:128].astype(bf16)
         d_keys[:, cols] = dk_pair[128:256]
         d_values[:, cols] = dv_pair[128:256]
+
+    def send_prior():
+        @pl.when(core == 1)
+        def _():
+            exchange(5, d_prior, d_back).start()
+
+    def packed_back():
+        @pl.when(core == 0)
+        def _():
+            exchange(5, d_prior, d_back).wait_recv()
+
+        for h in range(2):
+            cols = slice(h * COLS, (h + 1) * COLS)
+            r_ref[7, h] = (d_keys[:, cols] + d_back[0, :, cols].astype(f32)).astype(bf16)
+            r_ref[8, h] = (d_values[:, cols] + d_back[1, :, cols].astype(f32)).astype(bf16)
+        d_second[...] = sum(
+            nt(r_ref[6 + j, h], qkv_w[:, j * 768 + h * COLS : j * 768 + (h + 1) * COLS])
+            for j in range(3)
+            for h in range(2)
+        )
+
+    lat_copy = pltpu.make_async_copy(lat_out, latents_hbm, lat_sem)
+
+    def embed_back():
+        norm_back(d_second, xhat1, scale1, g1_ref[...].astype(f32), mid, d_hidden, 0)
+        low_top[...] = d_hidden[...].astype(bf16)
+        for t in range(2):
+            pos_ref[t * 128 : (t + 1) * 128] = low_top[:, t * COLS : (t + 1) * COLS]
+        patch_grad = tn(lat_pad[...].astype(bf16), low_top[...])
+        lat_out[1] = (cot_pad[...] * factor[...] + nt(low_top[...], patch_pad[...])).T
+        lat_copy.start()
+        class_grad = jnp.sum(d_hidden[...], 0, keepdims=True)
+        put(96, patch_grad[0:32])
+        put(128, patch_grad[32:48])
+        line = lax.broadcasted_iota(jnp.int32, (16, 768), 0)
+        put(144, jnp.where(line == dp, class_grad, 0.0))
+        put(160, jnp.zeros((96, 768), f32))
+
+    def both(t):
+        produce_now(t)
+
+        @pl.when(jnp.logical_and(t < 8, t % 2 == 0))
+        def _():
+            feed_back(t // 2)
+
+        pl.when(t == 8)(feed_norm_back)
+
+        @pl.when(jnp.logical_and(t >= 9, t < 15))
+        def _():
+            attend_back(t - 9)
+
+        pl.when(t == 14)(send_prior)
+        pl.when(t == 16)(packed_back)
+        pl.when(t == 18)(embed_back)
+
+    def produce_now(t):
+        pl.when(t <= LAST)(lambda: produce(t))
+
+    def step(t, carried):
+        both(t)
+        for lag, count, who, event in events:
+            u = t - lag
+            now = jnp.logical_and(u >= 0, u < count)
+            if who is not None:
+                now = jnp.logical_and(now, who)
+            pl.when(now)(lambda event=event, u=u: event(u))
         return carried
 
-    lax.fori_loop(0, 6, attend_back, 0)
-
-    @pl.when(core == 1)
-    def _():
-        exchange(5, d_prior, d_back).start()
-
-    @pl.when(core == 0)
-    def _():
-        exchange(5, d_prior, d_back).wait_recv()
-
-    for h in range(2):
-        cols = slice(h * COLS, (h + 1) * COLS)
-        r_ref[7, h] = (d_keys[:, cols] + d_back[0, :, cols].astype(f32)).astype(bf16)
-        r_ref[8, h] = (d_values[:, cols] + d_back[1, :, cols].astype(f32)).astype(bf16)
-    d_second[...] = sum(
-        nt(r_ref[6 + j, h], qkv_w[:, j * 768 + h * COLS : j * 768 + (h + 1) * COLS])
-        for j in range(3)
-        for h in range(2)
-    )
-    g1_grad, b1_grad = norm_back(d_second, xhat1, scale1, g1_ref[...].astype(f32), mid, d_hidden)
-    low_top[...] = d_hidden[...].astype(bf16)
-    for t in range(2):
-        pos_ref[t] = low_top[:, t * COLS : (t + 1) * COLS]
-    patch_grad = tn(lat_pad[...].astype(bf16), low_top[...])
-    lat_out[1] += nt(low_top[...], patch_pad[...])
-    lat_copy = pltpu.make_async_copy(lat_out, latents_hbm, lat_sem)
-    lat_copy.start()
-    class_grad = jnp.sum(d_hidden[...], 0, keepdims=True)
-    put(96, patch_grad[0:32])
-    put(128, patch_grad[32:48])
-    line = lax.broadcasted_iota(jnp.int32, (16, 768), 0)
-    put(144, jnp.where(line == dp, class_grad, 0.0))
-    lane1 = lax.broadcasted_iota(jnp.int32, (1, 128), 1)
-    high = logdet.astype(bf16).astype(f32)
-    slot = lane1 == core * 16 + dp
-    misc = jnp.concatenate(
-        (
-            head_bias_grad,
-            jnp.where(slot, high, 0.0),
-            jnp.where(slot, logdet - high, 0.0),
-            jnp.zeros((1, 384), f32),
-        ),
-        1,
-    )
-    lines = [g1_grad, b1_grad, g2_grad, b2_grad] + [ub_grad[j : j + 1] for j in range(4)] + [misc]
-    block = jnp.zeros((16, 768), f32)
-    for i, one in enumerate(lines):
-        block = jnp.where(line == i, one, block)
-    put(160, block)
-    put(176, jnp.zeros((80, 768), f32))
-    lax.fori_loop(0, UNITS + 11, step, 0)
-
+    lax.fori_loop(0, LAST + 9, step, 0)
+
+    def sent(u, units, rows):
+        ref = full.at[0:units, 0:rows]
+        copy(u, 0, ref, ref, to_core).wait_send()
 
     def drain(u, carried):
-        @pl.when(u < UNITS)
-        def _():
-            place(u, core, 0, 512, lambda dst: to_other(u, 27, 0, 512)(dst).wait_send())
-            place(u, core, 0, 512, lambda dst: to_own(u, 0, 0, 512)(dst).wait())
-            place(u, 1 - core, 0, 512, lambda dst: to_other(u, 27, 0, 512)(dst).wait_recv())
-            place(u, core, 512, 256, lambda dst: to_other(u, 28, 512, 256)(dst).wait_send())
-            place(u, core, 512, 256, lambda dst: to_own(u, 1, 512, 256)(dst).wait())
-            place(u, 1 - core, 512, 256, lambda dst: to_other(u, 28, 512, 256)(dst).wait_recv())
-            c_x(u).wait_send()
-            c_y(u).wait_send()
-            c_back_y(u, mine).wait_send()
-            c_back_x(u, half).wait_send()
-
-            @pl.when(outer)
-            def _():
-                c_z1(u).wait_send()
-                c_z4(u).wait_send()
-
-            @pl.when(inner)
-            def _():
-                c_z2(u).wait_send()
-                c_z3(u).wait_send()
-                c_z5(u, side * 128).wait_send()
-                c_z6(u).wait_send()
-
-        for t in range(2):
-            ab_first(u, t).wait_send()
-            ab_second(u, t).wait_send()
-            ab_back2(u, t, ab_base(t)).wait_send()
-            ab_back1(u, t, first[t] * 128).wait_send()
-
-        @pl.when(outer)
-        def _():
-            for t in range(2):
-                ab_z1(u, t).wait_send()
-
-        @pl.when(inner)
-        def _():
-            for t in range(2):
-                ab_z2(u, t).wait_send()
-                ab_z3(u, t, ab_base(t) + (z - 1) * 32).wait_send()
-                ab_z4(u, t).wait_send()
-
+        pl.when(outer)(lambda: sent(u, 3, 336))
+        pl.when(inner)(lambda: sent(u, 5, 240))
+        place(u, core, 0, 3 * SLAB, lambda dst: to_own(u, full.at[u], dst).wait())
+        place(u, 1 - core, 0, 3 * SLAB, lambda dst: to_other(u, full.at[u], dst).wait_recv())
         return carried
 
-    lax.fori_loop(0, UNITS + 1, drain, 0)
+    lax.fori_loop(0, UNITS, drain, 0)
+    pl.when(outer)(lambda: sent(UNITS, 2, 224))
+    pl.when(inner)(lambda: sent(UNITS, 2, 256))
+    to_own(UNITS, pos_hbm, pos_hbm).wait()
+    pl.when(outer)(lambda: sent(LAST, 2, 352))
+    pl.when(inner)(lambda: sent(LAST, 2, 384))
+    own_small = small_hbm.at[pl.ds(pl.multiple_of(core * 128, 128), 128)]
+    other_small = small_hbm.at[pl.ds(pl.multiple_of((1 - core) * 128, 128), 128)]
+    to_own(LAST, own_small, own_small).wait()
+    to_other(LAST, other_small, other_small).wait_recv()
     for u in range(UNITS - STAGES, UNITS):
         core_first(u).wait_send()
-    for t in range(2):
-        small_first(t).wait_send()
-        small_other(t).wait_send()
-        arrived(UNITS, 27 + t, small_out(1 - core, t))
-        small_own(t).wait()
-        pos_own(t).wait()
+    small_first().wait_send()
     lat_copy.wait()
+    line_out.wait()
+    for k in range(3):
+        line_go(k).wait_send()
+    pl.when(outer)(line_go(3).wait_send)
+
+    @pl.when(inner)
+    def _():
+        line_go(4).wait_send()
+        line_go(5).wait_send()
 
     @pl.when(core == 0)
     def _():
@@ -900,28 +916,32 @@
             jax.ShapeDtypeStruct((128, 768), bf16),
             jax.ShapeDtypeStruct((256, 768), bf16),
             jax.ShapeDtypeStruct((2, 128, 128), f32),
+            jax.ShapeDtypeStruct((16, 768), f32),
         ),
         in_specs=[smem] * 3 + [vmem] * 12 + [hbm] * 5,
-        out_specs=(hbm,) * 7,
+        out_specs=(hbm,) * 8,
         scratch_shapes=[
-            pltpu.VMEM((STAGES, 3 * ROWS, COLS), bf16),
-            pltpu.VMEM((UNITS + 1, 3 * ROWS, COLS), bf16),
-            pltpu.VMEM((UNITS + 1, 3 * ROWS, COLS), bf16),
-            pltpu.VMEM((UNITS + 1, 3 * ROWS, COLS), bf16),
-            pltpu.VMEM((UNITS + 1, 2, 288, COLS), bf16),
-            pltpu.VMEM((UNITS, 432, COLS), bf16),
-            pltpu.SemaphoreType.DMA((UNITS + 1, 29)),
-            pltpu.SemaphoreType.DMA((UNITS + 1, 29)),
-            pltpu.SemaphoreType.DMA((UNITS + 1, 4)),
+            pltpu.VMEM((STAGES, 3 * SLAB, COLS), bf16),
+            pltpu.VMEM((LAST + 1, 3 * SLAB, COLS), bf16),
+            pltpu.VMEM((LAST + 1, 3 * SLAB, COLS), bf16),
+            pltpu.VMEM((UNITS, 3 * SLAB, COLS), bf16),
+            pltpu.VMEM((256, COLS), bf16),
+            pltpu.VMEM((LAST + 1, 2, 160, COLS), bf16),
+            pltpu.VMEM((UNITS, 224, COLS), bf16),
+            pltpu.SemaphoreType.DMA((LAST + 1,)),
+            pltpu.SemaphoreType.DMA((14, TURNS)),
+            pltpu.SemaphoreType.DMA((STAGES + 1,)),
+            pltpu.SemaphoreType.DMA((LAST + 1,)),
+            pltpu.SemaphoreType.DMA((LAST + 1,)),
             pltpu.VMEM((768, 2304), bf16),
             pltpu.VMEM((768, 768), bf16),
             pltpu.VMEM((768, 3072), bf16),
             pltpu.VMEM((3072, 768), bf16),
-            pltpu.SemaphoreType.DMA((8,)),
+            pltpu.SemaphoreType.DMA((10,)),
             pltpu.VMEM((128, 128), f32),
             pltpu.VMEM((128, 128), f32),
             pltpu.VMEM(wide, bf16),
-            pltpu.VMEM((768, 128), bf16),
+            pltpu.VMEM(wide, bf16),
             pltpu.VMEM(wide, f32),
             pltpu.VMEM(wide, f32),
             pltpu.VMEM(wide, f32),
@@ -948,12 +968,18 @@
             pltpu.VMEM((8, 128), f32),
             pltpu.VMEM((128, 128), f32),
             pltpu.VMEM((8, 128), f32),
+            pltpu.VMEM((128, 128), f32),
             pltpu.VMEM((2, 128, 128), f32),
+            pltpu.VMEM((16, 768), f32),
+            pltpu.VMEM((5, 16, 768), f32),
+            pltpu.VMEM((5, 16, 768), f32),
+            pltpu.SemaphoreType.DMA((6,)),
+            pltpu.SemaphoreType.DMA((6,)),
+            pltpu.SemaphoreType.DMA,
             pltpu.VMEM((7, 768, 128), bf16),
             pltpu.VMEM((9, 2, 128, COLS), bf16),
-            pltpu.VMEM((2, 128, COLS), bf16),
-            pltpu.VMEM((2, 2, 128, COLS), bf16),
-            pltpu.VMEM((8, 768), f32),
+            pltpu.VMEM((256, COLS), bf16),
+            pltpu.VMEM((2, 256, COLS), bf16),
             pltpu.VMEM(wide, bf16),
             pltpu.SemaphoreType.DMA((6,)),
             pltpu.SemaphoreType.DMA((6,)),
@@ -971,80 +997,93 @@
 
 
 def finish_kernel(
-    labels_ref, down_ref, up_ref, out_ref, qkv_ref, pos_ref, small_ref, lat_ref,
+    labels_ref, pos_ref, small_ref, lat_ref, line_ref, down_ref, up_ref, out_ref, qkv_ref,
     new_latents, logdet, latents_grad, patch, pos, classes, g1, b1, qkv, out, g2, b2, up, ub, down, head, hb,
+    *scratch,
 ):
     dp = lax.axis_index("dp")
-    down[0] = down_ref[...].astype(f32)
-    up[0] = up_ref[...].astype(f32)
-    out[0] = out_ref[...].astype(f32)
-    qkv[0] = qkv_ref[...].astype(f32)
-
-    @pl.when(pl.program_id(0) == 0)
-    def _():
-        new_latents[0] = lat_ref[0, :, 0:48]
-        latents_grad[0] = lat_ref[1, :, 0:48]
-        pos[...] = pos_ref[...].astype(f32)
-        patch[...] = small_ref[96:144].astype(f32)
-        head[...] = small_ref[0:128].astype(f32).T[:, 0:96]
-        block = small_ref[160:176].astype(f32)
-        for i, one in enumerate((g1, b1, g2, b2)):
-            one[...] = block[i : i + 1]
-        for i in range(4):
-            ub[:, i * 768 : (i + 1) * 768] = block[4 + i : 5 + i]
-        hb[...] = block[8:9, 0:96]
-        count = labels_ref.shape[1]
-        terms = block[8:9, 128:256] + block[8:9, 256:384]
-        lane = lax.broadcasted_iota(jnp.int32, (1, 128), 1)
-        mine = jnp.logical_or(lane == dp, lane == count + dp)
-        logdet[...] = jnp.sum(jnp.where(mine, terms, 0.0), 1, keepdims=True)
-        by_lane = jnp.broadcast_to(labels_ref[...], (count, count)).astype(f32)
-        first = lax.broadcasted_iota(jnp.int32, (count, count), 0)
-        second = lax.broadcasted_iota(jnp.int32, (count, count), 1)
-        by_row = jnp.sum(jnp.where(first == second, by_lane, 0.0), 1, keepdims=True)
-        before = (by_lane < by_row) | ((by_lane == by_row) & (second < first))
-        rank = jnp.sum(jnp.where(before, 1.0, 0.0), 1, keepdims=True)
-        stored = jnp.sum(jnp.where(rank == second.astype(f32), by_row, 0.0), 0, keepdims=True)
-        owned = classes.shape[0]
-        wanted = (dp * owned + lax.broadcasted_iota(jnp.int32, (owned, count), 0)).astype(f32)
-        hot = jnp.where(stored == wanted, 1.0, 0.0).astype(bf16)
-        classes[...] = jnp.dot(hot, small_ref[144:160], preferred_element_type=f32)
-
-
-def finish(class_labels, down, up, out, qkv, pos, small, lat):
-    steps = 16
-
-    def blocked(rows, width):
-        return pl.BlockSpec((rows // steps, width), lambda i: (i, 0))
-
-    def blocked_out(rows, width):
-        return pl.BlockSpec((1, rows // steps, width), lambda i: (0, i, 0))
-
-    def kept(*shape):
-        return pl.BlockSpec(shape, lambda i: (0,) * len(shape))
-
+    narrow, wide, read_sem, write_sem = scratch[0:6:2], scratch[1:6:2], scratch[6], scratch[7]
+    moves = []
+    used = [0, 0, 0]
+    for src, dst, i, rows in (
+        (down_ref, down, 0, FINISH_ROWS), (up_ref, up, 2, FINISH_ROWS // 4),
+        (qkv_ref, qkv, 1, FINISH_ROWS // 3), (out_ref, out, 0, FINISH_ROWS),
+    ):
+        for row in range(0, src.shape[0], rows):
+            moves.append((src.at[row : row + rows], dst.at[0, row : row + rows], i, used[i]))
+            used[i] += 1
+
+    def read(m):
+        src, dst, i, slot = moves[m]
+        return pltpu.make_async_copy(src, narrow[i].at[slot], read_sem.at[m])
+
+    def write(m):
+        src, dst, i, slot = moves[m]
+        return pltpu.make_async_copy(wide[i].at[slot], dst, write_sem.at[m])
+
+    for m in range(AHEAD):
+        read(m).start()
+    for m in range(len(moves)):
+        i, slot = moves[m][2:]
+        read(m).wait()
+        if m + AHEAD < len(moves):
+            read(m + AHEAD).start()
+        wide[i][slot] = narrow[i][slot].astype(f32)
+        write(m).start()
+    new_latents[0] = lat_ref[0, 0:48]
+    latents_grad[0] = lat_ref[1, 0:48]
+    pos[...] = pos_ref[...].astype(f32)
+    patch[...] = small_ref[96:144].astype(f32)
+    head[...] = small_ref[0:96].astype(f32)
+    block = line_ref[...]
+    for i, one in enumerate((g1, b1, g2, b2)):
+        one[...] = block[i : i + 1]
+    for i in range(4):
+        ub[:, i * 768 : (i + 1) * 768] = block[4 + i : 5 + i]
+    hb[...] = block[8:9, 0:96]
+    count = labels_ref.shape[1]
+    lane = lax.broadcasted_iota(jnp.int32, (1, 128), 1)
+    logdet[...] = jnp.sum(jnp.where(lane == dp, block[8:9, 128:256], 0.0), 1, keepdims=True)
+    by_lane = jnp.broadcast_to(labels_ref[...], (count, count)).astype(f32)
+    first = lax.broadcasted_iota(jnp.int32, (count, count), 0)
+    second = lax.broadcasted_iota(jnp.int32, (count, count), 1)
+    by_row = jnp.sum(jnp.where(first == second, by_lane, 0.0), 1, keepdims=True)
+    before = (by_lane < by_row) | ((by_lane == by_row) & (second < first))
+    rank = jnp.sum(jnp.where(before, 1.0, 0.0), 1, keepdims=True)
+    stored = jnp.sum(jnp.where(rank == second.astype(f32), by_row, 0.0), 0, keepdims=True)
+    owned = classes.shape[0]
+    wanted = (dp * owned + lax.broadcasted_iota(jnp.int32, (owned, count), 0)).astype(f32)
+    hot = jnp.where(stored == wanted, 1.0, 0.0).astype(bf16)
+    classes[...] = jnp.dot(hot, small_ref[144:160], preferred_element_type=f32)
+    for m in range(len(moves)):
+        write(m).wait()
+
+
+def finish(class_labels, down, up, out, qkv, pos, small, lat, line_sums):
     count = class_labels.shape[1]
     owned = 1024 // count
     shapes = [
-        (1, 128, 48), (1, 1), (1, 128, 48), (48, 768), (128, 768), (owned, 768), (1, 768), (1, 768),
+        (1, 48, 128), (1, 1), (1, 48, 128), (48, 768), (128, 768), (owned, 768), (1, 768), (1, 768),
         (1, 768, 2304), (1, 768, 768), (1, 768), (1, 768), (1, 768, 3072), (1, 3072), (1, 3072, 768),
-        (768, 96), (1, 96),
+        (96, 768), (1, 96),
     ]
-    specs = [kept(*shape) for shape in shapes]
-    specs[8], specs[9] = blocked_out(768, 2304), blocked_out(768, 768)
-    specs[12], specs[14] = blocked_out(768, 3072), blocked_out(3072, 768)
+    vmem = pl.BlockSpec(memory_space=pltpu.VMEM)
+    hbm = pl.BlockSpec(memory_space=pl.ANY)
+    buffers = []
+    for columns, total in ((768, 3840), (2304, 768), (3072, 768)):
+        rows = FINISH_ROWS * 768 // columns
+        for kind in (bf16, f32):
+            buffers.append(pltpu.VMEM((total // rows, rows, columns), kind))
+    pieces = 3840 // FINISH_ROWS + 2304 // FINISH_ROWS + 3072 // FINISH_ROWS
     return pl.pallas_call(
         finish_kernel,
-        grid=(steps,),
         out_shape=[jax.ShapeDtypeStruct(shape, f32) for shape in shapes],
-        in_specs=[
-            kept(1, count), blocked(3072, 768), blocked(768, 3072), blocked(768, 768), blocked(768, 2304),
-            kept(128, 768), kept(256, 768), kept(2, 128, 128),
-        ],
-        out_specs=specs,
-        compiler_params=pltpu.CompilerParams(vmem_limit_bytes=40 << 20),
+        in_specs=[vmem] * 5 + [hbm] * 4,
+        out_specs=[hbm if i in (8, 9, 12, 14) else vmem for i in range(17)],
+        scratch_shapes=buffers + [pltpu.SemaphoreType.DMA((pieces,)), pltpu.SemaphoreType.DMA((pieces,))],
+        compiler_params=pltpu.CompilerParams(vmem_limit_bytes=62 << 20),
         name="finish",
-    )(class_labels, down, up, out, qkv, pos, small, lat)
+    )(class_labels, pos, small, lat, line_sums, down, up, out, qkv)
 
 
 def fast_local(
@@ -1053,13 +1092,15 @@
     cot_latents, cot_logdet,
 ):
     sums = flow(
-        class_labels, group_perm, cot_logdet, latents, valid, patch_weight, pos_table, ln1_gain, ln1_bias,
-        ln2_gain, ln2_bias, up_bias, head_weight, head_bias[None], cot_latents, class_table,
+        class_labels, group_perm, cot_logdet, latents.swapaxes(1, 2), valid, patch_weight, pos_table, ln1_gain,
+        ln1_bias, ln2_gain, ln2_bias, up_bias, head_weight.T, head_bias[None], cot_latents.swapaxes(1, 2), class_table,
         qkv_weight, out_weight, up_weight, down_weight,
     )
     results = list(finish(class_labels[None], *sums))
     results[1] = results[1].reshape(1)
     results[16] = results[16].reshape(96)
+    results[0], results[2] = results[0].swapaxes(1, 2), results[2].swapaxes(1, 2)
+    results[15] = results[15].T
     return tuple(results)
 
 

time: 186 us -> 158 us (0.85)
  local copies, waits for them, and re-layouts: 15.3 us -> 0 us
  Pallas kernels: 168 us -> 156 us
    unnamed x20 -> x0, local copies, waits for them, and re-layouts: 15.3 us -> none
    pallas_call x1, Pallas kernels: 153 us -> 140 us  [flow(): pl.pallas_call(flow_kernel, out_shape=(jax.ShapeDtypeStruct((3072, 768),...]
where the time goes in v3:
time: 158 us; the launch traced here: 157 us
  Pallas kernels  156 us (99%)
  between operations  1.96 us (1%)
    pallas_call x1, Pallas kernels, flow(): pl.pallas_call(flow_kernel, out_shape=(jax.ShapeDtypeStruct((3072, 768),...  140 us
    pallas_call x1, Pallas kernels, finish(): pl.pallas_call(finish_kernel, out_shape=[jax.ShapeDtypeStruct(shape, f32)...  15.8 us

profile of v3, /device:TPU:0, one launch (start us, length us, event | category | flops | bytes accessed | tf_op | source)
XLA Modules:
  0.0 157.5 jit_solution(7474362252219623467)
XLA Ops:
  2.0 139.8 %flow.1 = (bf16[3072,768]{1,0:T(8,128)(2,1)}, bf16[768,3072]{1,0:T(8,128)(2,1)}, bf16[768,768]{1,0:T(8,128)(2,1)}, bf16[768,2304]{1,0:T(8,128)(2,1)}, bf16[128,7...) custom-call(s32[16]{0:T(128)} %labels_sm.1, s32[1]{0:T(128)S(6)} %copy.37.perm_sm, ...), custom_call_target="tpu_custom_call" | custom-call | tf_op jit(solution)/shard_map/flow/pallas_call | solution.py:909
  141.7 15.8 %finish.1 = (f32[1,48,128]{2,1,0:T(8,128)}, f32[1,1]{1,0:T(1,128)}, f32[1,48,128]{2,1,0:T(8,128)}, f32[48,768]{1,0:T(8,128)}, f32[128,768]{1,0:T(8,128)}, /*inde...) custom-call(s32[1,16]{1,0:T(1,128)} %bitcast.13, ...), custom_call_target="tpu_custom_call" | custom-call | tf_op jit(solution)/shard_map/finish/pallas_call | solution.py:1078

commit v4 on v3

--- a/solution.py
+++ b/solution.py
@@ -67,10 +67,10 @@
 UNITS = 24
 LAST = 25
 TURNS = 13
+STEPS = 38
+DRAIN = 14
 SLAB = 128
 TABLE_ROWS = ((0, 384), (384, 384), (768, 256))
-FINISH_ROWS = 768
-AHEAD = 6
 COLS = 384
 STAGES = 3
 CHUNK = 32
@@ -85,8 +85,8 @@
     latents_ref, valid_ref, patch_ref, pos_table_ref, g1_ref, b1_ref, g2_ref, b2_ref,
     up_bias_ref, head_w_ref, head_b_ref, cot_ref,
     class_hbm, qkv_any, out_any, up_any, down_any,
-    down_hbm, up_hbm, out_hbm, qkv_hbm, pos_hbm, small_hbm, latents_hbm, lines_hbm,
-    stage, part, full, core_in, small_in, ab_in, c_in, send_sem, recv_sem, stage_sem, back_sem, local_sem,
+    sums, latents_hbm, lines_hbm,
+    stage, part, core_in, small_in, ab_in, c_in, send_sem, recv_sem, stage_sem, back_sem,
     qkv_w, out_w, up_w, down_w, load_sem,
     lat_pad, cot_pad, patch_pad, head_pad, hidden, mid, xhat1, xhat2, scale1, scale2,
     keys, values, query, attended, bias, prior_mask, mask_row, probs, slope, d_hidden, d_second, d_att, d_keys, d_values,
@@ -127,11 +127,15 @@
     @pl.when(inner)
     def _():
         pl.semaphore_signal(barrier, inc=1, device_id=to_inner, device_id_type=MESH)
-        pl.semaphore_wait(barrier, 5)
-
-    @pl.when(outer)
-    def _():
-        pl.semaphore_wait(barrier, 4)
+
+    def meet():
+        @pl.when(inner)
+        def _():
+            pl.semaphore_wait(barrier, 5)
+
+        @pl.when(outer)
+        def _():
+            pl.semaphore_wait(barrier, 4)
 
     def copy(u, k, src, dst, target):
         return pltpu.make_async_remote_copy(
@@ -151,7 +155,7 @@
     to_second = (to_y, to_x)
 
     def out_rows(u, t, start, count):
-        return full.at[u, rows_at(t * SLAB + start, count)]
+        return sums.at[u, core, rows_at(t * SLAB + start, count)]
 
     def part_rows(u, t, start, count):
         return part.at[u, rows_at(t * SLAB + start, count)]
@@ -168,7 +172,7 @@
 
     def core_first(u):
         return pltpu.make_async_remote_copy(
-            src_ref=stage.at[u % STAGES], dst_ref=core_in.at[u], send_sem=stage_sem.at[u % STAGES],
+            src_ref=stage.at[u % STAGES], dst_ref=core_in.at[u % TURNS], send_sem=stage_sem.at[u % STAGES],
             recv_sem=recv_sem.at[0, u % TURNS], device_id=to_core, device_id_type=MESH,
         )
 
@@ -221,10 +225,10 @@
     def begin(u):
         @pl.when(u < UNITS)
         def _():
-            arrived(u, 0, core_in.at[u])
+            arrived(u, 0, core_in.at[u % TURNS])
             for t in range(3):
                 rows = slice(t * SLAB, (t + 1) * SLAB)
-                part[u, rows] = (product(u, t, core) + core_in[u, rows].astype(f32)).astype(bf16)
+                part[u, rows] = (product(u, t, core) + core_in[u % TURNS, rows].astype(f32)).astype(bf16)
                 if t < 2:
                     ab_first(u, t).start()
             pl.when(outer)(lambda: c_z1(u).start())
@@ -248,17 +252,17 @@
         return first[t] * 64 + second[t] * 32
 
     def ab_first(u, t):
-        return copy(u, 1, part_rows(u, t, (1 - first[t]) * 64, 64), ab_in.at[u, t, 0:64], to_first[t])
+        return copy(u, 1, part_rows(u, t, (1 - first[t]) * 64, 64), ab_in.at[u % TURNS, t, 0:64], to_first[t])
 
     def ab_second(u, t):
         row = first[t] * 64 + (1 - second[t]) * 32
-        return copy(u, 2, part_rows(u, t, row, 32), ab_in.at[u, t, 64:96], to_second[t])
+        return copy(u, 2, part_rows(u, t, row, 32), ab_in.at[u % TURNS, t, 64:96], to_second[t])
 
     def ab_z1(u, t):
-        return copy(u, 3, part_rows(u, t, ab_base(t), 32), ab_in.at[u, t, 96:128], to_mate)
+        return copy(u, 3, part_rows(u, t, ab_base(t), 32), ab_in.at[u % TURNS, t, 96:128], to_mate)
 
     def ab_z2(u, t):
-        return copy(u, 4, part_rows(u, t, ab_base(t), 32), ab_in.at[u, t, 128:160], to_inner)
+        return copy(u, 4, part_rows(u, t, ab_base(t), 32), ab_in.at[u % TURNS, t, 128:160], to_inner)
 
     def ab_z3(u, t):
         block = out_rows(u, t, ab_base(t), 32)
@@ -273,10 +277,10 @@
         return copy(u, 6, block, block, to_first[t])
 
     def ab1(u):
-        arrived(u, 1, ab_in.at[u, :, 0:64])
+        arrived(u, 1, ab_in.at[u % TURNS, :, 0:64])
         for t in range(2):
             kept = part_rows(u, t, first[t] * 64, 64)
-            added(kept, kept, ab_in.at[u, t, 0:64])
+            added(kept, kept, ab_in.at[u % TURNS, t, 0:64])
             ab_second(u, t).start()
 
         @pl.when(u == LAST)
@@ -285,10 +289,10 @@
             line_go(2).start()
 
     def ab2(u):
-        arrived(u, 2, ab_in.at[u, :, 64:96])
+        arrived(u, 2, ab_in.at[u % TURNS, :, 64:96])
         for t in range(2):
             kept = part_rows(u, t, ab_base(t), 32)
-            added(kept, kept, ab_in.at[u, t, 64:96])
+            added(kept, kept, ab_in.at[u % TURNS, t, 64:96])
             pl.when(outer)(lambda: ab_z1(u, t).start())
 
         @pl.when(u == LAST)
@@ -297,10 +301,10 @@
             pl.when(outer)(line_go(3).start)
 
     def ab3_inner(u):
-        arrived(u, 3, ab_in.at[u, :, 96:128])
+        arrived(u, 3, ab_in.at[u % TURNS, :, 96:128])
         for t in range(2):
             kept = part_rows(u, t, ab_base(t), 32)
-            added(kept, kept, ab_in.at[u, t, 96:128])
+            added(kept, kept, ab_in.at[u % TURNS, t, 96:128])
             ab_z2(u, t).start()
 
         @pl.when(u == LAST)
@@ -309,9 +313,9 @@
             line_go(4).start()
 
     def ab4_inner(u):
-        arrived(u, 4, ab_in.at[u, :, 128:160])
+        arrived(u, 4, ab_in.at[u % TURNS, :, 128:160])
         for t in range(2):
-            added(out_rows(u, t, ab_base(t), 32), part_rows(u, t, ab_base(t), 32), ab_in.at[u, t, 128:160])
+            added(out_rows(u, t, ab_base(t), 32), part_rows(u, t, ab_base(t), 32), ab_in.at[u % TURNS, t, 128:160])
             ab_z3(u, t).start()
             ab_back2(u, t).start()
 
@@ -322,7 +326,7 @@
             line_out.start()
 
     def ab5_outer(u):
-        arrived(u, 3, full.at[u, 0:64])
+        arrived(u, 3, sums.at[u, core, 0:64])
         for t in range(2):
             ab_back2(u, t).start()
 
@@ -332,66 +336,23 @@
             line_out.start()
 
     def ab6(u):
-        arrived(u, 5, full.at[u, 0:64])
+        arrived(u, 5, sums.at[u, core, 0:64])
         for t in range(2):
             ab_back1(u, t).start()
 
-    def place(u, h, row, count, act):
-        def columns(base):
-            return pl.ds(pl.multiple_of(base + h * COLS, 128), COLS)
-
-        block, top = u // 2, (u % 2) * 384 + row
-
-        @pl.when(block < 4)
-        def _():
-            act(down_hbm.at[rows_at(block * 768 + top, count), columns(0)])
-
-        @pl.when(jnp.logical_and(block >= 4, block < 8))
-        def _():
-            act(up_hbm.at[rows_at(top, count), columns((block - 4) * 768)])
-
-        @pl.when(block == 8)
-        def _():
-            act(out_hbm.at[rows_at(top, count), columns(0)])
-
-        @pl.when(jnp.logical_and(block >= 9, block < 12))
-        def _():
-            act(qkv_hbm.at[rows_at(top, count), columns((block - 9) * 768)])
-
-    def to_other(u, src, dst):
+    def spread(u, row, count):
+        block = sums.at[u, core, row : row + count]
+        to_other(u, block).start()
+
+    def to_other(u, block):
         return pltpu.make_async_remote_copy(
-            src_ref=src, dst_ref=dst, send_sem=send_sem.at[u], recv_sem=back_sem.at[u],
+            src_ref=block, dst_ref=block, send_sem=send_sem.at[u], recv_sem=back_sem.at[u],
             device_id=to_core, device_id_type=MESH,
         )
 
-    def to_own(u, src, dst):
-        return pltpu.make_async_copy(src, dst, local_sem.at[u])
-
-    def both_ways(u, src, dst):
-        to_other(u, src, dst).start()
-        to_own(u, src, dst).start()
-
-    def spread(u, row, count):
-        place(u, core, row, count, lambda dst: both_ways(u, full.at[u, row : row + count], dst))
-
-    def small_out(h, t):
-        return small_hbm.at[pl.ds(pl.multiple_of(h * 128, 128), 128), t * COLS : (t + 1) * COLS]
-
     def ab7(u):
-        arrived(u, 6, full.at[u, 0:128])
-        spread(u, 0, 2 * SLAB)
-
-        @pl.when(u == UNITS)
-        def _():
-            for t in range(2):
-                to_own(
-                    UNITS, full.at[UNITS, t * 128 : (t + 1) * 128], pos_hbm.at[:, t * COLS : (t + 1) * COLS]
-                ).start()
-
-        @pl.when(u == LAST)
-        def _():
-            for t in range(2):
-                both_ways(LAST, full.at[LAST, t * 128 : (t + 1) * 128], small_out(core, t))
+        arrived(u, 6, sums.at[u, core, 0:128])
+        pl.when(u != UNITS)(lambda: spread(u, 0, 2 * SLAB))
 
     far = 32 * (1 - side)
     own_end = 96 * side
@@ -399,19 +360,19 @@
     half = shard + x * 16
 
     def c_z1(u):
-        return copy(u, 7, part_rows(u, 2, far, 96), c_in.at[u, 0:96], to_mate)
+        return copy(u, 7, part_rows(u, 2, far, 96), c_in.at[u % TURNS, 0:96], to_mate)
 
     def c_z2(u):
-        return copy(u, 8, part_rows(u, 2, (1 - side) * 64, 64), c_in.at[u, 96:160], to_inner)
+        return copy(u, 8, part_rows(u, 2, (1 - side) * 64, 64), c_in.at[u % TURNS, 96:160], to_inner)
 
     def c_z3(u):
-        return copy(u, 7, part_rows(u, 2, own_end, 32), c_in.at[u, 160:192], to_mate)
+        return copy(u, 7, part_rows(u, 2, own_end, 32), c_in.at[u % TURNS, 160:192], to_mate)
 
     def c_x(u):
-        return copy(u, 9, part_rows(u, 2, shard + (1 - x) * 16, 16), c_in.at[u, 192:208], to_x)
+        return copy(u, 9, part_rows(u, 2, shard + (1 - x) * 16, 16), c_in.at[u % TURNS, 192:208], to_x)
 
     def c_y(u):
-        return copy(u, 10, part_rows(u, 2, half, 16), c_in.at[u, 208:224], to_y)
+        return copy(u, 10, part_rows(u, 2, half, 16), c_in.at[u % TURNS, 208:224], to_y)
 
     def c_back_x(u):
         block = out_rows(u, 2, half, 16)
@@ -430,40 +391,41 @@
         return copy(u, 12, block, block, to_mate)
 
     def c1_inner(u):
-        arrived(u, 7, c_in.at[u, 0:96])
+        arrived(u, 7, c_in.at[u % TURNS, 0:96])
         kept = part_rows(u, 2, far, 96)
-        added(kept, kept, c_in.at[u, 0:96])
+        added(kept, kept, c_in.at[u % TURNS, 0:96])
         c_z2(u).start()
 
     def c2_inner(u):
-        arrived(u, 8, c_in.at[u, 96:160])
+        arrived(u, 8, c_in.at[u % TURNS, 96:160])
         kept = part_rows(u, 2, side * 64, 64)
-        added(kept, kept, c_in.at[u, 96:160])
+        added(kept, kept, c_in.at[u % TURNS, 96:160])
         c_z3(u).start()
         c_x(u).start()
 
     def c3_outer(u):
-        arrived(u, 7, c_in.at[u, 160:192])
+        arrived(u, 7, c_in.at[u % TURNS, 160:192])
         kept = part_rows(u, 2, shard, 32)
-        added(kept, kept, c_in.at[u, 160:192])
+        added(kept, kept, c_in.at[u % TURNS, 160:192])
         c_x(u).start()
 
     def c4(u):
-        arrived(u, 9, c_in.at[u, 192:208])
+        arrived(u, 9, c_in.at[u % TURNS, 192:208])
         kept = part_rows(u, 2, half, 16)
-        added(kept, kept, c_in.at[u, 192:208])
+        added(kept, kept, c_in.at[u % TURNS, 192:208])
         c_y(u).start()
 
     def c5(u):
-        arrived(u, 10, c_in.at[u, 208:224])
-        added(out_rows(u, 2, half, 16), part_rows(u, 2, half, 16), c_in.at[u, 208:224])
+        arrived(u, 10, c_in.at[u % TURNS, 208:224])
+        added(out_rows(u, 2, half, 16), part_rows(u, 2, half, 16), c_in.at[u % TURNS, 208:224])
         c_back_x(u).start()
 
-    def c7(u):
+    def c7_outer(u):
         arrived(u, 11, out_rows(u, 2, shard + (1 - x) * 16, 16))
-        pl.when(outer)(lambda: c_z4(u).start())
+        c_z4(u).start()
 
     def c8_inner(u):
+        arrived(u, 11, out_rows(u, 2, shard + (1 - x) * 16, 16))
         arrived(u, 12, out_rows(u, 2, own_end, 32))
         c_z5(u).start()
 
@@ -476,31 +438,14 @@
         arrived(u, 12, out_rows(u, 2, far, 96))
         spread(u, 2 * SLAB, SLAB)
 
-    everyone, inners, outers = None, inner, outer
-    events = [
-        (1, LAST + 1, everyone, begin),
-        (2, LAST + 1, everyone, ab1),
-        (3, LAST + 1, everyone, ab2),
-        (2, UNITS, inners, c1_inner),
-        (3, UNITS, inners, c2_inner),
-        (4, UNITS, outers, c3_outer),
-        (4, LAST + 1, inners, ab3_inner),
-        (5, LAST + 1, inners, ab4_inner),
-        (6, LAST + 1, outers, ab5_outer),
-        (4, UNITS, inners, c4),
-        (5, UNITS, outers, c4),
-        (5, UNITS, inners, c5),
-        (6, UNITS, outers, c5),
-        (6, UNITS, inners, c7),
-        (7, UNITS, outers, c7),
-        (6, LAST + 1, inners, ab6),
-        (7, LAST + 1, outers, ab6),
-        (7, LAST + 1, inners, ab7),
-        (8, LAST + 1, outers, ab7),
-        (8, UNITS, inners, c8_inner),
-        (9, UNITS, inners, c9_inner),
-        (10, UNITS, outers, c10_outer),
-    ]
+    def sent(u, units, rows):
+        ref = part.at[0:units, 0:rows]
+        copy(u, 0, ref, ref, to_core).wait_send()
+
+    def drain(u):
+        pl.when(outer)(lambda: sent(u, 3, 336))
+        pl.when(inner)(lambda: sent(u, 5, 240))
+        to_other(u, sums.at[u, 1 - core]).wait_recv()
 
     mm_nt = (((1,), (1,)), ((), ()))
     mm_tn = (((0,), (0,)), ((), ()))
@@ -552,10 +497,6 @@
         grad_in[...] = jnp.zeros((8, 128), f32)
         d_back[...] = jnp.zeros((2, 128, 768), bf16)
 
-    @pl.when(core == 0)
-    def _():
-        exchange(2, mask_row, prior_mask).start()
-
     def normalize(src, hat, scale, gain, shift, put):
         for r in chunks:
             v = src[r]
@@ -588,9 +529,11 @@
     load(6).wait()
     normed = low_top[...]
     keys[128:256] = nn(normed, qkv_w[:, 768:1536]).astype(bf16)
+    meet()
 
     @pl.when(core == 0)
     def _():
+        exchange(2, mask_row, prior_mask).start()
         exchange(0, keys.at[128:256], keys.at[0:128]).start()
 
     values[128:256] = nn(normed, qkv_w[:, 1536:2304]).astype(bf16)
@@ -614,7 +557,7 @@
     def columns128(p):
         return pl.ds(pl.multiple_of(p * 128, 128), 128)
 
-    def attend(p, carried):
+    def attend(p):
         cols = columns128(p)
         q_pair = query[:, cols]
         k_pair = keys[:, cols]
@@ -629,9 +572,9 @@
             probs[2 * p + i] = soft
             outs.append(nn(soft.astype(bf16), v_pair))
         attended[:, cols] = jnp.where(low_half, outs[0], outs[1]).astype(bf16)
-        return carried
-
-    lax.fori_loop(0, 6, attend, 0)
+
+    for p in range(6):
+        attend(p)
     load(7).wait()
     mid[...] = hidden[...] + nn(attended[...], out_w[...])
     lt_ref[5] = attended[...].astype(f32).T.astype(bf16)
@@ -817,9 +760,7 @@
         put(144, jnp.where(line == dp, class_grad, 0.0))
         put(160, jnp.zeros((96, 768), f32))
 
-    def both(t):
-        produce_now(t)
-
+    def piece(t):
         @pl.when(jnp.logical_and(t < 8, t % 2 == 0))
         def _():
             feed_back(t // 2)
@@ -834,11 +775,35 @@
         pl.when(t == 16)(packed_back)
         pl.when(t == 18)(embed_back)
 
-    def produce_now(t):
-        pl.when(t <= LAST)(lambda: produce(t))
+    everyone, inners, outers = None, inner, outer
+    events = [
+        (0, LAST + 1, everyone, produce),
+        (2, UNITS, inners, c1_inner),
+        (1, LAST + 1, everyone, begin),
+        (7, UNITS, inners, c5),
+        (9, LAST + 1, inners, ab6),
+        (3, UNITS, inners, c2_inner),
+        (4, LAST + 1, inners, ab3_inner),
+        (0, LAST + 1, everyone, piece),
+        (2, LAST + 1, everyone, ab1),
+        (5, LAST + 1, inners, ab4_inner),
+        (11, LAST + 1, outers, ab7),
+        (5, UNITS, inners, c4),
+        (8, UNITS, inners, c8_inner),
+        (12, LAST + 1, inners, ab7),
+        (9, UNITS, inners, c9_inner),
+        (3, LAST + 1, everyone, ab2),
+        (6, UNITS, outers, c5),
+        (7, UNITS, outers, c7_outer),
+        (4, UNITS, outers, c3_outer),
+        (5, UNITS, outers, c4),
+        (12, UNITS, outers, c10_outer),
+        (7, LAST + 1, outers, ab5_outer),
+        (8, LAST + 1, outers, ab6),
+        (DRAIN, UNITS, everyone, drain),
+    ]
 
     def step(t, carried):
-        both(t)
         for lag, count, who, event in events:
             u = t - lag
             now = jnp.logical_and(u >= 0, u < count)
@@ -847,29 +812,19 @@
             pl.when(now)(lambda event=event, u=u: event(u))
         return carried
 
-    lax.fori_loop(0, LAST + 9, step, 0)
-
-    def sent(u, units, rows):
-        ref = full.at[0:units, 0:rows]
-        copy(u, 0, ref, ref, to_core).wait_send()
-
-    def drain(u, carried):
-        pl.when(outer)(lambda: sent(u, 3, 336))
-        pl.when(inner)(lambda: sent(u, 5, 240))
-        place(u, core, 0, 3 * SLAB, lambda dst: to_own(u, full.at[u], dst).wait())
-        place(u, 1 - core, 0, 3 * SLAB, lambda dst: to_other(u, full.at[u], dst).wait_recv())
+    lax.fori_loop(0, STEPS, step, 0)
+
+
+    def drain_more(u, carried):
+        drain(u)
         return carried
 
-    lax.fori_loop(0, UNITS, drain, 0)
+    lax.fori_loop(STEPS - DRAIN, UNITS, drain_more, 0)
     pl.when(outer)(lambda: sent(UNITS, 2, 224))
     pl.when(inner)(lambda: sent(UNITS, 2, 256))
-    to_own(UNITS, pos_hbm, pos_hbm).wait()
     pl.when(outer)(lambda: sent(LAST, 2, 352))
     pl.when(inner)(lambda: sent(LAST, 2, 384))
-    own_small = small_hbm.at[pl.ds(pl.multiple_of(core * 128, 128), 128)]
-    other_small = small_hbm.at[pl.ds(pl.multiple_of((1 - core) * 128, 128), 128)]
-    to_own(LAST, own_small, own_small).wait()
-    to_other(LAST, other_small, other_small).wait_recv()
+    to_other(LAST, sums.at[LAST, 1 - core, 0 : 2 * SLAB]).wait_recv()
     for u in range(UNITS - STAGES, UNITS):
         core_first(u).wait_send()
     small_first().wait_send()
@@ -904,34 +859,27 @@
 ):
     smem = pl.BlockSpec(memory_space=pltpu.SMEM)
     vmem = pl.BlockSpec(memory_space=pltpu.VMEM)
-    hbm = pl.BlockSpec(memory_space=pl.ANY)
+    hbm = pl.BlockSpec(memory_space=pltpu.HBM)
     wide = (128, 768)
     return pl.pallas_call(
         flow_kernel,
         out_shape=(
-            jax.ShapeDtypeStruct((3072, 768), bf16),
-            jax.ShapeDtypeStruct((768, 3072), bf16),
-            jax.ShapeDtypeStruct((768, 768), bf16),
-            jax.ShapeDtypeStruct((768, 2304), bf16),
-            jax.ShapeDtypeStruct((128, 768), bf16),
-            jax.ShapeDtypeStruct((256, 768), bf16),
+            pltpu.VMEM((LAST + 1, 2, 3 * SLAB, COLS), bf16),
             jax.ShapeDtypeStruct((2, 128, 128), f32),
             jax.ShapeDtypeStruct((16, 768), f32),
         ),
         in_specs=[smem] * 3 + [vmem] * 12 + [hbm] * 5,
-        out_specs=(hbm,) * 8,
+        out_specs=(vmem, hbm, hbm),
         scratch_shapes=[
             pltpu.VMEM((STAGES, 3 * SLAB, COLS), bf16),
             pltpu.VMEM((LAST + 1, 3 * SLAB, COLS), bf16),
-            pltpu.VMEM((LAST + 1, 3 * SLAB, COLS), bf16),
-            pltpu.VMEM((UNITS, 3 * SLAB, COLS), bf16),
+            pltpu.VMEM((TURNS, 3 * SLAB, COLS), bf16),
             pltpu.VMEM((256, COLS), bf16),
-            pltpu.VMEM((LAST + 1, 2, 160, COLS), bf16),
-            pltpu.VMEM((UNITS, 224, COLS), bf16),
+            pltpu.VMEM((TURNS, 2, 160, COLS), bf16),
+            pltpu.VMEM((TURNS, 224, COLS), bf16),
             pltpu.SemaphoreType.DMA((LAST + 1,)),
             pltpu.SemaphoreType.DMA((14, TURNS)),
             pltpu.SemaphoreType.DMA((STAGES + 1,)),
-            pltpu.SemaphoreType.DMA((LAST + 1,)),
             pltpu.SemaphoreType.DMA((LAST + 1,)),
             pltpu.VMEM((768, 2304), bf16),
             pltpu.VMEM((768, 768), bf16),
@@ -986,7 +934,7 @@
             pltpu.SemaphoreType.DMA,
         ],
         compiler_params=pltpu.CompilerParams(
-            collective_id=0, has_side_effects=True, vmem_limit_bytes=62 << 20
+            collective_id=0, has_side_effects=True, vmem_limit_bytes=46 << 20
         ),
         name="flow",
     )(
@@ -997,69 +945,89 @@
 
 
 def finish_kernel(
-    labels_ref, pos_ref, small_ref, lat_ref, line_ref, down_ref, up_ref, out_ref, qkv_ref,
+    labels_ref, sums, lat_hbm, line_hbm,
     new_latents, logdet, latents_grad, patch, pos, classes, g1, b1, qkv, out, g2, b2, up, ub, down, head, hb,
-    *scratch,
+    wide, write_sem, lat_ref, line_ref, pos_wide, small_wide, class_wide, in_sem, out_sem,
 ):
     dp = lax.axis_index("dp")
-    narrow, wide, read_sem, write_sem = scratch[0:6:2], scratch[1:6:2], scratch[6], scratch[7]
-    moves = []
-    used = [0, 0, 0]
-    for src, dst, i, rows in (
-        (down_ref, down, 0, FINISH_ROWS), (up_ref, up, 2, FINISH_ROWS // 4),
-        (qkv_ref, qkv, 1, FINISH_ROWS // 3), (out_ref, out, 0, FINISH_ROWS),
-    ):
-        for row in range(0, src.shape[0], rows):
-            moves.append((src.at[row : row + rows], dst.at[0, row : row + rows], i, used[i]))
-            used[i] += 1
-
-    def read(m):
-        src, dst, i, slot = moves[m]
-        return pltpu.make_async_copy(src, narrow[i].at[slot], read_sem.at[m])
-
-    def write(m):
-        src, dst, i, slot = moves[m]
-        return pltpu.make_async_copy(wide[i].at[slot], dst, write_sem.at[m])
-
-    for m in range(AHEAD):
-        read(m).start()
-    for m in range(len(moves)):
-        i, slot = moves[m][2:]
-        read(m).wait()
-        if m + AHEAD < len(moves):
-            read(m + AHEAD).start()
-        wide[i][slot] = narrow[i][slot].astype(f32)
-        write(m).start()
-    new_latents[0] = lat_ref[0, 0:48]
-    latents_grad[0] = lat_ref[1, 0:48]
-    pos[...] = pos_ref[...].astype(f32)
-    patch[...] = small_ref[96:144].astype(f32)
-    head[...] = small_ref[0:96].astype(f32)
-    block = line_ref[...]
-    for i, one in enumerate((g1, b1, g2, b2)):
-        one[...] = block[i : i + 1]
-    for i in range(4):
-        ub[:, i * 768 : (i + 1) * 768] = block[4 + i : 5 + i]
-    hb[...] = block[8:9, 0:96]
-    count = labels_ref.shape[1]
-    lane = lax.broadcasted_iota(jnp.int32, (1, 128), 1)
-    logdet[...] = jnp.sum(jnp.where(lane == dp, block[8:9, 128:256], 0.0), 1, keepdims=True)
-    by_lane = jnp.broadcast_to(labels_ref[...], (count, count)).astype(f32)
-    first = lax.broadcasted_iota(jnp.int32, (count, count), 0)
-    second = lax.broadcasted_iota(jnp.int32, (count, count), 1)
-    by_row = jnp.sum(jnp.where(first == second, by_lane, 0.0), 1, keepdims=True)
-    before = (by_lane < by_row) | ((by_lane == by_row) & (second < first))
-    rank = jnp.sum(jnp.where(before, 1.0, 0.0), 1, keepdims=True)
-    stored = jnp.sum(jnp.where(rank == second.astype(f32), by_row, 0.0), 0, keepdims=True)
+    core = lax.axis_index("seq")
     owned = classes.shape[0]
-    wanted = (dp * owned + lax.broadcasted_iota(jnp.int32, (owned, count), 0)).astype(f32)
-    hot = jnp.where(stored == wanted, 1.0, 0.0).astype(bf16)
-    classes[...] = jnp.dot(hot, small_ref[144:160], preferred_element_type=f32)
-    for m in range(len(moves)):
-        write(m).wait()
-
-
-def finish(class_labels, down, up, out, qkv, pos, small, lat, line_sums):
+    inputs = [
+        pltpu.make_async_copy(src, dst, in_sem.at[i])
+        for i, (src, dst) in enumerate(
+            ((lat_hbm, lat_ref), (line_hbm, line_ref))
+        )
+    ]
+    outputs = [
+        pltpu.make_async_copy(src, dst, out_sem.at[i])
+        for i, (src, dst) in enumerate(
+            (
+                (lat_ref.at[0, 0:48], new_latents.at[0]),
+                (lat_ref.at[1, 0:48], latents_grad.at[0]),
+                (small_wide.at[0:96], head),
+                (small_wide.at[96:144], patch),
+                (pos_wide, pos),
+                (class_wide, classes),
+            )
+        )
+    ]
+    def write(u):
+        block, row = u // 2, (u % 2) * 384
+        if block < 4:
+            dst = down.at[0, block * 768 + row : block * 768 + row + 384]
+        else:
+            target, column = (up, block - 4) if block < 8 else (out, 0) if block == 8 else (qkv, block - 9)
+            dst = target.at[0, row : row + 384, column * 768 : (column + 1) * 768]
+        return pltpu.make_async_copy(wide.at[u], dst, write_sem.at[u])
+
+    def little():
+        for one in inputs:
+            one.wait()
+        outputs[0].start()
+        outputs[1].start()
+        for t in range(2):
+            rows, cols = slice(t * 128, (t + 1) * 128), slice(t * COLS, (t + 1) * COLS)
+            pos_wide[:, cols] = sums[UNITS, core, rows].astype(f32)
+            for h in range(2):
+                small_wide[h * 128 : (h + 1) * 128, cols] = sums[LAST, h, rows].astype(f32)
+        for one in outputs[2:5]:
+            one.start()
+        block = line_ref[...]
+        for i, one in enumerate((g1, b1, g2, b2)):
+            one[...] = block[i : i + 1]
+        for i in range(4):
+            ub[:, i * 768 : (i + 1) * 768] = block[4 + i : 5 + i]
+        hb[...] = block[8:9, 0:96]
+        count = labels_ref.shape[1]
+        lane = lax.broadcasted_iota(jnp.int32, (1, 128), 1)
+        logdet[...] = jnp.sum(jnp.where(lane == dp, block[8:9, 128:256], 0.0), 1, keepdims=True)
+        by_lane = jnp.broadcast_to(labels_ref[...], (count, count)).astype(f32)
+        first = lax.broadcasted_iota(jnp.int32, (count, count), 0)
+        second = lax.broadcasted_iota(jnp.int32, (count, count), 1)
+        by_row = jnp.sum(jnp.where(first == second, by_lane, 0.0), 1, keepdims=True)
+        before = (by_lane < by_row) | ((by_lane == by_row) & (second < first))
+        rank = jnp.sum(jnp.where(before, 1.0, 0.0), 1, keepdims=True)
+        stored = jnp.sum(jnp.where(rank == second.astype(f32), by_row, 0.0), 0, keepdims=True)
+        wanted = (dp * owned + lax.broadcasted_iota(jnp.int32, (owned, count), 0)).astype(f32)
+        hot = jnp.where(stored == wanted, 1.0, 0.0).astype(bf16)
+        class_wide[...] = jnp.dot(hot, small_wide[144:160].astype(bf16), preferred_element_type=f32)
+        outputs[5].start()
+
+    for one in inputs:
+        one.start()
+    for u in range(UNITS):
+        for h in range(2):
+            wide[u, :, h * COLS : (h + 1) * COLS] = sums[u, h].astype(f32)
+        write(u).start()
+        if u == 1:
+            little()
+    for u in range(UNITS):
+        write(u).wait()
+    for one in outputs:
+        one.wait()
+
+
+def finish(class_labels, sums, lat, line_sums):
     count = class_labels.shape[1]
     owned = 1024 // count
     shapes = [
@@ -1069,21 +1037,25 @@
     ]
     vmem = pl.BlockSpec(memory_space=pltpu.VMEM)
     hbm = pl.BlockSpec(memory_space=pl.ANY)
-    buffers = []
-    for columns, total in ((768, 3840), (2304, 768), (3072, 768)):
-        rows = FINISH_ROWS * 768 // columns
-        for kind in (bf16, f32):
-            buffers.append(pltpu.VMEM((total // rows, rows, columns), kind))
-    pieces = 3840 // FINISH_ROWS + 2304 // FINISH_ROWS + 3072 // FINISH_ROWS
     return pl.pallas_call(
         finish_kernel,
         out_shape=[jax.ShapeDtypeStruct(shape, f32) for shape in shapes],
-        in_specs=[vmem] * 5 + [hbm] * 4,
-        out_specs=[hbm if i in (8, 9, 12, 14) else vmem for i in range(17)],
-        scratch_shapes=buffers + [pltpu.SemaphoreType.DMA((pieces,)), pltpu.SemaphoreType.DMA((pieces,))],
-        compiler_params=pltpu.CompilerParams(vmem_limit_bytes=62 << 20),
+        in_specs=[vmem, vmem] + [pl.BlockSpec(memory_space=pltpu.HBM)] * 2,
+        out_specs=[vmem if i in (1, 6, 7, 10, 11, 13, 16) else hbm for i in range(17)],
+        scratch_shapes=[
+            pltpu.VMEM((UNITS, 384, 768), f32),
+            pltpu.SemaphoreType.DMA((UNITS,)),
+            pltpu.VMEM((2, 128, 128), f32),
+            pltpu.VMEM((16, 768), f32),
+            pltpu.VMEM((128, 768), f32),
+            pltpu.VMEM((256, 768), f32),
+            pltpu.VMEM((owned, 768), f32),
+            pltpu.SemaphoreType.DMA((2,)),
+            pltpu.SemaphoreType.DMA((6,)),
+        ],
+        compiler_params=pltpu.CompilerParams(vmem_limit_bytes=34 << 20),
         name="finish",
-    )(class_labels, pos, small, lat, line_sums, down, up, out, qkv)
+    )(class_labels, sums, lat, line_sums)
 
 
 def fast_local(

time: 158 us -> 146 us (0.924)
  Pallas kernels: 156 us -> 142 us
  local copies, waits for them, and re-layouts: 0 us -> 1.7 us
    pallas_call x1, Pallas kernels: 140 us -> 131 us  [flow(): pl.pallas_call(flow_kernel, out_shape=(pltpu.VMEM((LAST + 1, 2, 3 * SLAB,...]
    pallas_call x1, Pallas kernels: 15.8 us -> 10.9 us  [finish(): pl.pallas_call(finish_kernel, out_shape=[jax.ShapeDtypeStruct(shape, f32)...]
    unnamed x0 -> x6, local copies, waits for them, and re-layouts: none -> 1.7 us
where the time goes in v4:
time: 146 us
  Pallas kernels  142 us (97%)
  between operations  1.99 us (1%)
  local copies, waits for them, and re-layouts  1.7 us (1%)
    pallas_call x1, Pallas kernels, flow(): pl.pallas_call(flow_kernel, out_shape=(pltpu.VMEM((LAST + 1, 2, 3 * SLAB,...  131 us
    pallas_call x1, Pallas kernels, finish(): pl.pallas_call(finish_kernel, out_shape=[jax.ShapeDtypeStruct(shape, f32)...  10.9 us

profile of v4, /device:TPU:0, one launch (start us, length us, event | category | flops | bytes accessed | tf_op | source)
XLA Modules:
  0.0 145.9 jit_solution(13855887400530000444)
XLA Ops:
  2.0 0.0 copy-start.2
  2.0 131.3 %flow.1 = (bf16[26,2,384,384]{3,2,1,0:T(8,128)(2,1)S(1)}, f32[2,128,128]{2,1,0:T(8,128)}, f32[16,768]{1,0:T(8,128)}) custom-call(s32[16]{0:T(128)} %labels_sm.1, s32[1]{0:T(128)S(6)} %copy.37.perm_sm, f32[1]{0:T(128)S(6)} %copy.38.cot_logdet_sm, f32[1,48,128]{2,1,0:T(8,128)} %bitcast.12, s32[1,128]{1,0:T(1,128)} %valid_ref.1, bf16[48,768]{1,0:T(8,128)(2,1)} %patch_ref.1, ...), custom_call_target="tpu_custom_call" | custom-call | tf_op jit(solution)/shard_map/flow/pallas_call | solution.py:864
  133.3 0.0 copy-done.2
  133.3 0.0 copy-start
  133.3 0.9 copy-done
  134.2 0.0 copy-start.1
  134.2 0.8 copy-done.1
  135.0 10.9 %finish.1 = (f32[1,48,128]{2,1,0:T(8,128)}, f32[1,1]{1,0:T(1,128)}, f32[1,48,128]{2,1,0:T(8,128)}, f32[48,768]{1,0:T(8,128)}, f32[128,768]{1,0:T(8,128)}, /*inde...) custom-call(s32[1,16]{1,0:T(1,128)S(1)} %bitcast.10, ...), custom_call_target="tpu_custom_call" | custom-call | tf_op jit(solution)/shard_map/finish/pallas_call | solution.py:1040
Async XLA Ops:
  2.0 131.4 %copy-start.2 = (s32[16]{0:T(128)S(1)}, s32[16]{0:T(128)}, u32[]{:S(2)}) copy-start(s32[16]{0:T(128)} %labels_sm.1) | copy-start | bytes 196
  133.3 0.9 copy-start
  134.2 0.8 copy-start.1

commit v5 on v4

--- a/solution.py
+++ b/solution.py
@@ -66,11 +66,12 @@
 MESH = pl.DeviceIdType.MESH
 UNITS = 24
 LAST = 25
-TURNS = 13
+TURNS = 8
 STEPS = 38
 DRAIN = 14
 SLAB = 128
-TABLE_ROWS = ((0, 384), (384, 384), (768, 256))
+LABELS = 448
+TABLE_ROWS = ((0, 384), (384, 64))
 COLS = 384
 STAGES = 3
 CHUNK = 32
@@ -85,14 +86,14 @@
     latents_ref, valid_ref, patch_ref, pos_table_ref, g1_ref, b1_ref, g2_ref, b2_ref,
     up_bias_ref, head_w_ref, head_b_ref, cot_ref,
     class_hbm, qkv_any, out_any, up_any, down_any,
-    sums, latents_hbm, lines_hbm,
-    stage, part, core_in, small_in, ab_in, c_in, send_sem, recv_sem, stage_sem, back_sem,
+    sums,
+    stage, part, core_in, small_in, ab_in, c_in, shared, send_sem, recv_sem, stage_sem, back_sem,
     qkv_w, out_w, up_w, down_w, load_sem,
     lat_pad, cot_pad, patch_pad, head_pad, hidden, mid, xhat1, xhat2, scale1, scale2,
     keys, values, query, attended, bias, prior_mask, mask_row, probs, slope, d_hidden, d_second, d_att, d_keys, d_values,
-    d_prior, d_back, row_out, row_in, grad_out, grad_in, factor, lat_out,
-    lines, line_sum, line_in, line_send, line_recv, line_sem,
-    lt_ref, r_ref, pos_ref, small_ref, low_top, exch_send, exch_recv, lat_sem,
+    d_prior, d_back, row_out, row_in, peek_out, peek_in, factor,
+    lines, line_sum, line_in, line_send, line_recv,
+    lt_ref, r_ref, pos_ref, small_ref, low_top, exch_send, exch_recv,
 ):
     dp = lax.axis_index("dp")
     core = lax.axis_index("seq")
@@ -111,14 +112,24 @@
 
     sources = [class_hbm.at[r : r + n, h * COLS : (h + 1) * COLS] for h in range(2) for r, n in TABLE_ROWS]
     targets = [part.at[3 * h + i, 0:n] for h in range(2) for i, (r, n) in enumerate(TABLE_ROWS)]
-    sources += [qkv_any.at[0], out_any.at[0], up_any.at[0], down_any.at[0]]
-    targets += [qkv_w, out_w, up_w, down_w]
+    sources += [qkv_any.at[0], out_any.at[0]]
+    targets += [qkv_w, out_w]
 
     def load(i):
         return pltpu.make_async_copy(sources[i], targets[i], load_sem.at[i])
 
-    for i in range(10):
+    def load_feed(j):
+        cols = rows = pl.ds(pl.multiple_of(j * 768, 128), 768)
+        return (
+            pltpu.make_async_copy(up_any.at[0, :, cols], up_w.at[:, cols], load_sem.at[6 + 2 * j]),
+            pltpu.make_async_copy(down_any.at[0, rows], down_w.at[rows], load_sem.at[7 + 2 * j]),
+        )
+
+    for i in range(6):
         load(i).start()
+    for j in range(4):
+        for one in load_feed(j):
+            one.start()
 
     barrier = pltpu.get_barrier_semaphore()
     for target in (to_core, to_x, to_y, to_mate):
@@ -204,7 +215,13 @@
         line_go(k).wait_recv()
         line_sum[k] = line_steps[k][0][...] + line_in[k]
 
-    line_out = pltpu.make_async_copy(line_sum.at[4], lines_hbm, line_sem)
+    def keep_lines():
+        v = line_sum[4]
+        for i in range(3):
+            term = v.astype(bf16)
+            v = v - term.astype(f32)
+            for h in range(2):
+                sums[LAST, h, 256 + i * 16 : 272 + i * 16] = term[:, h * COLS : (h + 1) * COLS]
 
     def produce(u):
         @pl.when(jnp.logical_and(u >= STAGES, u < UNITS))
@@ -323,7 +340,7 @@
         def _():
             line_add(4)
             line_go(5).start()
-            line_out.start()
+            keep_lines()
 
     def ab5_outer(u):
         arrived(u, 3, sums.at[u, core, 0:64])
@@ -333,7 +350,7 @@
         @pl.when(u == LAST)
         def _():
             line_go(5).wait_recv()
-            line_out.start()
+            keep_lines()
 
     def ab6(u):
         arrived(u, 5, sums.at[u, core, 0:64])
@@ -357,7 +374,6 @@
     far = 32 * (1 - side)
     own_end = 96 * side
     shard = z * 32
-    half = shard + x * 16
 
     def c_z1(u):
         return copy(u, 7, part_rows(u, 2, far, 96), c_in.at[u % TURNS, 0:96], to_mate)
@@ -369,14 +385,10 @@
         return copy(u, 7, part_rows(u, 2, own_end, 32), c_in.at[u % TURNS, 160:192], to_mate)
 
     def c_x(u):
-        return copy(u, 9, part_rows(u, 2, shard + (1 - x) * 16, 16), c_in.at[u % TURNS, 192:208], to_x)
+        return copy(u, 9, part_rows(u, 2, shard, 32), c_in.at[u % TURNS, 192:224], to_x)
 
     def c_y(u):
-        return copy(u, 10, part_rows(u, 2, half, 16), c_in.at[u % TURNS, 208:224], to_y)
-
-    def c_back_x(u):
-        block = out_rows(u, 2, half, 16)
-        return copy(u, 11, block, block, to_x)
+        return copy(u, 10, shared.at[u], c_in.at[u % TURNS, 224:256], to_y)
 
     def c_z4(u):
         block = out_rows(u, 2, own_end, 32)
@@ -410,22 +422,18 @@
         c_x(u).start()
 
     def c4(u):
-        arrived(u, 9, c_in.at[u % TURNS, 192:208])
-        kept = part_rows(u, 2, half, 16)
-        added(kept, kept, c_in.at[u % TURNS, 192:208])
+        arrived(u, 9, c_in.at[u % TURNS, 192:224])
+        kept = part_rows(u, 2, shard, 32)
+        part_y = shared.at[u]
+        added(part_y, kept, c_in.at[u % TURNS, 192:224])
         c_y(u).start()
 
     def c5(u):
-        arrived(u, 10, c_in.at[u % TURNS, 208:224])
-        added(out_rows(u, 2, half, 16), part_rows(u, 2, half, 16), c_in.at[u % TURNS, 208:224])
-        c_back_x(u).start()
-
-    def c7_outer(u):
-        arrived(u, 11, out_rows(u, 2, shard + (1 - x) * 16, 16))
-        c_z4(u).start()
+        arrived(u, 10, c_in.at[u % TURNS, 224:256])
+        added(out_rows(u, 2, shard, 32), shared.at[u], c_in.at[u % TURNS, 224:256])
+        pl.when(outer)(lambda: c_z4(u).start())
 
     def c8_inner(u):
-        arrived(u, 11, out_rows(u, 2, shard + (1 - x) * 16, 16))
         arrived(u, 12, out_rows(u, 2, own_end, 32))
         c_z5(u).start()
 
@@ -443,8 +451,8 @@
         copy(u, 0, ref, ref, to_core).wait_send()
 
     def drain(u):
-        pl.when(outer)(lambda: sent(u, 3, 336))
-        pl.when(inner)(lambda: sent(u, 5, 240))
+        pl.when(outer)(lambda: sent(u, 4, 256))
+        pl.when(inner)(lambda: sent(u, 4, 304))
         to_other(u, sums.at[u, 1 - core]).wait_recv()
 
     mm_nt = (((1,), (1,)), ((), ()))
@@ -494,8 +502,11 @@
 
     @pl.when(core == 1)
     def _():
-        grad_in[...] = jnp.zeros((8, 128), f32)
+        peek_in[...] = jnp.zeros((8, 128), f32)
         d_back[...] = jnp.zeros((2, 128, 768), bf16)
+
+    line8 = lax.broadcasted_iota(jnp.int32, (8, 128), 0)
+    peek_out[...] = jnp.where(line8 == 0, lat_pad[0:1], jnp.where(line8 == 1, cot_pad[0:1], valid_row[:, 0:1]))
 
     def normalize(src, hat, scale, gain, shift, put):
         for r in chunks:
@@ -508,8 +519,8 @@
             put(r, scaled * gain + shift)
 
     label = labels_sm[perm_sm[0]]
-    hot = jnp.where(lax.broadcasted_iota(jnp.int32, (16, 1024), 1) == label, 1.0, 0.0).astype(bf16)
-    for i in range(6):
+    hot = jnp.where(lax.broadcasted_iota(jnp.int32, (16, LABELS), 1) == label, 1.0, 0.0).astype(bf16)
+    for i in range(4):
         load(i).wait()
     class_row = jnp.concatenate(
         [
@@ -526,10 +537,14 @@
         low_top[r] = v.astype(bf16)
 
     normalize(hidden, xhat1, scale1, g1_ref[...].astype(f32), b1_ref[...].astype(f32), put_low)
-    load(6).wait()
+    load(4).wait()
     normed = low_top[...]
     keys[128:256] = nn(normed, qkv_w[:, 768:1536]).astype(bf16)
     meet()
+
+    @pl.when(core == 1)
+    def _():
+        exchange(4, peek_out, peek_in).start()
 
     @pl.when(core == 0)
     def _():
@@ -575,19 +590,19 @@
 
     for p in range(6):
         attend(p)
-    load(7).wait()
+    load(5).wait()
     mid[...] = hidden[...] + nn(attended[...], out_w[...])
     lt_ref[5] = attended[...].astype(f32).T.astype(bf16)
     normalize(mid, xhat2, scale2, g2_ref[...].astype(f32), b2_ref[...].astype(f32), put_low)
     lt_ref[4] = low_top[...].astype(f32).T.astype(bf16)
-    load(8).wait()
-    load(9).wait()
     d_hidden[...] = mid[...]
 
     def rows768(j):
         return pl.ds(pl.multiple_of(j * 768, 128), 768)
 
     def feed(j, carried):
+        for one in load_feed(j):
+            one.wait()
         d_second[...] = nn(low_top[...], up_w[:, rows768(j)])
         shift = up_bias_ref[:, rows768(j)].astype(f32)
         for r in chunks:
@@ -610,37 +625,52 @@
     def _():
         exchange(3, row_out.at[120:128], row_in).start()
 
+    def coupling(shifted, latent, cot):
+        inside = lax.broadcasted_iota(jnp.int32, shifted.shape, 1) < 48
+        alpha = jnp.where(inside, shifted, 0.0)
+        scale = jnp.exp(-alpha)
+        moved = (latent - jnp.where(inside, pltpu.roll(shifted, 80, 1), 0.0)) * scale
+        d_alpha = -cot * moved - cot_logdet_sm[0]
+        d_mean = pltpu.roll(jnp.where(inside, -cot * scale, 0.0), 48, 1)
+        return alpha, scale, moved, jnp.where(inside, d_alpha, d_mean)
+
     rolled = pltpu.roll(row_out[...], 1, 0)
-
-    @pl.when(core == 1)
-    def _():
-        exchange(3, row_out.at[120:128], row_in).wait_recv()
-
-    shifted = jnp.where(row == 0, jnp.broadcast_to(row_in[7:8], (128, 128)), rolled) * valid_col
-    inside = lane < 48
-    alpha = jnp.where(inside, shifted, 0.0)
-    shift_mean = jnp.where(inside, pltpu.roll(shifted, 80, 1), 0.0)
-    factor[...] = jnp.exp(-alpha)
-    new_latents = (lat_pad[...] - shift_mean) * factor[...]
-    lat_out[0] = new_latents.T
-    logdet = -jnp.sum(jnp.sum(alpha, 1, keepdims=True), 0, keepdims=True)
-    d_alpha = -cot_pad[...] * new_latents - cot_logdet_sm[0]
-    direct = cot_pad[...] * factor[...]
-    grad_out[...] = (
-        jnp.where(inside, d_alpha, pltpu.roll(jnp.where(inside, -direct, 0.0), 48, 1)) * valid_col
-    )
-
-    @pl.when(core == 1)
-    def _():
-        exchange(4, grad_out.at[0:8], grad_in).start()
-
-    rolled_back = pltpu.roll(grad_out[...], 127, 0)
+    d_shifted = coupling(jnp.where(row == 0, 0.0, rolled) * valid_col, lat_pad[...], cot_pad[...])[3] * valid_col
 
     @pl.when(core == 0)
     def _():
-        exchange(4, grad_out.at[0:8], grad_in).wait_recv()
-
-    d_head = jnp.where(row == 127, jnp.broadcast_to(grad_in[0:1], (128, 128)), rolled_back).astype(bf16)
+        exchange(4, peek_out, peek_in).wait_recv()
+
+    def peeked(i):
+        return jnp.broadcast_to(peek_in[i : i + 1], (8, 128))
+
+    after_last = jnp.broadcast_to(row_out[127:128], (8, 128)) * peeked(2)
+    d_next = coupling(after_last, peeked(0), peeked(1))[3] * peeked(2)
+    d_head = jnp.where(row == 127, d_next[0:1], pltpu.roll(d_shifted, 127, 0)).astype(bf16)
+
+    def outputs():
+        @pl.when(core == 1)
+        def _():
+            exchange(3, row_out.at[120:128], row_in).wait_recv()
+
+        before = jnp.where(row == 0, jnp.broadcast_to(row_in[7:8], (128, 128)), pltpu.roll(row_out[...], 1, 0))
+        alpha, scale, moved = coupling(before * valid_col, lat_pad[...], cot_pad[...])[0:3]
+        factor[...] = scale
+        store_exact(0, moved.T[0:48])
+        logdet = -jnp.sum(jnp.sum(alpha, 1, keepdims=True), 0, keepdims=True)
+        lines[8:9, 128:256] = jnp.where(lax.broadcasted_iota(jnp.int32, (1, 128), 1) == dp, logdet, 0.0)
+
+    def exact_terms(v):
+        terms = []
+        for i in range(3):
+            terms.append(v.astype(bf16))
+            v = v - terms[i].astype(f32)
+        return terms
+
+    def store_exact(h, v):
+        for i, term in enumerate(exact_terms(v)):
+            sums[UNITS, h, 256:304, i * 128 : (i + 1) * 128] = term
+
     head_grad = tn(d_head, low_top[...])
     head_bias_grad = jnp.sum(d_head.astype(f32), 0, keepdims=True)
     d_hidden[...] = nn(d_head, head_pad[...])
@@ -656,9 +686,7 @@
     put(0, head_grad[0:96])
 
     lines[...] = jnp.zeros((16, 768), f32)
-    lane1 = lax.broadcasted_iota(jnp.int32, (1, 128), 1)
     lines[8:9, 0:128] = head_bias_grad
-    lines[8:9, 128:256] = jnp.where(lane1 == dp, logdet, 0.0)
 
     d_second[...] = jnp.zeros((128, 768), f32)
 
@@ -743,16 +771,13 @@
             for h in range(2)
         )
 
-    lat_copy = pltpu.make_async_copy(lat_out, latents_hbm, lat_sem)
-
     def embed_back():
         norm_back(d_second, xhat1, scale1, g1_ref[...].astype(f32), mid, d_hidden, 0)
         low_top[...] = d_hidden[...].astype(bf16)
         for t in range(2):
             pos_ref[t * 128 : (t + 1) * 128] = low_top[:, t * COLS : (t + 1) * COLS]
         patch_grad = tn(lat_pad[...].astype(bf16), low_top[...])
-        lat_out[1] = (cot_pad[...] * factor[...] + nt(low_top[...], patch_pad[...])).T
-        lat_copy.start()
+        store_exact(1, (cot_pad[...] * factor[...] + nt(low_top[...], patch_pad[...])).T[0:48])
         class_grad = jnp.sum(d_hidden[...], 0, keepdims=True)
         put(96, patch_grad[0:32])
         put(128, patch_grad[32:48])
@@ -773,33 +798,33 @@
 
         pl.when(t == 14)(send_prior)
         pl.when(t == 16)(packed_back)
+        pl.when(t == 17)(outputs)
         pl.when(t == 18)(embed_back)
 
     everyone, inners, outers = None, inner, outer
     events = [
         (0, LAST + 1, everyone, produce),
+        (8, LAST + 1, outers, ab5_outer),
+        (11, LAST + 1, outers, ab7),
         (2, UNITS, inners, c1_inner),
         (1, LAST + 1, everyone, begin),
-        (7, UNITS, inners, c5),
         (9, LAST + 1, inners, ab6),
-        (3, UNITS, inners, c2_inner),
         (4, LAST + 1, inners, ab3_inner),
         (0, LAST + 1, everyone, piece),
         (2, LAST + 1, everyone, ab1),
+        (3, UNITS, inners, c2_inner),
         (5, LAST + 1, inners, ab4_inner),
-        (11, LAST + 1, outers, ab7),
+        (8, UNITS, inners, c5),
+        (5, UNITS, outers, c3_outer),
+        (12, LAST + 1, inners, ab7),
+        (8, UNITS, inners, c8_inner),
         (5, UNITS, inners, c4),
-        (8, UNITS, inners, c8_inner),
-        (12, LAST + 1, inners, ab7),
         (9, UNITS, inners, c9_inner),
+        (9, LAST + 1, outers, ab6),
+        (12, UNITS, outers, c10_outer),
         (3, LAST + 1, everyone, ab2),
-        (6, UNITS, outers, c5),
-        (7, UNITS, outers, c7_outer),
-        (4, UNITS, outers, c3_outer),
-        (5, UNITS, outers, c4),
-        (12, UNITS, outers, c10_outer),
-        (7, LAST + 1, outers, ab5_outer),
-        (8, LAST + 1, outers, ab6),
+        (6, UNITS, outers, c4),
+        (7, UNITS, outers, c5),
         (DRAIN, UNITS, everyone, drain),
     ]
 
@@ -828,8 +853,6 @@
     for u in range(UNITS - STAGES, UNITS):
         core_first(u).wait_send()
     small_first().wait_send()
-    lat_copy.wait()
-    line_out.wait()
     for k in range(3):
         line_go(k).wait_send()
     pl.when(outer)(line_go(3).wait_send)
@@ -848,7 +871,7 @@
 
     @pl.when(core == 1)
     def _():
-        exchange(4, grad_out.at[0:8], grad_in).wait_send()
+        exchange(4, peek_out, peek_in).wait_send()
         exchange(5, d_prior, d_back).wait_send()
 
 
@@ -863,20 +886,17 @@
     wide = (128, 768)
     return pl.pallas_call(
         flow_kernel,
-        out_shape=(
-            pltpu.VMEM((LAST + 1, 2, 3 * SLAB, COLS), bf16),
-            jax.ShapeDtypeStruct((2, 128, 128), f32),
-            jax.ShapeDtypeStruct((16, 768), f32),
-        ),
+        out_shape=pltpu.VMEM((LAST + 1, 2, 3 * SLAB, COLS), bf16),
         in_specs=[smem] * 3 + [vmem] * 12 + [hbm] * 5,
-        out_specs=(vmem, hbm, hbm),
+        out_specs=vmem,
         scratch_shapes=[
             pltpu.VMEM((STAGES, 3 * SLAB, COLS), bf16),
             pltpu.VMEM((LAST + 1, 3 * SLAB, COLS), bf16),
             pltpu.VMEM((TURNS, 3 * SLAB, COLS), bf16),
             pltpu.VMEM((256, COLS), bf16),
             pltpu.VMEM((TURNS, 2, 160, COLS), bf16),
-            pltpu.VMEM((TURNS, 224, COLS), bf16),
+            pltpu.VMEM((TURNS, 256, COLS), bf16),
+            pltpu.VMEM((UNITS, 32, COLS), bf16),
             pltpu.SemaphoreType.DMA((LAST + 1,)),
             pltpu.SemaphoreType.DMA((14, TURNS)),
             pltpu.SemaphoreType.DMA((STAGES + 1,)),
@@ -885,7 +905,7 @@
             pltpu.VMEM((768, 768), bf16),
             pltpu.VMEM((768, 3072), bf16),
             pltpu.VMEM((3072, 768), bf16),
-            pltpu.SemaphoreType.DMA((10,)),
+            pltpu.SemaphoreType.DMA((14,)),
             pltpu.VMEM((128, 128), f32),
             pltpu.VMEM((128, 128), f32),
             pltpu.VMEM(wide, bf16),
@@ -914,16 +934,14 @@
             pltpu.VMEM((2, 128, 768), bf16),
             pltpu.VMEM((128, 128), f32),
             pltpu.VMEM((8, 128), f32),
-            pltpu.VMEM((128, 128), f32),
+            pltpu.VMEM((8, 128), f32),
             pltpu.VMEM((8, 128), f32),
             pltpu.VMEM((128, 128), f32),
-            pltpu.VMEM((2, 128, 128), f32),
             pltpu.VMEM((16, 768), f32),
             pltpu.VMEM((5, 16, 768), f32),
             pltpu.VMEM((5, 16, 768), f32),
             pltpu.SemaphoreType.DMA((6,)),
             pltpu.SemaphoreType.DMA((6,)),
-            pltpu.SemaphoreType.DMA,
             pltpu.VMEM((7, 768, 128), bf16),
             pltpu.VMEM((9, 2, 128, COLS), bf16),
             pltpu.VMEM((256, COLS), bf16),
@@ -931,7 +949,6 @@
             pltpu.VMEM(wide, bf16),
             pltpu.SemaphoreType.DMA((6,)),
             pltpu.SemaphoreType.DMA((6,)),
-            pltpu.SemaphoreType.DMA,
         ],
         compiler_params=pltpu.CompilerParams(
             collective_id=0, has_side_effects=True, vmem_limit_bytes=46 << 20
@@ -945,25 +962,19 @@
 
 
 def finish_kernel(
-    labels_ref, sums, lat_hbm, line_hbm,
+    labels_ref, sums,
     new_latents, logdet, latents_grad, patch, pos, classes, g1, b1, qkv, out, g2, b2, up, ub, down, head, hb,
-    wide, write_sem, lat_ref, line_ref, pos_wide, small_wide, class_wide, in_sem, out_sem,
+    wide, write_sem, lat_wide, pos_wide, small_wide, class_wide, out_sem,
 ):
     dp = lax.axis_index("dp")
     core = lax.axis_index("seq")
     owned = classes.shape[0]
-    inputs = [
-        pltpu.make_async_copy(src, dst, in_sem.at[i])
-        for i, (src, dst) in enumerate(
-            ((lat_hbm, lat_ref), (line_hbm, line_ref))
-        )
-    ]
     outputs = [
         pltpu.make_async_copy(src, dst, out_sem.at[i])
         for i, (src, dst) in enumerate(
             (
-                (lat_ref.at[0, 0:48], new_latents.at[0]),
-                (lat_ref.at[1, 0:48], latents_grad.at[0]),
+                (lat_wide.at[0], new_latents.at[0]),
+                (lat_wide.at[1], latents_grad.at[0]),
                 (small_wide.at[0:96], head),
                 (small_wide.at[96:144], patch),
                 (pos_wide, pos),
@@ -981,8 +992,9 @@
         return pltpu.make_async_copy(wide.at[u], dst, write_sem.at[u])
 
     def little():
-        for one in inputs:
-            one.wait()
+        for h in range(2):
+            terms = [sums[UNITS, h, 256:304, i * 128 : (i + 1) * 128].astype(f32) for i in range(3)]
+            lat_wide[h] = terms[0] + terms[1] + terms[2]
         outputs[0].start()
         outputs[1].start()
         for t in range(2):
@@ -992,7 +1004,11 @@
                 small_wide[h * 128 : (h + 1) * 128, cols] = sums[LAST, h, rows].astype(f32)
         for one in outputs[2:5]:
             one.start()
-        block = line_ref[...]
+        halves = []
+        for h in range(2):
+            terms = [sums[LAST, h, 256 + i * 16 : 272 + i * 16].astype(f32) for i in range(3)]
+            halves.append(terms[0] + terms[1] + terms[2])
+        block = jnp.concatenate(halves, 1)
         for i, one in enumerate((g1, b1, g2, b2)):
             one[...] = block[i : i + 1]
         for i in range(4):
@@ -1013,8 +1029,6 @@
         class_wide[...] = jnp.dot(hot, small_wide[144:160].astype(bf16), preferred_element_type=f32)
         outputs[5].start()
 
-    for one in inputs:
-        one.start()
     for u in range(UNITS):
         for h in range(2):
             wide[u, :, h * COLS : (h + 1) * COLS] = sums[u, h].astype(f32)
@@ -1027,7 +1041,7 @@
         one.wait()
 
 
-def finish(class_labels, sums, lat, line_sums):
+def finish(class_labels, sums):
     count = class_labels.shape[1]
     owned = 1024 // count
     shapes = [
@@ -1040,22 +1054,20 @@
     return pl.pallas_call(
         finish_kernel,
         out_shape=[jax.ShapeDtypeStruct(shape, f32) for shape in shapes],
-        in_specs=[vmem, vmem] + [pl.BlockSpec(memory_space=pltpu.HBM)] * 2,
+        in_specs=[vmem, vmem],
         out_specs=[vmem if i in (1, 6, 7, 10, 11, 13, 16) else hbm for i in range(17)],
         scratch_shapes=[
             pltpu.VMEM((UNITS, 384, 768), f32),
             pltpu.SemaphoreType.DMA((UNITS,)),
-            pltpu.VMEM((2, 128, 128), f32),
-            pltpu.VMEM((16, 768), f32),
+            pltpu.VMEM((2, 48, 128), f32),
             pltpu.VMEM((128, 768), f32),
             pltpu.VMEM((256, 768), f32),
             pltpu.VMEM((owned, 768), f32),
-            pltpu.SemaphoreType.DMA((2,)),
             pltpu.SemaphoreType.DMA((6,)),
         ],
         compiler_params=pltpu.CompilerParams(vmem_limit_bytes=34 << 20),
         name="finish",
-    )(class_labels, sums, lat, line_sums)
+    )(class_labels, sums)
 
 
 def fast_local(
@@ -1068,7 +1080,7 @@
         ln1_bias, ln2_gain, ln2_bias, up_bias, head_weight.T, head_bias[None], cot_latents.swapaxes(1, 2), class_table,
         qkv_weight, out_weight, up_weight, down_weight,
     )
-    results = list(finish(class_labels[None], *sums))
+    results = list(finish(class_labels[None], sums))
     results[1] = results[1].reshape(1)
     results[16] = results[16].reshape(96)
     results[0], results[2] = results[0].swapaxes(1, 2), results[2].swapaxes(1, 2)

time: 146 us -> 140 us (0.959)
  Pallas kernels: 142 us -> 138 us
  local copies, waits for them, and re-layouts: 1.7 us -> 0.01 us
    pallas_call x1, Pallas kernels: 131 us -> 127 us  [flow(): pl.pallas_call(flow_kernel, out_shape=pltpu.VMEM((LAST + 1, 2, 3 * SLAB,...]
    unnamed x6 -> x2, local copies, waits for them, and re-layouts: 1.7 us -> 0.01 us
where the time goes in v5:
time: 140 us
  Pallas kernels  138 us (99%)
  between operations  1.98 us (1%)
    pallas_call x1, Pallas kernels, flow(): pl.pallas_call(flow_kernel, out_shape=pltpu.VMEM((LAST + 1, 2, 3 * SLAB,...  127 us
    pallas_call x1, Pallas kernels, finish(): pl.pallas_call(finish_kernel, out_shape=[jax.ShapeDtypeStruct(shape, f32)...  10.7 us

profile of v5, /device:TPU:0, one launch (start us, length us, event | category | flops | bytes accessed | tf_op | source)
XLA Modules:
  0.0 140.1 jit_solution(13474968415049659248)
XLA Ops:
  2.0 0.0 copy-start
  2.0 127.5 %flow.1.sums = bf16[26,2,384,384]{3,2,1,0:T(8,128)(2,1)S(1)} custom-call(s32[16]{0:T(128)} %labels_sm.1, s32[1]{0:T(128)S(6)} %copy.37.perm_sm, f32[1]{0:T(128)S(6)} %copy.38.cot_logdet_sm, f32[1,48,128]{2,1,0:T(8,128)} %bitcast.12, s32[1,128]{1,0:T(1,128)} %valid_ref.1, bf16[48,768]{1,0:T(8,128)(2,1)} %patch_ref.1, bf16[128,768]{1,0:T(8,128)(2,1)} %pos_table_ref.1, ...), custom_call_target="tpu_custom_call" | custom-call | tf_op jit(solution)/shard_map/flow/pallas_call | solution.py:887
  129.4 0.0 copy-done
  129.4 10.7 %finish.1 = (f32[1,48,128]{2,1,0:T(8,128)}, f32[1,1]{1,0:T(1,128)}, f32[1,48,128]{2,1,0:T(8,128)}, f32[48,768]{1,0:T(8,128)}, f32[128,768]{1,0:T(8,128)}, /*inde...) custom-call(s32[1,16]{1,0:T(1,128)S(1)} %bitcast.10, ...), custom_call_target="tpu_custom_call" | custom-call | tf_op jit(solution)/shard_map/finish/pallas_call | solution.py:1054
Async XLA Ops:
  2.0 127.5 %copy-start = (s32[16]{0:T(128)S(1)}, s32[16]{0:T(128)}, u32[]{:S(2)}) copy-start(s32[16]{0:T(128)} %labels_sm.1) | copy-start | bytes 196

commit v6 on v5

--- a/solution.py
+++ b/solution.py
@@ -68,7 +68,7 @@
 LAST = 25
 TURNS = 8
 STEPS = 38
-DRAIN = 14
+DRAIN = 16
 SLAB = 128
 LABELS = 448
 TABLE_ROWS = ((0, 384), (384, 64))
@@ -87,7 +87,8 @@
     up_bias_ref, head_w_ref, head_b_ref, cot_ref,
     class_hbm, qkv_any, out_any, up_any, down_any,
     sums,
-    stage, part, core_in, small_in, ab_in, c_in, shared, send_sem, recv_sem, stage_sem, back_sem,
+    stage, part, core_in, small_in, ab_in, c_in, shared,
+    down_left, down_right, up_left, up_right, bulk_send, bulk_recv, send_sem, recv_sem, stage_sem, back_sem,
     qkv_w, out_w, up_w, down_w, load_sem,
     lat_pad, cot_pad, patch_pad, head_pad, hidden, mid, xhat1, xhat2, scale1, scale2,
     keys, values, query, attended, bias, prior_mask, mask_row, probs, slope, d_hidden, d_second, d_att, d_keys, d_values,
@@ -105,6 +106,8 @@
     to_x = (dp + 1 - 2 * x, core)
     to_y = (dp + 2 - 4 * y, core)
     to_mate = (dp + 4 - 8 * (z % 2), core)
+    to_x_other = (dp + 1 - 2 * x, 1 - core)
+    to_y_other = (dp + 2 - 4 * y, 1 - core)
     to_inner = ((dp + 12 - 8 * z + 16) % 16, core)
 
     def rows_at(start, count):
@@ -132,7 +135,7 @@
             one.start()
 
     barrier = pltpu.get_barrier_semaphore()
-    for target in (to_core, to_x, to_y, to_mate):
+    for target in (to_core, to_x, to_y, to_mate, to_x_other, to_y_other):
         pl.semaphore_signal(barrier, inc=1, device_id=target, device_id_type=MESH)
 
     @pl.when(inner)
@@ -142,11 +145,11 @@
     def meet():
         @pl.when(inner)
         def _():
-            pl.semaphore_wait(barrier, 5)
+            pl.semaphore_wait(barrier, 7)
 
         @pl.when(outer)
         def _():
-            pl.semaphore_wait(barrier, 4)
+            pl.semaphore_wait(barrier, 6)
 
     def copy(u, k, src, dst, target):
         return pltpu.make_async_remote_copy(
@@ -171,15 +174,75 @@
     def part_rows(u, t, start, count):
         return part.at[u, rows_at(t * SLAB + start, count)]
 
-    def left_index(u):
-        return jnp.minimum(u // 2, 4) + jnp.minimum(jnp.maximum(u // 2 - 7, 0), 2)
-
-    def right_index(u):
-        return jnp.maximum(u // 2 - 3, 0)
-
-    def product(u, t, half):
-        rows = pl.ds(pl.multiple_of((u % 2) * 384 + t * SLAB, 128), SLAB)
-        return jnp.dot(lt_ref[left_index(u), rows], r_ref[right_index(u), half], preferred_element_type=f32)
+    def bulk(k, src, dst, target):
+        return pltpu.make_async_remote_copy(
+            src_ref=src, dst_ref=dst, send_sem=bulk_send.at[k], recv_sem=bulk_recv.at[k],
+            device_id=target, device_id_type=MESH,
+        )
+
+    def down_rows(i):
+        return pl.ds(pl.multiple_of(i * 768, 128), 768)
+
+    def down_left_core(i):
+        return bulk(i, down_left.at[down_rows(i), 0:128], down_left.at[down_rows(i), 128:256], to_core)
+
+    def down_left_x(i):
+        return bulk(2 + i, lt_ref.at[i], down_left.at[down_rows(i), 256:384], to_x)
+
+    def down_left_on(i):
+        return bulk(4 + i, down_left.at[down_rows(i), 256:384], down_left.at[down_rows(i), 384:512], to_core)
+
+    def down_right_go(i):
+        half, target = ((1 - core, to_core), (core, to_x), (1 - core, to_x_other))[i]
+        return bulk(6 + i, r_ref.at[0, half], down_right.at[128 * (i + 1) : 128 * (i + 2)], target)
+
+    def up_left_go(i):
+        first_lane, target = ((0, to_core), (0, to_y), (256, to_core))[i]
+        return bulk(
+            9 + i,
+            up_left.at[:, first_lane : first_lane + 128],
+            up_left.at[:, 128 * (i + 1) : 128 * (i + 2)],
+            target,
+        )
+
+    def up_right_go(i, j):
+        target = (to_core, to_y, to_y_other)[i]
+        return bulk(12 + i, r_ref.at[1 + j], up_right.at[:, 128 * (i + 1) : 128 * (i + 2)], target)
+
+    def pass_on(i):
+        down_left_x(i).wait_recv()
+        down_left_on(i).start()
+
+    def begin_ab(u):
+        @pl.when(u == 0)
+        def _():
+            for i in range(3):
+                down_right_go(i).wait_recv()
+                up_right_go(i, 0).wait_recv()
+            up_left_go(0).wait_recv()
+            up_left_go(2).wait_recv()
+            down_left_core(0).wait_recv()
+            down_left_on(0).wait_recv()
+
+        @pl.when(u == 12)
+        def _():
+            down_left_core(1).wait_recv()
+            down_left_on(1).wait_recv()
+
+        @pl.when(u < UNITS)
+        def _():
+            rows = pl.ds(pl.multiple_of(u * 64, 64), 64)
+            kept = part_rows(u, 0, x * 64, 64)
+            kept[...] = jnp.dot(down_left[rows], down_right[...], preferred_element_type=f32).astype(bf16)
+            ab_second(u, 0).start()
+            rows = pl.ds(pl.multiple_of((u // 2) * 64, 64), 64)
+            kept = part_rows(u, 1, y * 64, 64)
+            kept[...] = jnp.dot(up_left[rows], up_right[u % 2], preferred_element_type=f32).astype(bf16)
+            ab_second(u, 1).start()
+
+    def product(u, half):
+        block, rows = u // 6, pl.ds(pl.multiple_of((u % 6) * SLAB, 128), SLAB)
+        return jnp.dot(lt_ref[5 + jnp.minimum(block, 1), rows], r_ref[5 + block, half], preferred_element_type=f32)
 
     def core_first(u):
         return pltpu.make_async_remote_copy(
@@ -224,37 +287,23 @@
                 sums[LAST, h, 256 + i * 16 : 272 + i * 16] = term[:, h * COLS : (h + 1) * COLS]
 
     def produce(u):
-        @pl.when(jnp.logical_and(u >= STAGES, u < UNITS))
-        def _():
-            core_first(u - STAGES).wait_send()
-
-        @pl.when(u < UNITS)
-        def _():
-            for t in range(3):
-                stage[u % STAGES, t * SLAB : (t + 1) * SLAB] = product(u, t, 1 - core).astype(bf16)
-            core_first(u).start()
-
-        @pl.when(u == LAST)
-        def _():
-            small_first().start()
-            line_go(0).start()
+        pl.when(u >= STAGES)(lambda: core_first(u - STAGES).wait_send())
+        stage[u % STAGES] = product(u, 1 - core).astype(bf16)
+        core_first(u).start()
 
     def begin(u):
-        @pl.when(u < UNITS)
-        def _():
-            arrived(u, 0, core_in.at[u % TURNS])
-            for t in range(3):
-                rows = slice(t * SLAB, (t + 1) * SLAB)
-                part[u, rows] = (product(u, t, core) + core_in[u % TURNS, rows].astype(f32)).astype(bf16)
-                if t < 2:
-                    ab_first(u, t).start()
-            pl.when(outer)(lambda: c_z1(u).start())
-
+        arrived(u, 0, core_in.at[u % TURNS])
+        part[u, 2 * SLAB :] = (product(u, core) + core_in[u % TURNS].astype(f32)).astype(bf16)
+        pl.when(outer)(lambda: c_z1(u).start())
+
+    def begin_more(u):
         @pl.when(u == UNITS)
         def _():
             part[UNITS, 0:256] = pos_ref[...]
             for t in range(2):
                 ab_first(u, t).start()
+            small_first().start()
+            line_go(0).start()
 
         @pl.when(u == LAST)
         def _():
@@ -294,6 +343,9 @@
         return copy(u, 6, block, block, to_first[t])
 
     def ab1(u):
+        pl.when(u >= UNITS)(lambda: ab1_more(u))
+
+    def ab1_more(u):
         arrived(u, 1, ab_in.at[u % TURNS, :, 0:64])
         for t in range(2):
             kept = part_rows(u, t, first[t] * 64, 64)
@@ -451,8 +503,8 @@
         copy(u, 0, ref, ref, to_core).wait_send()
 
     def drain(u):
-        pl.when(outer)(lambda: sent(u, 4, 256))
-        pl.when(inner)(lambda: sent(u, 4, 304))
+        pl.when(outer)(lambda: sent(u, 4, 224))
+        pl.when(inner)(lambda: sent(u, 4, 272))
         to_other(u, sums.at[u, 1 - core]).wait_recv()
 
     mm_nt = (((1,), (1,)), ((), ()))
@@ -594,7 +646,9 @@
     mid[...] = hidden[...] + nn(attended[...], out_w[...])
     lt_ref[5] = attended[...].astype(f32).T.astype(bf16)
     normalize(mid, xhat2, scale2, g2_ref[...].astype(f32), b2_ref[...].astype(f32), put_low)
-    lt_ref[4] = low_top[...].astype(f32).T.astype(bf16)
+    up_left[:, 0:128] = low_top[...].astype(f32).T.astype(bf16)
+    for i in range(2):
+        up_left_go(i).start()
     d_hidden[...] = mid[...]
 
     def rows768(j):
@@ -613,7 +667,18 @@
             slope[j, r] = left + 0.5 * pre * (1.0 - bend * bend) * (GELU_A + (3.0 * GELU_A * GELU_B) * square)
             d_second[r] = pre * left
         act = d_second[...]
-        lt_ref[j] = act.T.astype(bf16)
+        turned = act.T.astype(bf16)
+
+        @pl.when(j // 2 == x)
+        def _():
+            down_left[down_rows(j % 2), 0:128] = turned
+            down_left_core(j % 2).start()
+
+        @pl.when(j // 2 != x)
+        def _():
+            lt_ref[j % 2] = turned
+            pl.when(j % 2 == 0)(lambda: down_left_x(0).start())
+
         d_hidden[...] += nn(act.astype(bf16), down_w[rows768(j)])
         return carried
 
@@ -677,6 +742,10 @@
     low_top[...] = d_hidden[...].astype(bf16)
     for h in range(2):
         r_ref[0, h] = low_top[:, h * COLS : (h + 1) * COLS]
+    for i in range(3):
+        down_right_go(i).start()
+    down_left_x(1).start()
+    down_right[0:128] = r_ref[0, core]
 
     def put(first_row, value):
         h, r = first_row // 128, first_row % 128
@@ -699,6 +768,16 @@
             total += jnp.sum(d_pre.astype(f32), 0, keepdims=True)
             for h in range(2):
                 r_ref[1 + j, h, r] = d_pre[:, h * COLS : (h + 1) * COLS]
+        near, same = j // 2 == y, j % 2 == core
+
+        @pl.when(jnp.logical_and(near, same))
+        def _():
+            for h in range(2):
+                up_right[h, 0:128] = r_ref[1 + j, h]
+
+        pl.when(jnp.logical_and(near, j % 2 != core))(lambda: up_right_go(0, j).start())
+        pl.when(jnp.logical_and(j // 2 != y, same))(lambda: up_right_go(1, j).start())
+        pl.when(jnp.logical_and(j // 2 != y, j % 2 != core))(lambda: up_right_go(2, j).start())
         lines[pl.ds(4 + j, 1)] = total
         d_second[...] += nt(d_att[...], up_w[:, rows768(j)])
 
@@ -785,46 +864,54 @@
         put(144, jnp.where(line == dp, class_grad, 0.0))
         put(160, jnp.zeros((96, 768), f32))
 
+    def feed_back_all(j, carried):
+        feed_back((j + 2 * (1 - y)) % 4)
+        return carried
+
+    lax.fori_loop(0, 4, feed_back_all, 0)
+    pass_on(0)
+    up_left_go(1).wait_recv()
+    up_left_go(2).start()
+    feed_norm_back()
+
     def piece(t):
-        @pl.when(jnp.logical_and(t < 8, t % 2 == 0))
-        def _():
-            feed_back(t // 2)
-
-        pl.when(t == 8)(feed_norm_back)
-
-        @pl.when(jnp.logical_and(t >= 9, t < 15))
-        def _():
-            attend_back(t - 9)
-
-        pl.when(t == 14)(send_prior)
-        pl.when(t == 16)(packed_back)
-        pl.when(t == 17)(outputs)
-        pl.when(t == 18)(embed_back)
+        @pl.when(jnp.logical_and(t >= 2, t < 5))
+        def _():
+            attend_back(2 * t - 4)
+            attend_back(2 * t - 3)
+
+        pl.when(t == 5)(lambda: pass_on(1))
+        pl.when(t == 4)(send_prior)
+        pl.when(t == 6)(packed_back)
+        pl.when(t == 7)(outputs)
+        pl.when(t == 8)(embed_back)
 
     everyone, inners, outers = None, inner, outer
     events = [
-        (0, LAST + 1, everyone, produce),
+        (10, LAST + 1, inners, ab7),
+        (11, UNITS, inners, c9_inner),
+        (2, UNITS, everyone, produce),
+        (4, UNITS, inners, c1_inner),
+        (8, LAST + 1, inners, ab6),
+        (7, UNITS, outers, c3_outer),
+        (8, UNITS, outers, c4),
+        (9, UNITS, inners, c5),
+        (9, UNITS, outers, c5),
+        (3, UNITS, everyone, begin),
+        (1, LAST + 1, everyone, begin_more),
+        (7, UNITS, inners, c4),
+        (5, UNITS, inners, c2_inner),
+        (14, UNITS, outers, c10_outer),
+        (0, LAST + 1, everyone, piece),
+        (12, LAST + 1, outers, ab7),
+        (5, LAST + 1, inners, ab3_inner),
+        (3, LAST + 1, everyone, begin_ab),
+        (3, LAST + 1, everyone, ab1),
+        (6, LAST + 1, inners, ab4_inner),
         (8, LAST + 1, outers, ab5_outer),
-        (11, LAST + 1, outers, ab7),
-        (2, UNITS, inners, c1_inner),
-        (1, LAST + 1, everyone, begin),
-        (9, LAST + 1, inners, ab6),
-        (4, LAST + 1, inners, ab3_inner),
-        (0, LAST + 1, everyone, piece),
-        (2, LAST + 1, everyone, ab1),
-        (3, UNITS, inners, c2_inner),
-        (5, LAST + 1, inners, ab4_inner),
-        (8, UNITS, inners, c5),
-        (5, UNITS, outers, c3_outer),
-        (12, LAST + 1, inners, ab7),
-        (8, UNITS, inners, c8_inner),
-        (5, UNITS, inners, c4),
-        (9, UNITS, inners, c9_inner),
         (9, LAST + 1, outers, ab6),
-        (12, UNITS, outers, c10_outer),
-        (3, LAST + 1, everyone, ab2),
-        (6, UNITS, outers, c4),
-        (7, UNITS, outers, c5),
+        (9, UNITS, inners, c8_inner),
+        (4, LAST + 1, everyone, ab2),
         (DRAIN, UNITS, everyone, drain),
     ]
 
@@ -837,7 +924,7 @@
             pl.when(now)(lambda event=event, u=u: event(u))
         return carried
 
-    lax.fori_loop(0, STEPS, step, 0)
+    lax.fori_loop(2, STEPS, step, 0)
 
 
     def drain_more(u, carried):
@@ -855,6 +942,13 @@
     small_first().wait_send()
     for k in range(3):
         line_go(k).wait_send()
+        down_right_go(k).wait_send()
+        up_left_go(k).wait_send()
+        up_right_go(k, 0).wait_send()
+    for i in range(2):
+        down_left_core(i).wait_send()
+        down_left_x(i).wait_send()
+        down_left_on(i).wait_send()
     pl.when(outer)(line_go(3).wait_send)
 
     @pl.when(inner)
@@ -890,13 +984,19 @@
         in_specs=[smem] * 3 + [vmem] * 12 + [hbm] * 5,
         out_specs=vmem,
         scratch_shapes=[
-            pltpu.VMEM((STAGES, 3 * SLAB, COLS), bf16),
+            pltpu.VMEM((STAGES, SLAB, COLS), bf16),
             pltpu.VMEM((LAST + 1, 3 * SLAB, COLS), bf16),
-            pltpu.VMEM((TURNS, 3 * SLAB, COLS), bf16),
+            pltpu.VMEM((TURNS, SLAB, COLS), bf16),
             pltpu.VMEM((256, COLS), bf16),
             pltpu.VMEM((TURNS, 2, 160, COLS), bf16),
             pltpu.VMEM((TURNS, 256, COLS), bf16),
             pltpu.VMEM((UNITS, 32, COLS), bf16),
+            pltpu.VMEM((1536, 512), bf16),
+            pltpu.VMEM((512, COLS), bf16),
+            pltpu.VMEM((768, 512), bf16),
+            pltpu.VMEM((2, 512, COLS), bf16),
+            pltpu.SemaphoreType.DMA((15,)),
+            pltpu.SemaphoreType.DMA((15,)),
             pltpu.SemaphoreType.DMA((LAST + 1,)),
             pltpu.SemaphoreType.DMA((14, TURNS)),
             pltpu.SemaphoreType.DMA((STAGES + 1,)),
@@ -964,7 +1064,7 @@
 def finish_kernel(
     labels_ref, sums,
     new_latents, logdet, latents_grad, patch, pos, classes, g1, b1, qkv, out, g2, b2, up, ub, down, head, hb,
-    wide, write_sem, lat_wide, pos_wide, small_wide, class_wide, out_sem,
+    wide_down, wide_up, wide_last, write_sem, lat_wide, pos_wide, small_wide, class_wide, out_sem,
 ):
     dp = lax.axis_index("dp")
     core = lax.axis_index("seq")
@@ -982,14 +1082,11 @@
             )
         )
     ]
-    def write(u):
-        block, row = u // 2, (u % 2) * 384
-        if block < 4:
-            dst = down.at[0, block * 768 + row : block * 768 + row + 384]
-        else:
-            target, column = (up, block - 4) if block < 8 else (out, 0) if block == 8 else (qkv, block - 9)
-            dst = target.at[0, row : row + 384, column * 768 : (column + 1) * 768]
-        return pltpu.make_async_copy(wide.at[u], dst, write_sem.at[u])
+    writes = []
+
+    def write(src, dst):
+        writes.append(pltpu.make_async_copy(src, dst, write_sem.at[len(writes)]))
+        writes[-1].start()
 
     def little():
         for h in range(2):
@@ -1030,13 +1127,30 @@
         outputs[5].start()
 
     for u in range(UNITS):
+        block, row, turn = u // 6, (u % 6) * SLAB, 64 * (u // 2)
         for h in range(2):
-            wide[u, :, h * COLS : (h + 1) * COLS] = sums[u, h].astype(f32)
-        write(u).start()
-        if u == 1:
+            cols = slice(h * COLS, (h + 1) * COLS)
+            for i in range(2):
+                wide_down[1536 * i + 64 * u : 1536 * i + 64 * (u + 1), cols] = sums[
+                    u, h, 64 * i : 64 * (i + 1)
+                ].astype(f32)
+                column = (2 * i + h) * 768 + (u % 2) * COLS
+                wide_up[turn : turn + 64, column : column + COLS] = sums[
+                    u, h, 128 + 64 * i : 128 + 64 * (i + 1)
+                ].astype(f32)
+            wide_last[block, row : row + SLAB, cols] = sums[u, h, 2 * SLAB :].astype(f32)
+        target, column = (out, 0) if block == 0 else (qkv, (block - 1) * 768)
+        write(wide_last.at[block, row : row + SLAB], target.at[0, row : row + SLAB, column : column + 768])
+        if u % 2 == 1:
+            write(wide_up.at[turn : turn + 64], up.at[0, turn : turn + 64])
+        if u % 4 == 3:
+            for i in range(2):
+                rows = slice(1536 * i + 64 * (u - 3), 1536 * i + 64 * (u + 1))
+                write(wide_down.at[rows], down.at[0, rows])
+        if u == 3:
             little()
-    for u in range(UNITS):
-        write(u).wait()
+    for one in writes:
+        one.wait()
     for one in outputs:
         one.wait()
 
@@ -1057,8 +1171,10 @@
         in_specs=[vmem, vmem],
         out_specs=[vmem if i in (1, 6, 7, 10, 11, 13, 16) else hbm for i in range(17)],
         scratch_shapes=[
-            pltpu.VMEM((UNITS, 384, 768), f32),
-            pltpu.SemaphoreType.DMA((UNITS,)),
+            pltpu.VMEM((3072, 768), f32),
+            pltpu.VMEM((768, 3072), f32),
+            pltpu.VMEM((4, 768, 768), f32),
+            pltpu.SemaphoreType.DMA((48,)),
             pltpu.VMEM((2, 48, 128), f32),
             pltpu.VMEM((128, 768), f32),
             pltpu.VMEM((256, 768), f32),

time: 140 us -> 138 us (0.986)
  Pallas kernels: 138 us -> 136 us
    pallas_call x1, Pallas kernels: 127 us -> 125 us  [flow(): pl.pallas_call(flow_kernel, out_shape=pltpu.VMEM((LAST + 1, 2, 3 * SLAB,...]
where the time goes in v6:
time: 138 us
  Pallas kernels  136 us (99%)
  between operations  1.98 us (1%)
    pallas_call x1, Pallas kernels, flow(): pl.pallas_call(flow_kernel, out_shape=pltpu.VMEM((LAST + 1, 2, 3 * SLAB,...  125 us
    pallas_call x1, Pallas kernels, finish(): pl.pallas_call(finish_kernel, out_shape=[jax.ShapeDtypeStruct(shape, f32)...  10.9 us

profile of v6, /device:TPU:0, one launch (start us, length us, event | category | flops | bytes accessed | tf_op | source)
XLA Modules:
  0.0 138.2 jit_solution(4341697539057458487)
XLA Ops:
  2.0 0.0 copy-start
  2.0 125.4 %flow.1.sums = bf16[26,2,384,384]{3,2,1,0:T(8,128)(2,1)S(1)} custom-call(s32[16]{0:T(128)} %labels_sm.1, s32[1]{0:T(128)S(6)} %copy.37.perm_sm, f32[1]{0:T(128)S(6)} %copy.38.cot_logdet_sm, f32[1,48,128]{2,1,0:T(8,128)} %bitcast.12, s32[1,128]{1,0:T(1,128)} %valid_ref.1, bf16[48,768]{1,0:T(8,128)(2,1)} %patch_ref.1, bf16[128,768]{1,0:T(8,128)(2,1)} %pos_table_ref.1, ...), custom_call_target="tpu_custom_call" | custom-call | tf_op jit(solution)/shard_map/flow/pallas_call | solution.py:981
  127.3 0.0 copy-done
  127.4 10.9 %finish.1 = (f32[1,48,128]{2,1,0:T(8,128)}, f32[1,1]{1,0:T(1,128)}, f32[1,48,128]{2,1,0:T(8,128)}, f32[48,768]{1,0:T(8,128)}, f32[128,768]{1,0:T(8,128)}, /*inde...) custom-call(s32[1,16]{1,0:T(1,128)S(1)} %bitcast.10, ...), custom_call_target="tpu_custom_call" | custom-call | tf_op jit(solution)/shard_map/finish/pallas_call | solution.py:1168
Async XLA Ops:
  2.0 125.4 %copy-start = (s32[16]{0:T(128)S(1)}, s32[16]{0:T(128)}, u32[]{:S(2)}) copy-start(s32[16]{0:T(128)} %labels_sm.1) | copy-start | bytes 196

commit v7 on v6

--- a/solution.py
+++ b/solution.py
@@ -64,14 +64,17 @@
 
 
 MESH = pl.DeviceIdType.MESH
-UNITS = 24
-LAST = 25
+OUTS = 3
+UNITS = 27
+LAST = 28
+THIRD = 18
 TURNS = 8
-STEPS = 38
-DRAIN = 16
+STEPS = 44
+DRAIN = 17
+DRAIN_C = 18
 SLAB = 128
 LABELS = 448
-TABLE_ROWS = ((0, 384), (384, 64))
+TABLE_ROWS = ((0, 256), (256, 192))
 COLS = 384
 STAGES = 3
 CHUNK = 32
@@ -87,8 +90,8 @@
     up_bias_ref, head_w_ref, head_b_ref, cot_ref,
     class_hbm, qkv_any, out_any, up_any, down_any,
     sums,
-    stage, part, core_in, small_in, ab_in, c_in, shared,
-    down_left, down_right, up_left, up_right, bulk_send, bulk_recv, send_sem, recv_sem, stage_sem, back_sem,
+    stage, part, part_c, out_stage, out_in, core_in, small_in, ab_in, c_in, shared,
+    down_left, down_right, up_left, up_right, bulk_send, bulk_recv, send_sem, recv_sem, stage_sem, back_sem, send_c, back_c, out_send, out_recv,
     qkv_w, out_w, up_w, down_w, load_sem,
     lat_pad, cot_pad, patch_pad, head_pad, hidden, mid, xhat1, xhat2, scale1, scale2,
     keys, values, query, attended, bias, prior_mask, mask_row, probs, slope, d_hidden, d_second, d_att, d_keys, d_values,
@@ -157,8 +160,17 @@
             device_id=target, device_id_type=MESH,
         )
 
+    def copy_c(u, k, src, dst, target):
+        return pltpu.make_async_remote_copy(
+            src_ref=src, dst_ref=dst, send_sem=send_c.at[u], recv_sem=recv_sem.at[k, u % TURNS],
+            device_id=target, device_id_type=MESH,
+        )
+
     def arrived(u, k, dst):
-        copy(u, k, dst, dst, to_core).wait_recv()
+        pltpu.make_async_remote_copy(
+            src_ref=dst, dst_ref=dst, send_sem=send_sem.at[0], recv_sem=recv_sem.at[k, u % TURNS],
+            device_id=to_core, device_id_type=MESH,
+        ).wait_recv()
 
     def added(dst, left, right):
         dst[...] = (left[...].astype(f32) + right[...].astype(f32)).astype(bf16)
@@ -169,10 +181,13 @@
     to_second = (to_y, to_x)
 
     def out_rows(u, t, start, count):
-        return sums.at[u, core, rows_at(t * SLAB + start, count)]
+        return third_rows(u, core, start, count) if t == 2 else sums.at[u, core, rows_at(t * SLAB + start, count)]
+
+    def third_rows(u, h, start, count):
+        return sums.at[LAST + 1 + u // 2, h, rows_at((u % 2) * SLAB + start, count)]
 
     def part_rows(u, t, start, count):
-        return part.at[u, rows_at(t * SLAB + start, count)]
+        return part_c.at[u, rows_at(start, count)] if t == 2 else part.at[u, rows_at(t * SLAB + start, count)]
 
     def bulk(k, src, dst, target):
         return pltpu.make_async_remote_copy(
@@ -213,7 +228,9 @@
         down_left_x(i).wait_recv()
         down_left_on(i).start()
 
-    def begin_ab(u):
+    def begin_ab(unit):
+        u = unit - OUTS
+
         @pl.when(u == 0)
         def _():
             for i in range(3):
@@ -229,20 +246,30 @@
             down_left_core(1).wait_recv()
             down_left_on(1).wait_recv()
 
-        @pl.when(u < UNITS)
+        @pl.when(jnp.logical_and(u >= 0, unit < UNITS))
         def _():
             rows = pl.ds(pl.multiple_of(u * 64, 64), 64)
-            kept = part_rows(u, 0, x * 64, 64)
+            kept = part_rows(unit, 0, x * 64, 64)
             kept[...] = jnp.dot(down_left[rows], down_right[...], preferred_element_type=f32).astype(bf16)
-            ab_second(u, 0).start()
+            ab_second(unit, 0).start()
             rows = pl.ds(pl.multiple_of((u // 2) * 64, 64), 64)
-            kept = part_rows(u, 1, y * 64, 64)
+            kept = part_rows(unit, 1, y * 64, 64)
             kept[...] = jnp.dot(up_left[rows], up_right[u % 2], preferred_element_type=f32).astype(bf16)
-            ab_second(u, 1).start()
+            ab_second(unit, 1).start()
 
     def product(u, half):
-        block, rows = u // 6, pl.ds(pl.multiple_of((u % 6) * SLAB, 128), SLAB)
-        return jnp.dot(lt_ref[5 + jnp.minimum(block, 1), rows], r_ref[5 + block, half], preferred_element_type=f32)
+        rows = pl.ds(pl.multiple_of((u % 6) * SLAB, 128), SLAB)
+        return jnp.dot(lt_ref[6, rows], r_ref[6 + u // 6, half], preferred_element_type=f32)
+
+    def out_product(u, half):
+        rows = pl.ds(pl.multiple_of(u * 256, 256), 256)
+        return jnp.dot(lt_ref[5, rows], r_ref[5, half], preferred_element_type=f32)
+
+    def out_first(u):
+        return pltpu.make_async_remote_copy(
+            src_ref=out_stage.at[u], dst_ref=out_in.at[u], send_sem=out_send.at[u], recv_sem=out_recv.at[u],
+            device_id=to_core, device_id_type=MESH,
+        )
 
     def core_first(u):
         return pltpu.make_async_remote_copy(
@@ -284,7 +311,7 @@
             term = v.astype(bf16)
             v = v - term.astype(f32)
             for h in range(2):
-                sums[LAST, h, 256 + i * 16 : 272 + i * 16] = term[:, h * COLS : (h + 1) * COLS]
+                sums[LAST + 1 + THIRD // 2, h, 64 + i * 16 : 80 + i * 16] = term[:, h * COLS : (h + 1) * COLS]
 
     def produce(u):
         pl.when(u >= STAGES)(lambda: core_first(u - STAGES).wait_send())
@@ -293,13 +320,20 @@
 
     def begin(u):
         arrived(u, 0, core_in.at[u % TURNS])
-        part[u, 2 * SLAB :] = (product(u, core) + core_in[u % TURNS].astype(f32)).astype(bf16)
+        part_c[u] = (product(u, core) + core_in[u % TURNS].astype(f32)).astype(bf16)
         pl.when(outer)(lambda: c_z1(u).start())
 
     def begin_more(u):
+        @pl.when(u < OUTS)
+        def _():
+            out_first(u).wait_recv()
+            part[u] = (out_product(u, core) + out_in[u].astype(f32)).astype(bf16)
+            for t in range(2):
+                ab_first(u, t).start()
+
         @pl.when(u == UNITS)
         def _():
-            part[UNITS, 0:256] = pos_ref[...]
+            part[UNITS] = pos_ref[...]
             for t in range(2):
                 ab_first(u, t).start()
             small_first().start()
@@ -308,7 +342,7 @@
         @pl.when(u == LAST)
         def _():
             small_first().wait_recv()
-            part[LAST, 0:256] = (small_ref[core].astype(f32) + small_in[...].astype(f32)).astype(bf16)
+            part[LAST] = (small_ref[core].astype(f32) + small_in[...].astype(f32)).astype(bf16)
             for t in range(2):
                 ab_first(u, t).start()
             line_add(0)
@@ -343,7 +377,7 @@
         return copy(u, 6, block, block, to_first[t])
 
     def ab1(u):
-        pl.when(u >= UNITS)(lambda: ab1_more(u))
+        pl.when(jnp.logical_or(u < OUTS, u >= UNITS))(lambda: ab1_more(u))
 
     def ab1_more(u):
         arrived(u, 1, ab_in.at[u % TURNS, :, 0:64])
@@ -409,50 +443,53 @@
         for t in range(2):
             ab_back1(u, t).start()
 
-    def spread(u, row, count):
-        block = sums.at[u, core, row : row + count]
-        to_other(u, block).start()
-
     def to_other(u, block):
         return pltpu.make_async_remote_copy(
             src_ref=block, dst_ref=block, send_sem=send_sem.at[u], recv_sem=back_sem.at[u],
             device_id=to_core, device_id_type=MESH,
         )
 
+    def to_other_c(u, half):
+        block = third_rows(u, half, 0, SLAB)
+        return pltpu.make_async_remote_copy(
+            src_ref=block, dst_ref=block, send_sem=send_c.at[u], recv_sem=back_c.at[u],
+            device_id=to_core, device_id_type=MESH,
+        )
+
     def ab7(u):
         arrived(u, 6, sums.at[u, core, 0:128])
-        pl.when(u != UNITS)(lambda: spread(u, 0, 2 * SLAB))
+        pl.when(u != UNITS)(lambda: to_other(u, sums.at[u, core]).start())
 
     far = 32 * (1 - side)
     own_end = 96 * side
     shard = z * 32
 
     def c_z1(u):
-        return copy(u, 7, part_rows(u, 2, far, 96), c_in.at[u % TURNS, 0:96], to_mate)
+        return copy_c(u, 7, part_rows(u, 2, far, 96), c_in.at[u % TURNS, 0:96], to_mate)
 
     def c_z2(u):
-        return copy(u, 8, part_rows(u, 2, (1 - side) * 64, 64), c_in.at[u % TURNS, 96:160], to_inner)
+        return copy_c(u, 8, part_rows(u, 2, (1 - side) * 64, 64), c_in.at[u % TURNS, 96:160], to_inner)
 
     def c_z3(u):
-        return copy(u, 7, part_rows(u, 2, own_end, 32), c_in.at[u % TURNS, 160:192], to_mate)
+        return copy_c(u, 7, part_rows(u, 2, own_end, 32), c_in.at[u % TURNS, 160:192], to_mate)
 
     def c_x(u):
-        return copy(u, 9, part_rows(u, 2, shard, 32), c_in.at[u % TURNS, 192:224], to_x)
+        return copy_c(u, 9, part_rows(u, 2, shard, 32), c_in.at[u % TURNS, 192:224], to_x)
 
     def c_y(u):
-        return copy(u, 10, shared.at[u], c_in.at[u % TURNS, 224:256], to_y)
+        return copy_c(u, 10, shared.at[u], c_in.at[u % TURNS, 224:256], to_y)
 
     def c_z4(u):
         block = out_rows(u, 2, own_end, 32)
-        return copy(u, 12, block, block, to_mate)
+        return copy_c(u, 12, block, block, to_mate)
 
     def c_z5(u):
         block = out_rows(u, 2, side * 64, 64)
-        return copy(u, 13, block, block, to_inner)
+        return copy_c(u, 13, block, block, to_inner)
 
     def c_z6(u):
         block = out_rows(u, 2, far, 96)
-        return copy(u, 12, block, block, to_mate)
+        return copy_c(u, 12, block, block, to_mate)
 
     def c1_inner(u):
         arrived(u, 7, c_in.at[u % TURNS, 0:96])
@@ -492,20 +529,31 @@
     def c9_inner(u):
         arrived(u, 13, out_rows(u, 2, (1 - side) * 64, 64))
         c_z6(u).start()
-        spread(u, 2 * SLAB, SLAB)
+        to_other_c(u, core).start()
 
     def c10_outer(u):
         arrived(u, 12, out_rows(u, 2, far, 96))
-        spread(u, 2 * SLAB, SLAB)
-
-    def sent(u, units, rows):
+        to_other_c(u, core).start()
+
+    def sent(sem, units, rows):
         ref = part.at[0:units, 0:rows]
-        copy(u, 0, ref, ref, to_core).wait_send()
+        pltpu.make_async_remote_copy(
+            src_ref=ref, dst_ref=ref, send_sem=sem, recv_sem=back_sem.at[0],
+            device_id=to_core, device_id_type=MESH,
+        ).wait_send()
+
+    def sent_either(sem, at_outer, at_inner):
+        pl.when(outer)(lambda: sent(sem, *at_outer))
+        pl.when(inner)(lambda: sent(sem, *at_inner))
 
     def drain(u):
-        pl.when(outer)(lambda: sent(u, 4, 224))
-        pl.when(inner)(lambda: sent(u, 4, 272))
+        pl.when(u < OUTS)(lambda: sent_either(send_sem.at[u], (4, 176), (3, 256)))
+        pl.when(u >= OUTS)(lambda: sent_either(send_sem.at[u], (4, 144), (4, 160)))
         to_other(u, sums.at[u, 1 - core]).wait_recv()
+
+    def drain_c(u):
+        sent_either(send_c.at[u], (2, 160), (2, 224))
+        to_other_c(u, 1 - core).wait_recv()
 
     mm_nt = (((1,), (1,)), ((), ()))
     mm_tn = (((0,), (0,)), ((), ()))
@@ -734,7 +782,7 @@
 
     def store_exact(h, v):
         for i, term in enumerate(exact_terms(v)):
-            sums[UNITS, h, 256:304, i * 128 : (i + 1) * 128] = term
+            sums[LAST + 1 + THIRD // 2, h, 0:48, i * 128 : (i + 1) * 128] = term
 
     head_grad = tn(d_head, low_top[...])
     head_bias_grad = jnp.sum(d_head.astype(f32), 0, keepdims=True)
@@ -873,52 +921,61 @@
     up_left_go(1).wait_recv()
     up_left_go(2).start()
     feed_norm_back()
+    for u in range(OUTS):
+        out_stage[u] = out_product(u, 1 - core).astype(bf16)
+        out_first(u).start()
 
     def piece(t):
-        @pl.when(jnp.logical_and(t >= 2, t < 5))
-        def _():
-            attend_back(2 * t - 4)
-            attend_back(2 * t - 3)
-
-        pl.when(t == 5)(lambda: pass_on(1))
-        pl.when(t == 4)(send_prior)
-        pl.when(t == 6)(packed_back)
-        pl.when(t == 7)(outputs)
-        pl.when(t == 8)(embed_back)
+        @pl.when(jnp.logical_and(t >= 2, t < 4))
+        def _():
+            for i in range(3):
+                attend_back(3 * t - 6 + i)
+
+        pl.when(t == 4)(lambda: pass_on(1))
+        pl.when(t == 3)(send_prior)
+        pl.when(t == 5)(packed_back)
+        pl.when(t == 6)(outputs)
+        pl.when(t == 7)(embed_back)
 
     everyone, inners, outers = None, inner, outer
     events = [
-        (10, LAST + 1, inners, ab7),
-        (11, UNITS, inners, c9_inner),
-        (2, UNITS, everyone, produce),
-        (4, UNITS, inners, c1_inner),
-        (8, LAST + 1, inners, ab6),
-        (7, UNITS, outers, c3_outer),
-        (8, UNITS, outers, c4),
-        (9, UNITS, inners, c5),
-        (9, UNITS, outers, c5),
-        (3, UNITS, everyone, begin),
-        (1, LAST + 1, everyone, begin_more),
-        (7, UNITS, inners, c4),
-        (5, UNITS, inners, c2_inner),
-        (14, UNITS, outers, c10_outer),
+        (4, None, everyone, produce),
+        (5, None, everyone, begin),
+        (2, LAST + 1, everyone, begin_more),
+        (9, None, inners, c4),
+        (4, LAST + 1, everyone, begin_ab),
+        (9, None, outers, c3_outer),
+        (4, LAST + 1, everyone, ab1),
+        (10, LAST + 1, outers, ab5_outer),
+        (7, None, inners, c2_inner),
+        (6, LAST + 1, inners, ab3_inner),
+        (13, LAST + 1, outers, ab7),
+        (11, None, inners, c5),
+        (12, LAST + 1, inners, ab6),
+        (14, None, inners, c9_inner),
         (0, LAST + 1, everyone, piece),
-        (12, LAST + 1, outers, ab7),
-        (5, LAST + 1, inners, ab3_inner),
-        (3, LAST + 1, everyone, begin_ab),
-        (3, LAST + 1, everyone, ab1),
-        (6, LAST + 1, inners, ab4_inner),
-        (8, LAST + 1, outers, ab5_outer),
-        (9, LAST + 1, outers, ab6),
-        (9, UNITS, inners, c8_inner),
-        (4, LAST + 1, everyone, ab2),
+        (15, LAST + 1, inners, ab7),
+        (5, None, inners, c1_inner),
+        (7, LAST + 1, inners, ab4_inner),
+        (5, LAST + 1, everyone, ab2),
+        (10, None, outers, c4),
+        (11, LAST + 1, outers, ab6),
+        (11, None, outers, c5),
+        (12, None, inners, c8_inner),
+        (16, None, outers, c10_outer),
         (DRAIN, UNITS, everyone, drain),
+        (DRAIN_C, None, everyone, drain_c),
     ]
 
     def step(t, carried):
         for lag, count, who, event in events:
-            u = t - lag
-            now = jnp.logical_and(u >= 0, u < count)
+            if count is None:
+                turn = t - lag + 48
+                u = 2 * (turn // 3) + turn % 3 - 32
+                now = jnp.logical_and(turn >= 48, jnp.logical_and(turn % 3 < 2, u < THIRD))
+            else:
+                u = t - lag
+                now = jnp.logical_and(u >= 0, u < count)
             if who is not None:
                 now = jnp.logical_and(now, who)
             pl.when(now)(lambda event=event, u=u: event(u))
@@ -932,12 +989,14 @@
         return carried
 
     lax.fori_loop(STEPS - DRAIN, UNITS, drain_more, 0)
-    pl.when(outer)(lambda: sent(UNITS, 2, 224))
-    pl.when(inner)(lambda: sent(UNITS, 2, 256))
-    pl.when(outer)(lambda: sent(LAST, 2, 352))
-    pl.when(inner)(lambda: sent(LAST, 2, 384))
-    to_other(LAST, sums.at[LAST, 1 - core, 0 : 2 * SLAB]).wait_recv()
-    for u in range(UNITS - STAGES, UNITS):
+    for u in range(18, THIRD):
+        drain_c(u)
+    sent_either(send_sem.at[UNITS], (2, 224), (2, 256))
+    sent_either(send_sem.at[LAST], (4, 176), (3, 256))
+    to_other(LAST, sums.at[LAST, 1 - core]).wait_recv()
+    for u in range(OUTS):
+        out_first(u).wait_send()
+    for u in range(THIRD - STAGES, THIRD):
         core_first(u).wait_send()
     small_first().wait_send()
     for k in range(3):
@@ -980,17 +1039,20 @@
     wide = (128, 768)
     return pl.pallas_call(
         flow_kernel,
-        out_shape=pltpu.VMEM((LAST + 1, 2, 3 * SLAB, COLS), bf16),
+        out_shape=pltpu.VMEM((LAST + 2 + THIRD // 2, 2, 2 * SLAB, COLS), bf16),
         in_specs=[smem] * 3 + [vmem] * 12 + [hbm] * 5,
         out_specs=vmem,
         scratch_shapes=[
             pltpu.VMEM((STAGES, SLAB, COLS), bf16),
-            pltpu.VMEM((LAST + 1, 3 * SLAB, COLS), bf16),
+            pltpu.VMEM((LAST + 1, 2 * SLAB, COLS), bf16),
+            pltpu.VMEM((THIRD, SLAB, COLS), bf16),
+            pltpu.VMEM((OUTS, 2 * SLAB, COLS), bf16),
+            pltpu.VMEM((OUTS, 2 * SLAB, COLS), bf16),
             pltpu.VMEM((TURNS, SLAB, COLS), bf16),
             pltpu.VMEM((256, COLS), bf16),
             pltpu.VMEM((TURNS, 2, 160, COLS), bf16),
             pltpu.VMEM((TURNS, 256, COLS), bf16),
-            pltpu.VMEM((UNITS, 32, COLS), bf16),
+            pltpu.VMEM((THIRD, 32, COLS), bf16),
             pltpu.VMEM((1536, 512), bf16),
             pltpu.VMEM((512, COLS), bf16),
             pltpu.VMEM((768, 512), bf16),
@@ -1001,6 +1063,10 @@
             pltpu.SemaphoreType.DMA((14, TURNS)),
             pltpu.SemaphoreType.DMA((STAGES + 1,)),
             pltpu.SemaphoreType.DMA((LAST + 1,)),
+            pltpu.SemaphoreType.DMA((THIRD,)),
+            pltpu.SemaphoreType.DMA((THIRD,)),
+            pltpu.SemaphoreType.DMA((OUTS,)),
+            pltpu.SemaphoreType.DMA((OUTS,)),
             pltpu.VMEM((768, 2304), bf16),
             pltpu.VMEM((768, 768), bf16),
             pltpu.VMEM((768, 3072), bf16),
@@ -1090,7 +1156,7 @@
 
     def little():
         for h in range(2):
-            terms = [sums[UNITS, h, 256:304, i * 128 : (i + 1) * 128].astype(f32) for i in range(3)]
+            terms = [sums[LAST + 1 + THIRD // 2, h, 0:48, i * 128 : (i + 1) * 128].astype(f32) for i in range(3)]
             lat_wide[h] = terms[0] + terms[1] + terms[2]
         outputs[0].start()
         outputs[1].start()
@@ -1103,7 +1169,7 @@
             one.start()
         halves = []
         for h in range(2):
-            terms = [sums[LAST, h, 256 + i * 16 : 272 + i * 16].astype(f32) for i in range(3)]
+            terms = [sums[LAST + 1 + THIRD // 2, h, 64 + i * 16 : 80 + i * 16].astype(f32) for i in range(3)]
             halves.append(terms[0] + terms[1] + terms[2])
         block = jnp.concatenate(halves, 1)
         for i, one in enumerate((g1, b1, g2, b2)):
@@ -1126,21 +1192,23 @@
         class_wide[...] = jnp.dot(hot, small_wide[144:160].astype(bf16), preferred_element_type=f32)
         outputs[5].start()
 
-    for u in range(UNITS):
-        block, row, turn = u // 6, (u % 6) * SLAB, 64 * (u // 2)
+    for u in range(OUTS):
+        rows = slice(256 * u, 256 * (u + 1))
+        for h in range(2):
+            wide_last[0, rows, h * COLS : (h + 1) * COLS] = sums[u, h].astype(f32)
+        write(wide_last.at[0, rows], out.at[0, rows])
+    for u in range(UNITS - OUTS):
+        turn = 64 * (u // 2)
         for h in range(2):
             cols = slice(h * COLS, (h + 1) * COLS)
             for i in range(2):
                 wide_down[1536 * i + 64 * u : 1536 * i + 64 * (u + 1), cols] = sums[
-                    u, h, 64 * i : 64 * (i + 1)
+                    u + OUTS, h, 64 * i : 64 * (i + 1)
                 ].astype(f32)
                 column = (2 * i + h) * 768 + (u % 2) * COLS
                 wide_up[turn : turn + 64, column : column + COLS] = sums[
-                    u, h, 128 + 64 * i : 128 + 64 * (i + 1)
+                    u + OUTS, h, 128 + 64 * i : 128 + 64 * (i + 1)
                 ].astype(f32)
-            wide_last[block, row : row + SLAB, cols] = sums[u, h, 2 * SLAB :].astype(f32)
-        target, column = (out, 0) if block == 0 else (qkv, (block - 1) * 768)
-        write(wide_last.at[block, row : row + SLAB], target.at[0, row : row + SLAB, column : column + 768])
         if u % 2 == 1:
             write(wide_up.at[turn : turn + 64], up.at[0, turn : turn + 64])
         if u % 4 == 3:
@@ -1149,6 +1217,16 @@
                 write(wide_down.at[rows], down.at[0, rows])
         if u == 3:
             little()
+    for u in range(THIRD):
+        block, row = u // 6, (u % 6) * SLAB
+        for h in range(2):
+            wide_last[block + 1, row : row + SLAB, h * COLS : (h + 1) * COLS] = sums[
+                LAST + 1 + u // 2, h, (u % 2) * SLAB : (u % 2 + 1) * SLAB
+            ].astype(f32)
+        write(
+            wide_last.at[block + 1, row : row + SLAB],
+            qkv.at[0, row : row + SLAB, block * 768 : (block + 1) * 768],
+        )
     for one in writes:
         one.wait()
     for one in outputs:
@@ -1174,7 +1252,7 @@
             pltpu.VMEM((3072, 768), f32),
             pltpu.VMEM((768, 3072), f32),
             pltpu.VMEM((4, 768, 768), f32),
-            pltpu.SemaphoreType.DMA((48,)),
+            pltpu.SemaphoreType.DMA((45,)),
             pltpu.VMEM((2, 48, 128), f32),
             pltpu.VMEM((128, 768), f32),
             pltpu.VMEM((256, 768), f32),

time: 138 us -> 137 us (level)
  no operation moved by 1% of the time
where the time goes in v7:
time: 137 us
  Pallas kernels  135 us (99%)
  between operations  1.98 us (1%)
    pallas_call x1, Pallas kernels, flow(): pl.pallas_call(flow_kernel, out_shape=pltpu.VMEM((LAST + 2 + THIRD // 2,...  124 us
    pallas_call x1, Pallas kernels, finish(): pl.pallas_call(finish_kernel, out_shape=[jax.ShapeDtypeStruct(shape, f32)...  10.8 us

profile of v7, /device:TPU:0, one launch (start us, length us, event | category | flops | bytes accessed | tf_op | source)
XLA Modules:
  0.0 137.3 jit_solution(15368952457375151667)
XLA Ops:
  2.0 0.0 copy-start
  2.0 124.5 %flow.1.sums = bf16[39,2,256,384]{3,2,1,0:T(8,128)(2,1)S(1)} custom-call(s32[16]{0:T(128)} %labels_sm.1, s32[1]{0:T(128)S(6)} %copy.37.perm_sm, f32[1]{0:T(128)S(6)} %copy.38.cot_logdet_sm, f32[1,48,128]{2,1,0:T(8,128)} %bitcast.12, s32[1,128]{1,0:T(1,128)} %valid_ref.1, bf16[48,768]{1,0:T(8,128)(2,1)} %patch_ref.1, bf16[128,768]{1,0:T(8,128)(2,1)} %pos_table_ref.1, ...), custom_call_target="tpu_custom_call" | custom-call | tf_op jit(solution)/shard_map/flow/pallas_call | solution.py:1040
  126.5 0.0 copy-done
  126.5 10.8 %finish.1 = (f32[1,48,128]{2,1,0:T(8,128)}, f32[1,1]{1,0:T(1,128)}, f32[1,48,128]{2,1,0:T(8,128)}, f32[48,768]{1,0:T(8,128)}, f32[128,768]{1,0:T(8,128)}, /*inde...) custom-call(s32[1,16]{1,0:T(1,128)S(1)} %bitcast.10, ...), custom_call_target="tpu_custom_call" | custom-call | tf_op jit(solution)/shard_map/finish/pallas_call | solution.py:1246
Async XLA Ops:
  2.0 124.5 %copy-start = (s32[16]{0:T(128)S(1)}, s32[16]{0:T(128)}, u32[]{:S(2)}) copy-start(s32[16]{0:T(128)} %labels_sm.1) | copy-start | bytes 196

commit v8 on v7

--- a/solution.py
+++ b/solution.py
@@ -191,7 +191,7 @@
 
     def bulk(k, src, dst, target):
         return pltpu.make_async_remote_copy(
-            src_ref=src, dst_ref=dst, send_sem=bulk_send.at[k], recv_sem=bulk_recv.at[k],
+            src_ref=src, dst_ref=dst, send_sem=bulk_send, recv_sem=bulk_recv.at[k],
             device_id=target, device_id_type=MESH,
         )
 
@@ -481,15 +481,15 @@
 
     def c_z4(u):
         block = out_rows(u, 2, own_end, 32)
-        return copy_c(u, 12, block, block, to_mate)
+        return copy_c(u, 11, block, block, to_mate)
 
     def c_z5(u):
         block = out_rows(u, 2, side * 64, 64)
-        return copy_c(u, 13, block, block, to_inner)
+        return copy_c(u, 12, block, block, to_inner)
 
     def c_z6(u):
         block = out_rows(u, 2, far, 96)
-        return copy_c(u, 12, block, block, to_mate)
+        return copy_c(u, 11, block, block, to_mate)
 
     def c1_inner(u):
         arrived(u, 7, c_in.at[u % TURNS, 0:96])
@@ -523,16 +523,16 @@
         pl.when(outer)(lambda: c_z4(u).start())
 
     def c8_inner(u):
-        arrived(u, 12, out_rows(u, 2, own_end, 32))
+        arrived(u, 11, out_rows(u, 2, own_end, 32))
         c_z5(u).start()
 
     def c9_inner(u):
-        arrived(u, 13, out_rows(u, 2, (1 - side) * 64, 64))
+        arrived(u, 12, out_rows(u, 2, (1 - side) * 64, 64))
         c_z6(u).start()
         to_other_c(u, core).start()
 
     def c10_outer(u):
-        arrived(u, 12, out_rows(u, 2, far, 96))
+        arrived(u, 11, out_rows(u, 2, far, 96))
         to_other_c(u, core).start()
 
     def sent(sem, units, rows):
@@ -730,7 +730,7 @@
         d_hidden[...] += nn(act.astype(bf16), down_w[rows768(j)])
         return carried
 
-    lax.fori_loop(0, 4, feed, 0)
+    lax.fori_loop(0, 4, feed, 0, unroll=True)
     low_top[...] = d_hidden[...].astype(bf16)
     row_out[...] = nt(low_top[...], head_pad[...]) + head_bias
 
@@ -1001,13 +1001,8 @@
     small_first().wait_send()
     for k in range(3):
         line_go(k).wait_send()
-        down_right_go(k).wait_send()
-        up_left_go(k).wait_send()
-        up_right_go(k, 0).wait_send()
-    for i in range(2):
-        down_left_core(i).wait_send()
-        down_left_x(i).wait_send()
-        down_left_on(i).wait_send()
+    every = part.at[0:18, 0:192]
+    bulk(0, every, every, to_core).wait_send()
     pl.when(outer)(line_go(3).wait_send)
 
     @pl.when(inner)
@@ -1057,10 +1052,10 @@
             pltpu.VMEM((512, COLS), bf16),
             pltpu.VMEM((768, 512), bf16),
             pltpu.VMEM((2, 512, COLS), bf16),
-            pltpu.SemaphoreType.DMA((15,)),
+            pltpu.SemaphoreType.DMA,
             pltpu.SemaphoreType.DMA((15,)),
             pltpu.SemaphoreType.DMA((LAST + 1,)),
-            pltpu.SemaphoreType.DMA((14, TURNS)),
+            pltpu.SemaphoreType.DMA((13, TURNS)),
             pltpu.SemaphoreType.DMA((STAGES + 1,)),
             pltpu.SemaphoreType.DMA((LAST + 1,)),
             pltpu.SemaphoreType.DMA((THIRD,)),
@@ -1148,11 +1143,8 @@
             )
         )
     ]
-    writes = []
-
-    def write(src, dst):
-        writes.append(pltpu.make_async_copy(src, dst, write_sem.at[len(writes)]))
-        writes[-1].start()
+    def write(k, src, dst):
+        pltpu.make_async_copy(src, dst, write_sem.at[k]).start()
 
     def little():
         for h in range(2):
@@ -1196,7 +1188,7 @@
         rows = slice(256 * u, 256 * (u + 1))
         for h in range(2):
             wide_last[0, rows, h * COLS : (h + 1) * COLS] = sums[u, h].astype(f32)
-        write(wide_last.at[0, rows], out.at[0, rows])
+        write(0, wide_last.at[0, rows], out.at[0, rows])
     for u in range(UNITS - OUTS):
         turn = 64 * (u // 2)
         for h in range(2):
@@ -1210,11 +1202,11 @@
                     u + OUTS, h, 128 + 64 * i : 128 + 64 * (i + 1)
                 ].astype(f32)
         if u % 2 == 1:
-            write(wide_up.at[turn : turn + 64], up.at[0, turn : turn + 64])
+            write(1, wide_up.at[turn : turn + 64], up.at[0, turn : turn + 64])
         if u % 4 == 3:
             for i in range(2):
                 rows = slice(1536 * i + 64 * (u - 3), 1536 * i + 64 * (u + 1))
-                write(wide_down.at[rows], down.at[0, rows])
+                write(2, wide_down.at[rows], down.at[0, rows])
         if u == 3:
             little()
     for u in range(THIRD):
@@ -1224,11 +1216,12 @@
                 LAST + 1 + u // 2, h, (u % 2) * SLAB : (u % 2 + 1) * SLAB
             ].astype(f32)
         write(
+            0,
             wide_last.at[block + 1, row : row + SLAB],
             qkv.at[0, row : row + SLAB, block * 768 : (block + 1) * 768],
         )
-    for one in writes:
-        one.wait()
+    for k, buffer in enumerate((wide_last, wide_up, wide_down)):
+        pltpu.make_async_copy(buffer, buffer, write_sem.at[k]).wait()
     for one in outputs:
         one.wait()
 
@@ -1252,7 +1245,7 @@
             pltpu.VMEM((3072, 768), f32),
             pltpu.VMEM((768, 3072), f32),
             pltpu.VMEM((4, 768, 768), f32),
-            pltpu.SemaphoreType.DMA((45,)),
+            pltpu.SemaphoreType.DMA((3,)),
             pltpu.VMEM((2, 48, 128), f32),
             pltpu.VMEM((128, 768), f32),
             pltpu.VMEM((256, 768), f32),

time: 137 us -> 137 us (level)
  no operation moved by 1% of the time
where the time goes in v8:
time: 137 us
  Pallas kernels  135 us (99%)
  between operations  2.14 us (2%)
    pallas_call x1, Pallas kernels, flow(): pl.pallas_call(flow_kernel, out_shape=pltpu.VMEM((LAST + 2 + THIRD // 2,...  124 us
    pallas_call x1, Pallas kernels, finish(): pl.pallas_call(finish_kernel, out_shape=[jax.ShapeDtypeStruct(shape, f32)...  10.4 us

profile of v8, /device:TPU:0, one launch (start us, length us, event | category | flops | bytes accessed | tf_op | source)
XLA Modules:
  0.0 136.8 jit_solution(14234796084384851853)
XLA Ops:
  2.0 0.0 copy-start
  2.0 124.2 %flow.1.sums = bf16[39,2,256,384]{3,2,1,0:T(8,128)(2,1)S(1)} custom-call(s32[16]{0:T(128)} %labels_sm.1, s32[1]{0:T(128)S(6)} %copy.37.perm_sm, f32[1]{0:T(128)S(6)} %copy.38.cot_logdet_sm, f32[1,48,128]{2,1,0:T(8,128)} %bitcast.12, s32[1,128]{1,0:T(1,128)} %valid_ref.1, bf16[48,768]{1,0:T(8,128)(2,1)} %patch_ref.1, bf16[128,768]{1,0:T(8,128)(2,1)} %pos_table_ref.1, ...), custom_call_target="tpu_custom_call" | custom-call | tf_op jit(solution)/shard_map/flow/pallas_call | solution.py:1035
  126.2 0.0 copy-done
  126.2 10.4 %finish.1 = (f32[1,48,128]{2,1,0:T(8,128)}, f32[1,1]{1,0:T(1,128)}, f32[1,48,128]{2,1,0:T(8,128)}, f32[48,768]{1,0:T(8,128)}, f32[128,768]{1,0:T(8,128)}, /*inde...) custom-call(s32[1,16]{1,0:T(1,128)S(1)} %bitcast.10, ...), custom_call_target="tpu_custom_call" | custom-call | tf_op jit(solution)/shard_map/finish/pallas_call | solution.py:1239
Async XLA Ops:
  2.0 124.2 %copy-start = (s32[16]{0:T(128)S(1)}, s32[16]{0:T(128)}, u32[]{:S(2)}) copy-start(s32[16]{0:T(128)} %labels_sm.1) | copy-start | bytes 196
